TPU v7x, 512 devices: a whole 4x4x16 slice. The times are simulated.
512 devices in a mesh: region: 128 (over z, x, core), pair: 4 (over y).
Axes of the slice: x: 4, y: 4, z: 16, core: 2. Of those that a mesh axis runs over, the one named last changes fastest.
Arguments:
- phi: bfloat16 [1024, 128, 32, 128], P('region', None, 'pair'), may hold values from -0.09375 to 0.09375
- potential: float32 [128, 32, 128], P('region', 'pair'), may hold values from -2 to 2
- pair_list: int32 [32, 2], replicated, may hold values from 0 to 7, as said below
- support: int32 [8, 128], replicated, may hold values 0 or 1
Outputs:
- intersection: float32 [32, 16384], P('pair', 'region')
- hamiltonian: float32 [32, 16384], P('pair', 'region')
- hphi: bfloat16 [1024, 128, 32, 128], P('region', None, 'pair')
Inputs may be any that keep to these rules, and one draw needn't show every extreme that they name: `pair_list`: each row is an ordered pair of block numbers; no pair appears twice.
All inputs are finite; a program needn't handle non-finite values.
Results may differ from a plain program's by a relative error of at most 0.0029.
Values may be sent and summed in bfloat16 or wider, within the bound.
No kernel may reach another device: no remote copies, remote signals or barrier semaphores. Data moves between devices by JAX's collectives and lax.ppermute only.
A program may use at most 64 MiB of HBM per device.

v0:
```python
import jax
import jax.numpy as jnp
from jax import lax
from jax.sharding import PartitionSpec as P

W = 128


def padded_2(block, sides, width):
    for axis, dim in sides:
        count = lax.axis_size(axis)
        forward = [(i, i + 1) for i in range(count - 1)]
        forward.append((count - 1, 0))
        backward = [(target, source) for source, target in forward]
        low = lax.ppermute(
            lax.slice_in_dim(block, block.shape[dim] - width, None, axis=dim), axis, forward
        )
        high = lax.ppermute(lax.slice_in_dim(block, 0, width, axis=dim), axis, backward)
        block = jnp.concatenate([low, block, high], axis=dim)
    return block


def apply_region(padded, potential, keep_value):
    values = padded.astype(jnp.float32)
    center = values[:, 1:-1, 1:-1]
    laplace_sum = values[:, 2:, 1:-1] + values[:, :-2, 1:-1] - 6.0 * center
    laplace_sum = laplace_sum + values[:, 1:-1, 2:] + values[:, 1:-1, :-2]
    z_padded = jnp.pad(center, ((0, 0), (0, 0), (0, 0), (1, 1)))
    laplace_sum = laplace_sum + z_padded[..., 2:] + z_padded[..., :-2]
    applied = (-0.5 * laplace_sum + potential[None] * center) * keep_value
    return applied.astype(jnp.bfloat16)


def local(phi, potential, pair_list, support):
    region_id = lax.axis_index("region")
    block_count = support.shape[0]
    all_funcs = block_count * W
    row_count = phi.shape[2]
    depth = phi.shape[3]
    plane_count = potential.shape[0]
    block_flags = lax.dynamic_slice_in_dim(support, region_id, 1, 1)[:, 0]
    func_live = jnp.repeat(block_flags > 0, W)
    region_data = lax.all_to_all(phi, "region", split_axis=1, concat_axis=0, tiled=True)
    confined = jnp.where(func_live[:, None, None, None], region_data, jnp.zeros_like(region_data))
    padded = padded_2(confined, (("region", 1), ("pair", 2)), 1)
    keep_values = block_flags.astype(jnp.float32)
    stacked = padded.reshape(block_count, W, plane_count + 2, row_count + 2, depth)
    applied_region = lax.map(
        lambda members: apply_region(members[0], potential, members[1]), (stacked, keep_values)
    )
    applied_region = applied_region.reshape(all_funcs, plane_count, row_count, depth)
    cell_count = plane_count * row_count * depth
    flat_data = confined.reshape(all_funcs, cell_count)
    flat_applied = applied_region.reshape(all_funcs, cell_count)
    contract_dims = (((1,), (1,)), ((), ()))

    def pair_terms(pair_row):
        left_rows = lax.dynamic_slice_in_dim(flat_data, pair_row[0] * W, W, 0)
        right_rows = lax.dynamic_slice_in_dim(flat_data, pair_row[1] * W, W, 0)
        ham_rows = lax.dynamic_slice_in_dim(flat_applied, pair_row[1] * W, W, 0)
        return (
            lax.dot_general(
                left_rows, right_rows, contract_dims, preferred_element_type=jnp.float32
            ),
            lax.dot_general(left_rows, ham_rows, contract_dims, preferred_element_type=jnp.float32),
        )

    intersection_part, hamil_part = lax.map(pair_terms, pair_list)
    pair_count = pair_list.shape[0]
    intersection_part = intersection_part.reshape(pair_count, W * W)
    hamil_part = hamil_part.reshape(pair_count, W * W)
    intersection_cols, hamil_cols = (
        lax.psum_scatter(intersection_part, "region", scatter_dimension=1, tiled=True),
        lax.psum_scatter(hamil_part, "region", scatter_dimension=1, tiled=True),
    )
    intersection, hamiltonian = (
        lax.psum_scatter(intersection_cols, "pair", scatter_dimension=0, tiled=True),
        lax.psum_scatter(hamil_cols, "pair", scatter_dimension=0, tiled=True),
    )
    hphi_out = lax.all_to_all(applied_region, "region", split_axis=0, concat_axis=1, tiled=True)
    return (intersection, hamiltonian, hphi_out)


def solution(mesh):
    in_specs = (P("region", None, "pair", None), P("region", "pair", None), P(), P())
    out_specs = (P("pair", "region"), P("pair", "region"), P("region", None, "pair", None))
    return jax.shard_map(local, mesh=mesh, in_specs=in_specs, out_specs=out_specs, check_vma=False)
```

profile of v0, /device:TPU:6, one launch (start us, length us, event | category | flops | bytes accessed | tf_op | source)
XLA Modules:
  0.0 986.5 jit_solution(11047298964091114942)
XLA Ops:
  7.2 3.5 copy.12
  10.7 19.5 %all-to-all-start = ((bf16[8,128,8,128]{3,2,0,1:T(8,128)(2,1)}), bf16[8,128,8,128]{3,2,0,1:T(8,128)(2,1)S(1)}, u32[]{:S(2)}, u32[]{:S(2)}) async-start(bf16[8,128,8,128]{3,2,0,1:T(8,128)(2,1)} %copy.12), calls=%async_computation | async-start | bytes 4194304 | tf_op jit(solution)/shard_map/all_to_all | solution.py:43
  30.5 96.7 %all-to-all-done = bf16[8,128,8,128]{3,2,0,1:T(8,128)(2,1)S(1)} async-done(((bf16[8,128,8,128]{3,2,0,1:T(8,128)(2,1)}), bf16[8,128,8,128]{3,2,0,1:T(8,128)(2,1)S(1)}, u32[]{:S(2)}, u32[]{:S(2)}) %all-to-all-start) | async-done | bytes 2097184 | tf_op jit(solution)/shard_map/all_to_all | solution.py:43
  127.1 3.7 bitcast_select_fusion.1
  130.9 2.8 collective-permute-start
  133.7 2.8 collective-permute-start.1
  136.4 21.8 %collective-permute-done = bf16[1024,1,8,128]{3,2,0,1:T(8,128)(2,1)S(1)} collective-permute-done((bf16[1024,1,8,128]{3,2,0,1:T(8,128)(2,1)S(1)}, bf16[1024,1,8,128]{3,2,0,1:T(8,128)(2,1)S(1)}, u32[]{:S(2)}, u32[]{:S(2)}) %collective-permute-start) | collective-permute-done | bytes 2097184 | tf_op jit(solution)/shard_map/ppermute | solution.py:15
  160.0 2.6 pad_maximum_fusion.3
  162.7 3.5 collective-permute-start.2
  167.3 3.6 collective-permute-start.3
  172.7 9.4 collective-permute-done.2
  182.1 2.3 copy.15
  185.9 2.3 copy.16
  188.3 10.7 %pad_maximum_fusion = bf16[1024,3,10,128]{3,2,0,1:T(8,128)(2,1)} fusion(bf16[1024,3,1,128]{3,2,0,1:T(2,128)(2,1)S(1)} %copy.16, bf16[1024,1,8,128]{3,2,0,1:T(8,128)(2,1)S(1)} %copy-done.7, bf16[1024,1,8,128]{3,2,0,1:T(8,128)(2,1)S(1)} %copy-done.1, bf16[1024,1,8,128]{3,2,0,1:T(8,128)(2,1)S(1)} %copy-done.5, bf16[1024,3,1,128]{3,2,0,1:T(2,128)(2,1)S(1)} %copy.15), kind=kLoop, calls=%fused_computation.25 | loop fusion | flops 39321600 | bytes 15728640 | tf_op jit(solution)/shard_map/concatenate | solution.py:19
  199.0 28.2 %while.24 = (s32[]{:T(128)}, bf16[8,128,1,8,128]{4,3,2,1,0:T(8,128)(2,1)S(1)}, bf16[8,128,3,10,128]{4,3,1,0,2:T(8,128)(2,1)}, f32[1,8,128]{2,1,0:T(8,128)S(1)}, f32[8]{0:T(128)S(1)}, /*index=5*/s32[]{:T(128)}) while((s32[]{:T(128)}, bf16[8,128,1,8,128]{4,3,2,1,0:T(8,128)(2,1)S(1)}, bf16[8,128,3,10,128]{4,3,1,0,2:T(8,128)(2,1)}, ...), condition=%wide.region_1.2_spmd, body=%wide.region_0.1_spmd.sunk | while | flops 2064386 | bytes 6885469 | solution.py:48
  227.3 2.0 copy.33
  229.2 14.0 %all-to-all-start.1 = ((bf16[1024,1,8,128]{3,2,1,0:T(8,128)(2,1)}), bf16[1024,1,8,128]{3,2,1,0:T(8,128)(2,1)S(1)}, u32[]{:S(2)}, u32[]{:S(2)}) async-start(bf16[1024,1,8,128]{3,2,1,0:T(8,128)(2,1)} %bitcast.76), calls=%async_computation.3 | async-start | bytes 4194304 | tf_op jit(solution)/shard_map/all_to_all | solution.py:80
  243.3 186.1 %while.25 = (s32[]{:T(128)}, f32[32,128,128]{2,1,0:T(8,128)}, f32[32,128,128]{2,1,0:T(8,128)}, s32[32,2]{0,1:T(2,128)S(1)}, bf16[1024,1024]{1,0:T(8,128)(2,1)}, ...) while((s32[]{:T(128)}, f32[32,128,128]{2,1,0:T(8,128)}, ...), condition=%wide.region_3.4_spmd, body=%wide.region_2.3_spmd.sunk | while | flops 67108872 | bytes 1180917 | solution.py:68
  251.1 1.9 fusion.29
  257.0 1.9 fusion.29
  262.8 1.9 fusion.29
  268.6 1.9 fusion.29
  274.4 1.9 fusion.29
  286.0 1.9 fusion.29
  291.8 1.9 fusion.29
  297.7 1.9 fusion.29
  303.5 1.9 fusion.29
  309.3 1.9 fusion.29
  315.1 1.9 fusion.29
  326.7 1.9 fusion.29
  338.4 1.9 fusion.29
  344.2 1.9 fusion.29
  350.0 1.9 fusion.29
  367.4 1.9 fusion.29
  373.2 1.9 fusion.29
  379.1 1.9 fusion.29
  390.7 1.9 fusion.29
  396.5 1.9 fusion.29
  402.3 1.9 fusion.29
  408.2 1.9 fusion.29
  414.0 1.9 fusion.29
  419.8 1.9 fusion.29
  425.6 1.9 fusion.29
  429.4 4.1 copy.32
  433.6 4.1 copy.31
  439.7 255.6 %reduce-scatter.3.cloned.1.call-done = f32[32,128]{1,0:T(8,128)} async-done(((f32[32,16384]{1,0:T(8,128)}), f32[32,128]{1,0:T(8,128)}) %reduce-scatter.3.cloned.1.call-update) | async-done | bytes 16400 | tf_op jit(solution)/shard_map/reduce_scatter | solution.py:73
  695.3 264.2 %reduce-scatter.5.cloned.1.call-done = f32[32,128]{1,0:T(8,128)} async-done(((f32[32,16384]{1,0:T(8,128)}), f32[32,128]{1,0:T(8,128)}) %reduce-scatter.5.cloned.1.call-update) | async-done | bytes 16400 | tf_op jit(solution)/shard_map/reduce_scatter | solution.py:74
  959.5 17.8 %all-reduce.3 = (f32[32,128]{1,0:T(8,128)S(1)}, f32[32,128]{1,0:T(8,128)S(1)}) all-reduce(f32[32,128]{1,0:T(8,128)} %reduce-scatter.3.cloned.1.call-done, f32[32,128]{1,0:T(8,128)} %reduce-scatter.5.cloned.1.call-done), channel_id=3, replica_groups=mesh['region'=128,'pair'=4] {'pair'}, use_global_device_ids=true, to_apply=%region_5.6.clone | all-reduce | flops 8192 | bytes 65536
  (176 shorter events, 133.5 us)
Async XLA Ops:
  10.7 19.5 %copy-start.10 = (s32[8,128]{1,0:T(8,128)S(1)}, s32[8,128]{1,0:T(8,128)}, u32[]{:S(2)}) copy-start(s32[8,128]{1,0:T(8,128)} %param.11) | copy-start | bytes 12292
  10.7 116.4 %all-to-all-start = ((bf16[8,128,8,128]{3,2,0,1:T(8,128)(2,1)}), bf16[8,128,8,128]{3,2,0,1:T(8,128)(2,1)S(1)}, u32[]{:S(2)}, u32[]{:S(2)}) async-start(bf16[8,128,8,128]{3,2,0,1:T(8,128)(2,1)} %copy.12), calls=%async_computation | async-start | bytes 4194304 | tf_op jit(solution)/shard_map/all_to_all | solution.py:43
  130.9 31.8 %copy-start = (bf16[1024,1,8,128]{3,2,0,1:T(8,128)(2,1)}, bf16[1024,1,8,128]{3,2,0,1:T(8,128)(2,1)S(1)}, u32[]{:S(2)}) copy-start(bf16[1024,1,8,128]{3,2,0,1:T(8,128)(2,1)S(1)} %bitcast_select_fusion.1) | copy-start | bytes 6291460
  130.9 27.4 %collective-permute-start = (bf16[1024,1,8,128]{3,2,0,1:T(8,128)(2,1)S(1)}, bf16[1024,1,8,128]{3,2,0,1:T(8,128)(2,1)S(1)}, u32[]{:S(2)}, u32[]{:S(2)}) collective-permute-start(bf16[1024,1,8,128]{3,2,0,1:T(8,128)(2,1)S(1)} %bitcast_select_fusion.1), channel_id=1, source_target_pairs={{0,4},{4,8},{8,12},{12,16},{16,20},{20,24},{24,28},{28,32},{32,36}... | collective-permute-start | bytes 6291464 | tf_op jit(solution)/shard_map/ppermute | solution.py:15
  133.7 26.3 %collective-permute-start.1 = (bf16[1024,1,8,128]{3,2,0,1:T(8,128)(2,1)S(1)}, bf16[1024,1,8,128]{3,2,0,1:T(8,128)(2,1)S(1)}, u32[]{:S(2)}, u32[]{:S(2)}) collective-permute-start(bf16[1024,1,8,128]{3,2,0,1:T(8,128)(2,1)S(1)} %bitcast_select_fusion.1), channel_id=1, source_target_pairs={{4,0},{8,4},{12,8},{16,12},{20,16},{24,20},{28,24},{32,28},{36,32}... | collective-permute-start | bytes 6291464 | tf_op jit(solution)/shard_map/ppermute | solution.py:18
  158.2 4.4 copy-start.4
  160.0 2.7 copy-start.6
  162.7 19.3 %collective-permute-start.2 = (bf16[1024,3,1,128]{3,0,2,1:T(8,128)(2,1)S(1)}, bf16[1024,3,1,128]{3,0,2,1:T(8,128)(2,1)}, u32[]{:S(2)}, u32[]{:S(2)}) collective-permute-start(bf16[1024,3,1,128]{3,0,2,1:T(8,128)(2,1)S(1)} %copy.13), channel_id=1, source_target_pairs={{0,1},{1,2},{2,3},{3,0},{4,5},{5,6},{6,7},{7,4},{8,9},{9,10},{10,1... | collective-permute-start | bytes 2359304 | tf_op jit(solution)/shard_map/ppermute | solution.py:15
  167.3 18.7 %collective-permute-start.3 = (bf16[1024,3,1,128]{3,0,2,1:T(8,128)(2,1)}, bf16[1024,3,1,128]{3,0,2,1:T(8,128)(2,1)}, u32[]{:S(2)}, u32[]{:S(2)}) collective-permute-start(bf16[1024,3,1,128]{3,0,2,1:T(8,128)(2,1)} %copy.14), channel_id=1, source_target_pairs={{1,0},{2,1},{3,2},{0,3},{5,4},{6,5},{7,6},{4,7},{9,8},{10,9},{11,1... | collective-permute-start | bytes 2359304 | tf_op jit(solution)/shard_map/ppermute | solution.py:18
  171.0 17.3 %copy-start.7 = (bf16[1024,1,8,128]{3,2,0,1:T(8,128)(2,1)S(1)}, bf16[1024,1,8,128]{3,2,0,1:T(8,128)(2,1)}, u32[]{:S(2)}) copy-start(bf16[1024,1,8,128]{3,2,0,1:T(8,128)(2,1)} %copy-done.6) | copy-start | bytes 6291460
  172.7 15.6 %copy-start.1 = (bf16[1024,1,8,128]{3,2,0,1:T(8,128)(2,1)S(1)}, bf16[1024,1,8,128]{3,2,0,1:T(8,128)(2,1)}, u32[]{:S(2)}) copy-start(bf16[1024,1,8,128]{3,2,0,1:T(8,128)(2,1)} %copy-done) | copy-start | bytes 6291460
  172.7 15.6 %copy-start.5 = (bf16[1024,1,8,128]{3,2,0,1:T(8,128)(2,1)S(1)}, bf16[1024,1,8,128]{3,2,0,1:T(8,128)(2,1)}, u32[]{:S(2)}) copy-start(bf16[1024,1,8,128]{3,2,0,1:T(8,128)(2,1)} %copy-done.4) | copy-start | bytes 6291460
  188.3 10.7 %copy-start.2 = (bf16[8,128,1,8,128]{4,3,2,1,0:T(8,128)(2,1)S(1)}, bf16[8,128,1,8,128]{4,3,2,1,0:T(8,128)(2,1)}, u32[]{:S(2)}) copy-start(bf16[8,128,1,8,128]{4,3,2,1,0:T(8,128)(2,1)} %custom-call) | copy-start | bytes 6291460
  188.3 10.7 %copy-start.8 = (f32[1,8,128]{2,1,0:T(8,128)S(1)}, f32[1,8,128]{2,1,0:T(8,128)}, u32[]{:S(2)}) copy-start(f32[1,8,128]{2,1,0:T(8,128)} %param.9) | copy-start | bytes 12292
  227.2 2.0 copy-start.3
  229.2 14.1 %copy-start.9 = (s32[32,2]{0,1:T(2,128)S(1)}, s32[32,2]{0,1:T(2,128)}, u32[]{:S(2)}) copy-start(s32[32,2]{0,1:T(2,128)} %param.10) | copy-start | bytes 772
  229.2 748.7 %all-to-all-start.1 = ((bf16[1024,1,8,128]{3,2,1,0:T(8,128)(2,1)}), bf16[1024,1,8,128]{3,2,1,0:T(8,128)(2,1)S(1)}, u32[]{:S(2)}, u32[]{:S(2)}) async-start(bf16[1024,1,8,128]{3,2,1,0:T(8,128)(2,1)} %bitcast.76), calls=%async_computation.3 | async-start | bytes 4194304 | tf_op jit(solution)/shard_map/all_to_all | solution.py:80
  243.2 452.0 %reduce-scatter.3.cloned.1.call-start = ((), (), s32[]{:S(2)}) async-start(), calls=%async_computation.4 | async-start | bytes 2113536 | tf_op jit(solution)/shard_map/reduce_scatter | solution.py:73
  433.6 525.9 %reduce-scatter.5.cloned.1.call-start = ((), (), s32[]{:S(2)}) async-start(), calls=%async_computation.5 | async-start | bytes 2113536 | tf_op jit(solution)/shard_map/reduce_scatter | solution.py:74
Sparse Core Ops, SparseCore 0:
  433.7 261.5 reduce-scatter.2
  700.5 258.9 reduce-scatter.4
where the time goes:
time: 989 us; the launch traced here: 986 us
  waiting for transfers between devices  651 us (66%)
  matrix products  121 us (12%)
  local copies, waits for them, and re-layouts  50.4 us (5%)
  starting transfers between devices  46.2 us (5%)
  loops' own time  43.5 us (4%)
  other arithmetic  41.4 us (4%)
  blocking collectives  17.8 us (2%)
  between operations  14.9 us (2%)
    reduce_scatter x1, waiting for transfers between devices, local(): lax.psum_scatter(hamil_part, 'region', scatter_dimension=1, tiled=True)  264 us
    reduce_scatter x1, waiting for transfers between devices, local(): lax.psum_scatter(intersection_part, 'region', scatter_dimension=1, tiled=...  256 us
    all_to_all x1, waiting for transfers between devices, local(): lax.all_to_all(phi, 'region', split_axis=1, concat_axis=0, tiled=True)  96.7 us
    dot_general x32, matrix products, pair_terms(): lax.dot_general(left_rows, ham_rows, contract_dims, preferred_element_typ...  60.8 us
    dot_general x32, matrix products, pair_terms(): lax.dot_general(left_rows, right_rows, contract_dims, preferred_element_t...  60.5 us
    another operation x1, loops' own time, local(): intersection_part, hamil_part = lax.map(pair_terms, pair_list)  43.2 us
    ppermute x2, waiting for transfers between devices, padded_2(): lax.ppermute(lax.slice_in_dim(block, block.shape[dim] - width, None, axis...  31.1 us
  transfers between devices with their start and end apart: 8, of which 7 were waited for; matrix products, arithmetic and copies ran while one was open for 16% of the time, Pallas kernels for 0%

commit v1 on v0

v1 whole, which is shorter than its diff:
```python
import functools

import jax
import jax.numpy as jnp
from jax import lax
from jax.experimental import pallas as pl
from jax.experimental.pallas import tpu as pltpu
from jax.sharding import Mesh, PartitionSpec as P

W = 128
NB = 8
ROWS = 8
DEPTH = 128
PLANES = 128
PAIRS = 32
ZD, XD, CD, YD = 16, 4, 2, 4
REGION = ("z", "x", "c")
F32 = jnp.float32
BF16 = jnp.bfloat16


def flag(support, block, plane):
    return (support[block * PLANES + plane] > 0).astype(F32)


def lane_neighbours(tile, lane):
    axis = tile.ndim - 1
    low = jnp.where(lane == 0, 0.0, pltpu.roll(tile, 1, axis))
    high = jnp.where(lane == DEPTH - 1, 0.0, pltpu.roll(tile, DEPTH - 1, axis))
    return low + high


def region_kernel(pairs, support, where, own, ahead, behind, below, above, pot,
                  mine, theirs, right, near, tmp_s, tmp_h):
    plane, core = where[0], where[1]
    nxt = lax.rem(plane + 1, PLANES)
    prv = lax.rem(plane + PLANES - 1, PLANES)
    lane = lax.broadcasted_iota(jnp.int32, (64, DEPTH), 1)

    @pl.loop(0, NB)
    def _(block):
        live_next = flag(support, block, nxt)
        live_prev = flag(support, block, prv)
        for y in range(ROWS):
            cols = slice(y * DEPTH, (y + 1) * DEPTH)
            centre_weight = 3.0 + pot[y : y + 1, :]
            for part in range(2):
                src = pl.ds(pl.multiple_of(block * 16 + part * 8, 8), 8)
                rows = slice(part * 64, part * 64 + 64)

                def tile(ref, *index):
                    return ref[(src,) + index].astype(F32).reshape(64, DEPTH)

                centre = tile(own, y)
                down = tile(own, y - 1) if y > 0 else tile(below)
                up = tile(own, y + 1) if y < ROWS - 1 else tile(above)
                if y < ROWS // 2:
                    beside, live = tile(ahead, y), live_next
                else:
                    beside, live = tile(behind, y - ROWS // 2), live_prev
                around = lane_neighbours(centre, lane) + down + up + beside * live
                applied = centre_weight * centre - 0.5 * around
                right[block, rows, cols] = centre.astype(BF16)
                right[block, 128 + part * 64 : 192 + part * 64, cols] = applied.astype(BF16)
                near[block, rows, cols] = beside.astype(BF16)

    contract = (((1,), (1,)), ((), ()))
    half = ROWS // 2 * DEPTH

    @pl.loop(0, PAIRS)
    def _(k):
        i, j = pairs[2 * k], pairs[2 * k + 1]
        live_j = flag(support, j, plane)
        both = flag(support, i, plane) * live_j
        up_scale = -0.5 * live_j * flag(support, j, nxt) * flag(support, i, nxt)
        down_scale = -0.5 * live_j * flag(support, j, prv) * flag(support, i, prv)
        product = lax.dot_general(right[i, 0:W, :], right[j], contract, preferred_element_type=F32)
        cross_up = lax.dot_general(near[i, :, 0:half], right[j, 0:W, 0:half], contract,
                                   preferred_element_type=F32)
        cross_down = lax.dot_general(near[i, :, half:], right[j, 0:W, half:], contract,
                                     preferred_element_type=F32)
        tmp_s[...] = product[:, 0:W] * both
        tmp_h[...] = product[:, W:] * both + cross_up * up_scale + cross_down * down_scale
        group, member = k // 8, lax.rem(k, 8)
        for x in range(XD):
            keep = pl.ds(2 * x + core, ZD, stride=8)
            give = pl.ds(2 * x + 1 - core, ZD, stride=8)
            mine[x, group, member, :, 0:W] = tmp_s[keep, :]
            mine[x, group, member, :, W:] = tmp_h[keep, :]
            theirs[x, group, member, :, 0:W] = tmp_s[give, :]
            theirs[x, group, member, :, W:] = tmp_h[give, :]


def region_products(pair_flat, support_flat, where, own, ahead, behind, below, above, pot):
    vmem = pl.BlockSpec(memory_space=pltpu.VMEM)
    smem = pl.BlockSpec(memory_space=pltpu.SMEM)
    part = jax.ShapeDtypeStruct((XD, YD, 8, ZD, 2 * W), F32)
    return pl.pallas_call(
        region_kernel,
        out_shape=(part, part),
        in_specs=[smem] * 3 + [vmem] * 6,
        out_specs=(vmem, vmem),
        scratch_shapes=[
            pltpu.VMEM((NB, 2 * W, ROWS * DEPTH), BF16),
            pltpu.VMEM((NB, W, ROWS * DEPTH), BF16),
            pltpu.VMEM((W, W), F32),
            pltpu.VMEM((W, W), F32),
        ],
        compiler_params=pltpu.CompilerParams(vmem_limit_bytes=40 << 20),
        name="region_products",
    )(pair_flat, support_flat, where, own, ahead, behind, below, above, pot)


def orbital_kernel(support, where, phi, below, above, pot, out):
    block = where[2]
    lane = lax.broadcasted_iota(jnp.int32, (8, ROWS, DEPTH), 2)
    row = lax.broadcasted_iota(jnp.int32, (8, ROWS, DEPTH), 1)

    def masked(x):
        return phi[:, x].astype(F32) * flag(support, block, x)

    def step(x, carry):
        before, _ = carry
        centre = phi[:, x].astype(F32)
        after = masked(lax.rem(x + 1, PLANES))
        low = jnp.where(row == 0, below[:, x].astype(F32), pltpu.roll(centre, 1, 1))
        high = jnp.where(row == ROWS - 1, above[:, x].astype(F32), pltpu.roll(centre, ROWS - 1, 1))
        around = lane_neighbours(centre, lane) + low + high + before + after
        live = flag(support, block, x)
        applied = ((3.0 + pot[x])[None] * centre - 0.5 * around) * live
        out[:, x] = applied.astype(BF16)
        return centre * live, 0

    lax.fori_loop(0, PLANES, step, (masked(PLANES - 1), 0))


def orbital_apply(support_flat, where, phi, below, above, pot):
    vmem = pl.BlockSpec(memory_space=pltpu.VMEM)
    smem = pl.BlockSpec(memory_space=pltpu.SMEM)
    return pl.pallas_call(
        orbital_kernel,
        out_shape=jax.ShapeDtypeStruct(phi.shape, BF16),
        in_specs=[smem] * 2 + [vmem] * 4,
        out_specs=vmem,
        compiler_params=pltpu.CompilerParams(vmem_limit_bytes=24 << 20),
        name="orbital_apply",
    )(support_flat, where, phi, below, above, pot)


def ring(count, shift):
    return [(i, (i + shift) % count) for i in range(count)]


def local(phi, potential, pair_list, support):
    region = lax.axis_index(REGION)
    core = lax.axis_index("c")
    where = jnp.stack([region, core, region // 16]).astype(jnp.int32)
    pair_flat = pair_list.reshape(-1)
    support_flat = support.reshape(-1)

    own = lax.all_to_all(phi.transpose(1, 2, 0, 3), REGION, split_axis=0, concat_axis=0, tiled=True)
    ahead = lax.ppermute(own[:, :4], REGION, ring(PLANES, -1))
    behind = lax.ppermute(own[:, 4:], REGION, ring(PLANES, 1))
    below = lax.ppermute(own[:, 7], "y", ring(YD, 1))
    above = lax.ppermute(own[:, 0], "y", ring(YD, -1))
    mine, theirs = region_products(pair_flat, support_flat, where, own, ahead, behind, below, above,
                                   potential[0])
    total = mine + lax.ppermute(theirs, "c", [(0, 1), (1, 0)])
    shares = lax.all_to_all(total.reshape(XD * YD, 8, ZD, 2 * W), ("x", "y"), split_axis=0,
                            concat_axis=0, tiled=True)
    partial = jnp.sum(shares, axis=0).transpose(1, 0, 2)
    shares = lax.all_to_all(partial, ("z",), split_axis=0, concat_axis=0, tiled=True)
    result = jnp.sum(shares, axis=0)

    pot_all = lax.all_gather(potential, REGION, axis=0, tiled=True)
    row_below = lax.ppermute(phi[:, :, 7:], "y", ring(YD, 1))
    row_above = lax.ppermute(phi[:, :, :1], "y", ring(YD, -1))
    hphi = orbital_apply(support_flat, where, phi, row_below, row_above, pot_all)
    return result[:, :W], result[:, W:], hphi


def solution(mesh):
    fine = Mesh(mesh.devices.reshape(ZD, XD, CD, YD), ("z", "x", "c", "y"))
    in_specs = (P(REGION, None, "y", None), P(REGION, "y", None), P(), P())
    out_specs = (P("y", REGION), P("y", REGION), P(REGION, None, "y", None))
    return jax.shard_map(local, mesh=fine, in_specs=in_specs, out_specs=out_specs, check_vma=False)
```

time: 989 us -> 321 us (0.32)
  waiting for transfers between devices: 651 us -> 10 us
  blocking collectives: 17.8 us -> 234 us
  matrix products: 121 us -> 0 us
  loops' own time: 43.5 us -> 0 us
  local copies, waits for them, and re-layouts: 50.4 us -> 9.08 us
  other arithmetic: 41.4 us -> 2.56 us
  Pallas kernels: 0 us -> 30.7 us
  starting transfers between devices: 46.2 us -> 30.6 us
  between operations: 14.9 us -> 0.79 us
    reduce_scatter x2 -> x0, waiting for transfers between devices: 520 us -> none  [the longest x1 264 us: local(): lax.psum_scatter(hamil_part, 'region', scatter_dimension=1, tiled=True)]
    all_to_all x0 -> x2, blocking collectives: none -> 151 us  [the longest x1 116 us: local(): lax.all_to_all(phi.transpose(1, 2, 0, 3), REGION, split_axis=0, concat_ax...]
    dot_general x64 -> x0, matrix products: 121 us -> none  [the longest x32 60.8 us: pair_terms(): lax.dot_general(left_rows, ham_rows, contract_dims, preferred_element_typ...]
    all_to_all x2 -> x1, waiting for transfers between devices: 96.7 us -> 0.01 us  [local(): lax.all_to_all(partial, ('z',), split_axis=0, concat_axis=0, tiled=True)]
    all_gather x0 -> x1, blocking collectives: none -> 83.7 us  [local(): pot_all = lax.all_gather(potential, REGION, axis=0, tiled=True)]
    another operation x2 -> x0, loops' own time: 43.5 us -> none  [the longest x1 43.2 us: local(): intersection_part, hamil_part = lax.map(pair_terms, pair_list)]
    pallas_call x0 -> x2, Pallas kernels: none -> 30.7 us  [the longest x1 17.1 us: region_products(): pl.pallas_call(region_kernel, out_shape=(part, part), in_specs=[smem] * 3...]
    all_to_all x2 -> x1, starting transfers between devices: 33.5 us -> 8.34 us  [local(): lax.all_to_all(partial, ('z',), split_axis=0, concat_axis=0, tiled=True)]
  transfers between devices with their start and end apart: 8 -> 8, of which waited for: 7 -> 4; matrix products, arithmetic and copies ran while one was open for 16% -> 1% of each run, Pallas kernels for 0% -> 4%
where the time goes in v1:
time: 321 us; the launch traced here: 318 us
  blocking collectives  234 us (73%)
  Pallas kernels  30.7 us (10%)
  starting transfers between devices  30.6 us (10%)
  waiting for transfers between devices  10 us (3%)
  local copies, waits for them, and re-layouts  9.08 us (3%)
    all_to_all x1, blocking collectives, local(): lax.all_to_all(phi.transpose(1, 2, 0, 3), REGION, split_axis=0, concat_ax...  116 us
    all_gather x1, blocking collectives, local(): pot_all = lax.all_gather(potential, REGION, axis=0, tiled=True)  83.7 us
    all_to_all x1, blocking collectives, local(): lax.all_to_all(total.reshape(XD * YD, 8, ZD, 2 * W), ('x', 'y'), split_ax...  34.4 us
    pallas_call x1, Pallas kernels, region_products(): pl.pallas_call(region_kernel, out_shape=(part, part), in_specs=[smem] * 3...  17.1 us
    pallas_call x1, Pallas kernels, orbital_apply(): pl.pallas_call(orbital_kernel, out_shape=jax.ShapeDtypeStruct(phi.shape,...  13.6 us
    all_to_all x1, starting transfers between devices, local(): lax.all_to_all(partial, ('z',), split_axis=0, concat_axis=0, tiled=True)  8.34 us
  transfers between devices with their start and end apart: 8, of which 4 were waited for; matrix products, arithmetic and copies ran while one was open for 1% of the time, Pallas kernels for 4%

profile of v1, /device:TPU:6, one launch (start us, length us, event | category | flops | bytes accessed | tf_op | source)
XLA Modules:
  0.0 318.1 jit_solution(10254738691484757144)
XLA Ops:
  0.6 4.0 %copy.29 = bf16[8,128,8,128]{3,0,2,1:T(8,128)(2,1)S(1)} copy(bf16[8,128,8,128]{3,2,1,0:T(8,128)(2,1)} %phi.1) | data formatting | bytes 4194304 | tf_op args[0]
  4.7 116.1 %all_to_all.15.own = bf16[128,8,8,128]{3,2,1,0:T(8,128)(2,1)S(1)} all-to-all(bf16[128,8,8,128]{3,2,1,0:T(8,128)(2,1)S(1)} %bitcast.22), channel_id=1, replica_groups=mesh['z'=16,'x'=4,'c'=2,'y'=4] {'z','x','c'}, dimensions={0} | all-to-all | bytes 4194304 | tf_op jit(solution)/shard_map/all_to_all | solution.py:161
  120.8 0.0 copy-start.3
  120.8 0.0 copy-start.1
  120.8 0.0 copy-start.2
  120.8 1.7 fusion.1
  122.5 3.2 %collective-permute-start = (bf16[128,4,8,128]{3,2,1,0:T(8,128)(2,1)}, bf16[128,4,8,128]{3,2,1,0:T(8,128)(2,1)S(1)}, u32[]{:S(2)}, u32[]{:S(2)}) collective-permute-start(bf16[128,4,8,128]{3,2,1,0:T(8,128)(2,1)} %get-tuple-element.12), channel_id=1, source_target_pairs={{0,508},{4,0},{8,4},{12,8},{16,12},{20,16},{24,20},{28,24},{32,28}... | collective-permute-start | bytes 3145736 | tf_op jit(solution)/shard_map/ppermute | solution.py:162
  125.7 1.9 collective-permute-start.1
  127.7 0.9 slice_bitcast_fusion
  128.5 3.5 %collective-permute-start.2 = (bf16[128,8,128]{2,1,0:T(8,128)(2,1)}, bf16[128,8,128]{2,1,0:T(8,128)(2,1)S(1)}, u32[]{:S(2)}, u32[]{:S(2)}) collective-permute-start(bf16[128,8,128]{2,1,0:T(8,128)(2,1)} %get-tuple-element.10), channel_id=1, source_target_pairs={{0,1},{1,2},{2,3},{3,0},{4,5},{5,6},{6,7},{7,4},{8,9},{9,10},{10,1... | collective-permute-start | bytes 786440 | tf_op jit(solution)/shard_map/ppermute | solution.py:164
  132.0 3.6 %collective-permute-start.3 = (bf16[128,8,128]{2,1,0:T(8,128)(2,1)}, bf16[128,8,128]{2,1,0:T(8,128)(2,1)}, u32[]{:S(2)}, u32[]{:S(2)}) collective-permute-start(bf16[128,8,128]{2,1,0:T(8,128)(2,1)} %get-tuple-element.9), channel_id=1, source_target_pairs={{0,3},{1,0},{2,1},{3,2},{4,7},{5,4},{6,5},{7,6},{8,11},{9,8},{10,9... | collective-permute-start | bytes 786440 | tf_op jit(solution)/shard_map/ppermute | solution.py:165
  135.6 0.0 copy-done.3
  135.6 0.1 copy.21
  135.7 0.1 reshape.15.pairs
  135.8 0.1 pad_add_fusion.where
  135.9 2.6 collective-permute-done.2.below
  138.5 2.7 collective-permute-done.3.above
  141.2 0.0 collective-permute-done.ahead
  141.2 0.9 collective-permute-done.1.behind
  142.2 0.0 copy-done.1
  142.2 0.0 copy-done.2
  142.2 17.1 %region_products.1 = (f32[4,4,8,16,256]{4,3,2,1,0:T(8,128)S(1)}, f32[4,4,8,16,256]{4,3,2,1,0:T(8,128)S(1)}) custom-call(s32[64]{0:T(128)S(1)} %reshape.15.pairs, s32[1024]{0:T(1024)S(1)} %bitcast.19, s32[3]{0:T(128)S(1)} %pad_add_fusion.where, bf16[128,8,8,128]{3,2,1,0:T(8,128)(2,1)S(1)} %all_to_all.15.own, ...), custom_call_target="tpu_custom_call" | custom-call | tf_op jit(solution)/shard_map/region_products/pallas_call | solution.py:98
  159.3 3.0 collective-permute-start.4
  162.3 3.8 %collective-permute-done.4 = f32[4,4,8,16,256]{4,3,2,1,0:T(8,128)S(1)} collective-permute-done((f32[4,4,8,16,256]{4,3,2,1,0:T(8,128)S(1)}, f32[4,4,8,16,256]{4,3,2,1,0:T(8,128)S(1)}, u32[]{:S(2)}, u32[]{:S(2)}) %collective-permute-start.4) | collective-permute-done | bytes 2097184 | tf_op jit(solution)/shard_map/ppermute | solution.py:168
  166.1 0.5 add.12
  166.6 34.4 %all_to_all.16 = f32[16,8,16,256]{3,2,1,0:T(8,128)} all-to-all(f32[16,8,16,256]{3,2,1,0:T(8,128)S(1)} %bitcast.21), channel_id=1, replica_groups=mesh['z'=16,'x'=4,'c'=2,'y'=4] {'x','y'}, dimensions={0} | all-to-all | bytes 4194304 | tf_op jit(solution)/shard_map/all_to_all | solution.py:169
  201.1 0.0 copy-start
  201.1 1.9 reduce_sum.18
  203.0 0.7 copy.25
  203.7 8.3 %all-to-all-start.2 = ((f32[16,8,256]{2,1,0:T(8,128)}), f32[16,8,256]{2,1,0:T(8,128)S(1)}, u32[]{:S(2)}, u32[]{:S(2)}) async-start(f32[16,8,256]{2,1,0:T(8,128)} %copy.25), calls=%async_computation.2 | async-start | bytes 262144 | tf_op jit(solution)/shard_map/all_to_all | solution.py:172
  212.1 0.0 copy-done
  212.1 0.9 fusion
  213.0 2.5 collective-permute-start.5
  215.5 4.6 %collective-permute-start.6 = (bf16[8,128,1,128]{3,2,1,0:T(2,128)(2,1)S(1)}, bf16[8,128,1,128]{3,2,1,0:T(2,128)(2,1)S(1)}, u32[]{:S(2)}, u32[]{:S(2)}) collective-permute-start(bf16[8,128,1,128]{3,2,1,0:T(2,128)(2,1)S(1)} %get-tuple-element.7), channel_id=1, source_target_pairs={{0,3},{1,0},{2,1},{3,2},{4,7},{5,4},{6,5},{7,6},{8,11},{9,8},{10,9... | collective-permute-start | bytes 786440 | tf_op jit(solution)/shard_map/ppermute | solution.py:177
  220.1 83.7 %all_gather.3.pot = f32[128,8,128]{2,1,0:T(8,128)S(1)} all-gather(f32[1,8,128]{2,1,0:T(8,128)S(1)} %copy-done.1), channel_id=1, replica_groups=mesh['z'=16,'x'=4,'c'=2,'y'=4] {'z','x','c'}, dimensions={0}, use_global_device_ids=true | all-gather | bytes 528384 | tf_op jit(solution)/shard_map/all_gather | solution.py:175
  303.8 0.0 collective-permute-done.5.below
  303.8 0.0 collective-permute-done.6.above
  303.8 13.6 %orbital_apply.1 = bf16[8,128,8,128]{3,2,1,0:T(8,128)(2,1)} custom-call(s32[1024]{0:T(1024)S(1)} %bitcast.20, s32[3]{0:T(128)S(1)} %pad_add_fusion.where, bf16[8,128,8,128]{3,2,1,0:T(8,128)(2,1)S(1)} %copy-done, bf16[8,128,1,128]{3,2,1,0:T(2,128)(2,1)S(1)} %collective-permute-done.5.below, bf16[8,128,1,128]{3,2,1,0:T(2,128)(2,1)S(1)} %collective-permute-done.6.above, ...), custom_call_target="tpu_custom_call" | custom-call | tf_op jit(solution)/shard_map/orbital_apply/pallas_call | solution.py:140
  317.4 0.0 all-to-all-done.2
  317.5 0.6 fusion.2
  (1 shorter events, 0.0 us)
Async XLA Ops:
  120.8 14.8 %copy-start.3 = (s32[32,2]{0,1:T(2,128)S(1)}, s32[32,2]{0,1:T(2,128)}, u32[]{:S(2)}) copy-start(s32[32,2]{0,1:T(2,128)} %param.6) | copy-start | bytes 772
  120.8 21.4 %copy-start.1 = (f32[1,8,128]{2,1,0:T(8,128)S(1)}, f32[1,8,128]{2,1,0:T(8,128)}, u32[]{:S(2)}) copy-start(f32[1,8,128]{2,1,0:T(8,128)} %param.5) | copy-start | bytes 12292
  120.8 21.4 %copy-start.2 = (s32[8,128]{1,0:T(8,128)S(1)}, s32[8,128]{1,0:T(8,128)}, u32[]{:S(2)}) copy-start(s32[8,128]{1,0:T(8,128)} %param.7) | copy-start | bytes 12292
  122.5 18.7 %collective-permute-start = (bf16[128,4,8,128]{3,2,1,0:T(8,128)(2,1)}, bf16[128,4,8,128]{3,2,1,0:T(8,128)(2,1)S(1)}, u32[]{:S(2)}, u32[]{:S(2)}) collective-permute-start(bf16[128,4,8,128]{3,2,1,0:T(8,128)(2,1)} %get-tuple-element.12), channel_id=1, source_target_pairs={{0,508},{4,0},{8,4},{12,8},{16,12},{20,16},{24,20},{28,24},{32,28}... | collective-permute-start | bytes 3145736 | tf_op jit(solution)/shard_map/ppermute | solution.py:162
  125.7 16.4 %collective-permute-start.1 = (bf16[128,4,8,128]{3,2,1,0:T(8,128)(2,1)}, bf16[128,4,8,128]{3,2,1,0:T(8,128)(2,1)}, u32[]{:S(2)}, u32[]{:S(2)}) collective-permute-start(bf16[128,4,8,128]{3,2,1,0:T(8,128)(2,1)} %get-tuple-element.11), channel_id=1, source_target_pairs={{0,4},{4,8},{8,12},{12,16},{16,20},{20,24},{24,28},{28,32},{32,36}... | collective-permute-start | bytes 3145736 | tf_op jit(solution)/shard_map/ppermute | solution.py:163
  128.5 9.9 %collective-permute-start.2 = (bf16[128,8,128]{2,1,0:T(8,128)(2,1)}, bf16[128,8,128]{2,1,0:T(8,128)(2,1)S(1)}, u32[]{:S(2)}, u32[]{:S(2)}) collective-permute-start(bf16[128,8,128]{2,1,0:T(8,128)(2,1)} %get-tuple-element.10), channel_id=1, source_target_pairs={{0,1},{1,2},{2,3},{3,0},{4,5},{5,6},{6,7},{7,4},{8,9},{9,10},{10,1... | collective-permute-start | bytes 786440 | tf_op jit(solution)/shard_map/ppermute | solution.py:164
  132.0 9.2 %collective-permute-start.3 = (bf16[128,8,128]{2,1,0:T(8,128)(2,1)}, bf16[128,8,128]{2,1,0:T(8,128)(2,1)}, u32[]{:S(2)}, u32[]{:S(2)}) collective-permute-start(bf16[128,8,128]{2,1,0:T(8,128)(2,1)} %get-tuple-element.9), channel_id=1, source_target_pairs={{0,3},{1,0},{2,1},{3,2},{4,7},{5,4},{6,5},{7,6},{8,11},{9,8},{10,9... | collective-permute-start | bytes 786440 | tf_op jit(solution)/shard_map/ppermute | solution.py:165
  159.3 6.8 %collective-permute-start.4 = (f32[4,4,8,16,256]{4,3,2,1,0:T(8,128)S(1)}, f32[4,4,8,16,256]{4,3,2,1,0:T(8,128)S(1)}, u32[]{:S(2)}, u32[]{:S(2)}) collective-permute-start(f32[4,4,8,16,256]{4,3,2,1,0:T(8,128)S(1)} %get-tuple-element.6), channel_id=1, source_target_pairs={{0,4},{4,0},{1,5},{5,1},{2,6},{6,2},{3,7},{7,3},{8,12},{12,8},{9,1... | collective-permute-start | bytes 6291464 | tf_op jit(solution)/shard_map/ppermute | solution.py:168
  201.1 11.0 %copy-start = (bf16[8,128,8,128]{3,2,1,0:T(8,128)(2,1)S(1)}, bf16[8,128,8,128]{3,2,1,0:T(8,128)(2,1)}, u32[]{:S(2)}) copy-start(bf16[8,128,8,128]{3,2,1,0:T(8,128)(2,1)} %phi.1) | copy-start | bytes 6291460
  203.7 113.7 %all-to-all-start.2 = ((f32[16,8,256]{2,1,0:T(8,128)}), f32[16,8,256]{2,1,0:T(8,128)S(1)}, u32[]{:S(2)}, u32[]{:S(2)}) async-start(f32[16,8,256]{2,1,0:T(8,128)} %copy.25), calls=%async_computation.2 | async-start | bytes 262144 | tf_op jit(solution)/shard_map/all_to_all | solution.py:172
  213.0 90.8 %collective-permute-start.5 = (bf16[8,128,1,128]{3,2,1,0:T(2,128)(2,1)S(1)}, bf16[8,128,1,128]{3,2,1,0:T(2,128)(2,1)S(1)}, u32[]{:S(2)}, u32[]{:S(2)}) collective-permute-start(bf16[8,128,1,128]{3,2,1,0:T(2,128)(2,1)S(1)} %get-tuple-element.8), channel_id=1, source_target_pairs={{0,1},{1,2},{2,3},{3,0},{4,5},{5,6},{6,7},{7,4},{8,9},{9,10},{10,1... | collective-permute-start | bytes 786440 | tf_op jit(solution)/shard_map/ppermute | solution.py:176
  215.5 88.3 %collective-permute-start.6 = (bf16[8,128,1,128]{3,2,1,0:T(2,128)(2,1)S(1)}, bf16[8,128,1,128]{3,2,1,0:T(2,128)(2,1)S(1)}, u32[]{:S(2)}, u32[]{:S(2)}) collective-permute-start(bf16[8,128,1,128]{3,2,1,0:T(2,128)(2,1)S(1)} %get-tuple-element.7), channel_id=1, source_target_pairs={{0,3},{1,0},{2,1},{3,2},{4,7},{5,4},{6,5},{7,6},{8,11},{9,8},{10,9... | collective-permute-start | bytes 786440 | tf_op jit(solution)/shard_map/ppermute | solution.py:177

commit v2 on v1

--- a/solution.py
+++ b/solution.py
@@ -127,7 +127,7 @@
         high = jnp.where(row == ROWS - 1, above[:, x].astype(F32), pltpu.roll(centre, ROWS - 1, 1))
         around = lane_neighbours(centre, lane) + low + high + before + after
         live = flag(support, block, x)
-        applied = ((3.0 + pot[x])[None] * centre - 0.5 * around) * live
+        applied = ((3.0 + pot[lax.rem(x, 8), x // 8])[None] * centre - 0.5 * around) * live
         out[:, x] = applied.astype(BF16)
         return centre * live, 0
 
@@ -159,6 +159,12 @@
     support_flat = support.reshape(-1)
 
     own = lax.all_to_all(phi.transpose(1, 2, 0, 3), REGION, split_axis=0, concat_axis=0, tiled=True)
+    column = lax.all_gather(potential, "z", axis=0, tiled=True)
+    pot_all = lax.all_gather(column[None], ("x", "c"), axis=0, tiled=True)
+    row_below = lax.ppermute(phi[:, :, 7:], "y", ring(YD, 1))
+    row_above = lax.ppermute(phi[:, :, :1], "y", ring(YD, -1))
+    hphi = orbital_apply(support_flat, where, phi, row_below, row_above, pot_all)
+    own, hphi = lax.optimization_barrier((own, hphi))
     ahead = lax.ppermute(own[:, :4], REGION, ring(PLANES, -1))
     behind = lax.ppermute(own[:, 4:], REGION, ring(PLANES, 1))
     below = lax.ppermute(own[:, 7], "y", ring(YD, 1))
@@ -172,10 +178,6 @@
     shares = lax.all_to_all(partial, ("z",), split_axis=0, concat_axis=0, tiled=True)
     result = jnp.sum(shares, axis=0)
 
-    pot_all = lax.all_gather(potential, REGION, axis=0, tiled=True)
-    row_below = lax.ppermute(phi[:, :, 7:], "y", ring(YD, 1))
-    row_above = lax.ppermute(phi[:, :, :1], "y", ring(YD, -1))
-    hphi = orbital_apply(support_flat, where, phi, row_below, row_above, pot_all)
     return result[:, :W], result[:, W:], hphi
 
 

time: 321 us -> 278 us (0.87)
  blocking collectives: 234 us -> 176 us
  starting transfers between devices: 30.6 us -> 40.5 us
  local copies, waits for them, and re-layouts: 9.08 us -> 14.7 us
    all_to_all x1, blocking collectives: 116 us -> 24.5 us  [local(): lax.all_to_all(partial, ('z',), split_axis=0, concat_axis=0, tiled=True)]
    all_gather x1 -> x2, blocking collectives: 83.7 us -> 118 us  [the longest x1 104 us: local(): column = lax.all_gather(potential, 'z', axis=0, tiled=True)]
    all_to_all x1, starting transfers between devices: 8.34 us -> 19.4 us  [local(): lax.all_to_all(phi.transpose(1, 2, 0, 3), REGION, split_axis=0, concat_ax...]
    slice x1, local copies, waits for them, and re-layouts: 0.94 us -> 4.26 us  [local(): row_above = lax.ppermute(phi[:, :, :1], 'y', ring(YD, -1))]
  transfers between devices with their start and end apart: 8 -> 8, of which waited for: 4 -> 3; matrix products, arithmetic and copies ran while one was open for 1% -> 2% of each run, Pallas kernels for 4% -> 5%
where the time goes in v2:
time: 278 us; the launch traced here: 277 us
  blocking collectives  176 us (63%)
  starting transfers between devices  40.5 us (15%)
  Pallas kernels  30.8 us (11%)
  local copies, waits for them, and re-layouts  14.7 us (5%)
  waiting for transfers between devices  12.5 us (4%)
    all_gather x1, blocking collectives, local(): column = lax.all_gather(potential, 'z', axis=0, tiled=True)  104 us
    all_to_all x1, blocking collectives, local(): lax.all_to_all(total.reshape(XD * YD, 8, ZD, 2 * W), ('x', 'y'), split_ax...  33.5 us
    all_to_all x1, blocking collectives, local(): lax.all_to_all(partial, ('z',), split_axis=0, concat_axis=0, tiled=True)  24.5 us
    all_to_all x1, starting transfers between devices, local(): lax.all_to_all(phi.transpose(1, 2, 0, 3), REGION, split_axis=0, concat_ax...  19.4 us
    pallas_call x1, Pallas kernels, region_products(): pl.pallas_call(region_kernel, out_shape=(part, part), in_specs=[smem] * 3...  17.2 us
    pallas_call x1, Pallas kernels, orbital_apply(): pl.pallas_call(orbital_kernel, out_shape=jax.ShapeDtypeStruct(phi.shape,...  13.6 us
    all_gather x1, blocking collectives, local(): pot_all = lax.all_gather(column[None], ('x', 'c'), axis=0, tiled=True)  13.1 us
    unnamed x10, local copies, waits for them, and re-layouts  7.05 us
  transfers between devices with their start and end apart: 8, of which 3 were waited for; matrix products, arithmetic and copies ran while one was open for 2% of the time, Pallas kernels for 5%

profile of v2, /device:TPU:6, one launch (start us, length us, event | category | flops | bytes accessed | tf_op | source)
XLA Modules:
  0.0 277.1 jit_solution(8653781829768559644)
XLA Ops:
  0.6 5.4 %copy.29 = bf16[8,128,8,128]{3,0,2,1:T(8,128)(2,1)} copy(bf16[8,128,8,128]{3,2,1,0:T(8,128)(2,1)} %phi.1) | data formatting | bytes 4194304 | tf_op args[0]
  6.0 19.4 %all-to-all-start = ((bf16[128,8,8,128]{3,2,1,0:T(8,128)(2,1)}), bf16[128,8,8,128]{3,2,1,0:T(8,128)(2,1)S(1)}, u32[]{:S(2)}, u32[]{:S(2)}) async-start(bf16[128,8,8,128]{3,2,1,0:T(8,128)(2,1)} %bitcast.20), calls=%async_computation | async-start | bytes 4194304 | tf_op jit(solution)/shard_map/all_to_all | solution.py:161
  25.4 0.0 copy-start.1
  25.4 0.0 copy-start.2
  25.4 4.3 %fusion.1 = (bf16[8,128,1,128]{3,2,1,0:T(2,128)(2,1)}, bf16[8,128,1,128]{3,2,1,0:T(2,128)(2,1)}) fusion(bf16[8,128,8,128]{3,2,1,0:T(8,128)(2,1)} %phi.1), kind=kLoop, calls=%fused_computation.5 | loop fusion | bytes 1048576 | tf_op jit(solution)/shard_map/slice | solution.py:165
  29.6 4.9 %collective-permute-start.1 = (bf16[8,128,1,128]{3,2,1,0:T(2,128)(2,1)}, bf16[8,128,1,128]{3,2,1,0:T(2,128)(2,1)S(1)}, u32[]{:S(2)}, u32[]{:S(2)}) collective-permute-start(bf16[8,128,1,128]{3,2,1,0:T(2,128)(2,1)} %get-tuple-element.15), channel_id=1, source_target_pairs={{0,3},{1,0},{2,1},{3,2},{4,7},{5,4},{6,5},{7,6},{8,11},{9,8},{10,9... | collective-permute-start | bytes 786440 | tf_op jit(solution)/shard_map/ppermute | solution.py:165
  34.6 1.9 collective-permute-start
  36.5 0.1 pad_add_fusion.where
  36.6 0.0 copy-done.1
  36.6 104.5 %all_gather.6 = f32[16,8,128]{2,1,0:T(8,128)S(1)} all-gather(f32[1,8,128]{2,1,0:T(8,128)S(1)} %copy-done.1), channel_id=1, replica_groups=mesh['z'=16,'x'=4,'c'=2,'y'=4] {'z'}, dimensions={0}, use_global_device_ids=true | all-gather | bytes 69632 | tf_op jit(solution)/shard_map/all_gather | solution.py:162
  141.1 13.1 %all-gather = f32[128,8,128]{2,1,0:T(8,128)S(1)} all-gather(f32[16,8,128]{2,1,0:T(8,128)S(1)} %all_gather.6), channel_id=2, replica_groups=mesh['z'=16,'x'=4,'c'=2,'y'=4] {'x','c'}, dimensions={0}, use_global_device_ids=true | all-gather | bytes 589824 | tf_op jit(solution)/shard_map/all_gather | solution.py:163
  154.2 0.0 collective-permute-done.1.above
  154.2 0.0 collective-permute-done.below
  154.2 0.0 copy-done.2
  154.2 0.0 copy-start
  154.2 1.6 copy-done
  155.8 13.6 %orbital_apply.1 = bf16[8,128,8,128]{3,2,1,0:T(8,128)(2,1)} custom-call(s32[1024]{0:T(1024)S(1)} %bitcast.17, s32[3]{0:T(128)S(1)} %pad_add_fusion.where, bf16[8,128,8,128]{3,2,1,0:T(8,128)(2,1)S(1)} %copy-done, bf16[8,128,1,128]{3,2,1,0:T(2,128)(2,1)S(1)} %collective-permute-done.below, bf16[8,128,1,128]{3,2,1,0:T(2,128)(2,1)S(1)} %collective-permute-done.1.above, ...), custom_call_target="tpu_custom_call" | custom-call | tf_op jit(solution)/shard_map/orbital_apply/pallas_call | solution.py:140
  169.3 0.0 copy-start.3
  169.4 0.0 all-to-all-done.own
  169.4 1.7 fusion
  171.1 2.2 collective-permute-start.3
  173.3 3.3 %collective-permute-start.2 = (bf16[128,4,8,128]{3,2,1,0:T(8,128)(2,1)}, bf16[128,4,8,128]{3,2,1,0:T(8,128)(2,1)}, u32[]{:S(2)}, u32[]{:S(2)}) collective-permute-start(bf16[128,4,8,128]{3,2,1,0:T(8,128)(2,1)} %get-tuple-element.14), channel_id=1, source_target_pairs={{0,508},{4,0},{8,4},{12,8},{16,12},{20,16},{24,20},{28,24},{32,28}... | collective-permute-start | bytes 3145736 | tf_op jit(solution)/shard_map/ppermute | solution.py:168
  176.6 0.9 slice_bitcast_fusion
  177.5 4.9 %collective-permute-start.5 = (bf16[128,8,128]{2,1,0:T(8,128)(2,1)}, bf16[128,8,128]{2,1,0:T(8,128)(2,1)S(1)}, u32[]{:S(2)}, u32[]{:S(2)}) collective-permute-start(bf16[128,8,128]{2,1,0:T(8,128)(2,1)} %get-tuple-element.11), channel_id=1, source_target_pairs={{0,3},{1,0},{2,1},{3,2},{4,7},{5,4},{6,5},{7,6},{8,11},{9,8},{10,9... | collective-permute-start | bytes 786440 | tf_op jit(solution)/shard_map/ppermute | solution.py:171
  182.4 1.9 collective-permute-start.4
  184.4 0.0 copy-done.3
  184.4 0.1 copy.21
  184.5 0.1 reshape.15.pairs
  184.6 3.0 %collective-permute-done.5.above = bf16[128,8,128]{2,1,0:T(8,128)(2,1)S(1)} collective-permute-done((bf16[128,8,128]{2,1,0:T(8,128)(2,1)}, bf16[128,8,128]{2,1,0:T(8,128)(2,1)S(1)}, u32[]{:S(2)}, u32[]{:S(2)}) %collective-permute-start.5) | collective-permute-done | bytes 262176 | tf_op jit(solution)/shard_map/ppermute | solution.py:171
  187.6 5.3 %collective-permute-done.4.below = bf16[128,8,128]{2,1,0:T(8,128)(2,1)} collective-permute-done((bf16[128,8,128]{2,1,0:T(8,128)(2,1)}, bf16[128,8,128]{2,1,0:T(8,128)(2,1)}, u32[]{:S(2)}, u32[]{:S(2)}) %collective-permute-start.4) | collective-permute-done | bytes 262176 | tf_op jit(solution)/shard_map/ppermute | solution.py:170
  192.9 0.0 collective-permute-done.3.behind
  192.9 0.0 collective-permute-done.2.ahead
  192.9 17.2 %region_products.1 = (f32[4,4,8,16,256]{4,3,2,1,0:T(8,128)S(1)}, f32[4,4,8,16,256]{4,3,2,1,0:T(8,128)S(1)}) custom-call(s32[64]{0:T(128)S(1)} %reshape.15.pairs, s32[1024]{0:T(1024)S(1)} %bitcast.18, s32[3]{0:T(128)S(1)} %pad_add_fusion.where, bf16[128,8,8,128]{3,2,1,0:T(8,128)(2,1)S(1)} %all-to-all-done.own, ...), custom_call_target="tpu_custom_call" | custom-call | tf_op jit(solution)/shard_map/region_products/pallas_call | solution.py:98
  210.1 1.9 collective-permute-start.6
  212.0 4.1 %collective-permute-done.6 = f32[4,4,8,16,256]{4,3,2,1,0:T(8,128)S(1)} collective-permute-done((f32[4,4,8,16,256]{4,3,2,1,0:T(8,128)S(1)}, f32[4,4,8,16,256]{4,3,2,1,0:T(8,128)S(1)}, u32[]{:S(2)}, u32[]{:S(2)}) %collective-permute-start.6) | collective-permute-done | bytes 2097184 | tf_op jit(solution)/shard_map/ppermute | solution.py:174
  216.1 0.5 add.12
  216.6 33.5 %all_to_all.15 = f32[16,8,16,256]{3,2,1,0:T(8,128)} all-to-all(f32[16,8,16,256]{3,2,1,0:T(8,128)S(1)} %bitcast.19), channel_id=1, replica_groups=mesh['z'=16,'x'=4,'c'=2,'y'=4] {'x','y'}, dimensions={0} | all-to-all | bytes 4194304 | tf_op jit(solution)/shard_map/all_to_all | solution.py:175
  250.1 1.8 reduce_sum.18
  251.9 0.1 copy.25
  252.0 24.5 %all_to_all.16 = f32[16,8,256]{2,1,0:T(8,128)S(1)} all-to-all(f32[16,8,256]{2,1,0:T(8,128)S(1)} %copy.25), channel_id=1, replica_groups=mesh['z'=16,'x'=4,'c'=2,'y'=4] {'z'}, dimensions={0} | all-to-all | bytes 262144 | tf_op jit(solution)/shard_map/all_to_all | solution.py:178
  276.5 0.6 fusion.2
  (1 shorter events, 0.0 us)
Async XLA Ops:
  6.0 163.4 %all-to-all-start = ((bf16[128,8,8,128]{3,2,1,0:T(8,128)(2,1)}), bf16[128,8,8,128]{3,2,1,0:T(8,128)(2,1)S(1)}, u32[]{:S(2)}, u32[]{:S(2)}) async-start(bf16[128,8,8,128]{3,2,1,0:T(8,128)(2,1)} %bitcast.20), calls=%async_computation | async-start | bytes 4194304 | tf_op jit(solution)/shard_map/all_to_all | solution.py:161
  25.4 11.2 %copy-start.1 = (f32[1,8,128]{2,1,0:T(8,128)S(1)}, f32[1,8,128]{2,1,0:T(8,128)}, u32[]{:S(2)}) copy-start(f32[1,8,128]{2,1,0:T(8,128)} %param.5) | copy-start | bytes 12292
  25.4 128.8 %copy-start.2 = (s32[8,128]{1,0:T(8,128)S(1)}, s32[8,128]{1,0:T(8,128)}, u32[]{:S(2)}) copy-start(s32[8,128]{1,0:T(8,128)} %param.7) | copy-start | bytes 12292
  29.6 124.5 %collective-permute-start.1 = (bf16[8,128,1,128]{3,2,1,0:T(2,128)(2,1)}, bf16[8,128,1,128]{3,2,1,0:T(2,128)(2,1)S(1)}, u32[]{:S(2)}, u32[]{:S(2)}) collective-permute-start(bf16[8,128,1,128]{3,2,1,0:T(2,128)(2,1)} %get-tuple-element.15), channel_id=1, source_target_pairs={{0,3},{1,0},{2,1},{3,2},{4,7},{5,4},{6,5},{7,6},{8,11},{9,8},{10,9... | collective-permute-start | bytes 786440 | tf_op jit(solution)/shard_map/ppermute | solution.py:165
  34.6 119.6 %collective-permute-start = (bf16[8,128,1,128]{3,2,1,0:T(2,128)(2,1)}, bf16[8,128,1,128]{3,2,1,0:T(2,128)(2,1)S(1)}, u32[]{:S(2)}, u32[]{:S(2)}) collective-permute-start(bf16[8,128,1,128]{3,2,1,0:T(2,128)(2,1)} %get-tuple-element.16), channel_id=1, source_target_pairs={{0,1},{1,2},{2,3},{3,0},{4,5},{5,6},{6,7},{7,4},{8,9},{9,10},{10,1... | collective-permute-start | bytes 786440 | tf_op jit(solution)/shard_map/ppermute | solution.py:164
  154.2 1.6 copy-start
  169.3 15.0 %copy-start.3 = (s32[32,2]{0,1:T(2,128)S(1)}, s32[32,2]{0,1:T(2,128)}, u32[]{:S(2)}) copy-start(s32[32,2]{0,1:T(2,128)} %param.6) | copy-start | bytes 772
  171.1 21.8 %collective-permute-start.3 = (bf16[128,4,8,128]{3,2,1,0:T(8,128)(2,1)}, bf16[128,4,8,128]{3,2,1,0:T(8,128)(2,1)S(1)}, u32[]{:S(2)}, u32[]{:S(2)}) collective-permute-start(bf16[128,4,8,128]{3,2,1,0:T(8,128)(2,1)} %get-tuple-element.13), channel_id=1, source_target_pairs={{0,4},{4,8},{8,12},{12,16},{16,20},{20,24},{24,28},{28,32},{32,36}... | collective-permute-start | bytes 3145736 | tf_op jit(solution)/shard_map/ppermute | solution.py:169
  173.3 19.6 %collective-permute-start.2 = (bf16[128,4,8,128]{3,2,1,0:T(8,128)(2,1)}, bf16[128,4,8,128]{3,2,1,0:T(8,128)(2,1)}, u32[]{:S(2)}, u32[]{:S(2)}) collective-permute-start(bf16[128,4,8,128]{3,2,1,0:T(8,128)(2,1)} %get-tuple-element.14), channel_id=1, source_target_pairs={{0,508},{4,0},{8,4},{12,8},{16,12},{20,16},{24,20},{28,24},{32,28}... | collective-permute-start | bytes 3145736 | tf_op jit(solution)/shard_map/ppermute | solution.py:168
  177.5 10.1 %collective-permute-start.5 = (bf16[128,8,128]{2,1,0:T(8,128)(2,1)}, bf16[128,8,128]{2,1,0:T(8,128)(2,1)S(1)}, u32[]{:S(2)}, u32[]{:S(2)}) collective-permute-start(bf16[128,8,128]{2,1,0:T(8,128)(2,1)} %get-tuple-element.11), channel_id=1, source_target_pairs={{0,3},{1,0},{2,1},{3,2},{4,7},{5,4},{6,5},{7,6},{8,11},{9,8},{10,9... | collective-permute-start | bytes 786440 | tf_op jit(solution)/shard_map/ppermute | solution.py:171
  182.4 10.5 %collective-permute-start.4 = (bf16[128,8,128]{2,1,0:T(8,128)(2,1)}, bf16[128,8,128]{2,1,0:T(8,128)(2,1)}, u32[]{:S(2)}, u32[]{:S(2)}) collective-permute-start(bf16[128,8,128]{2,1,0:T(8,128)(2,1)} %get-tuple-element.12), channel_id=1, source_target_pairs={{0,1},{1,2},{2,3},{3,0},{4,5},{5,6},{6,7},{7,4},{8,9},{9,10},{10,1... | collective-permute-start | bytes 786440 | tf_op jit(solution)/shard_map/ppermute | solution.py:170
  210.1 6.1 %collective-permute-start.6 = (f32[4,4,8,16,256]{4,3,2,1,0:T(8,128)S(1)}, f32[4,4,8,16,256]{4,3,2,1,0:T(8,128)S(1)}, u32[]{:S(2)}, u32[]{:S(2)}) collective-permute-start(f32[4,4,8,16,256]{4,3,2,1,0:T(8,128)S(1)} %get-tuple-element.9), channel_id=1, source_target_pairs={{0,4},{4,0},{1,5},{5,1},{2,6},{6,2},{3,7},{7,3},{8,12},{12,8},{9,1... | collective-permute-start | bytes 6291464 | tf_op jit(solution)/shard_map/ppermute | solution.py:174

commit v3 on v2

v3 whole, which is shorter than its diff:
```python
import functools

import jax
import jax.numpy as jnp
from jax import lax
from jax.experimental import pallas as pl
from jax.experimental.pallas import tpu as pltpu
from jax.sharding import Mesh, PartitionSpec as P

W = 128
NB = 8
ROWS = 8
DEPTH = 128
PLANES = 128
PAIRS = 32
ZD, XD, CD, YD = 16, 4, 2, 4
REGION = ("z", "x", "c")
F32 = jnp.float32
BF16 = jnp.bfloat16


def flag(support, block, plane):
    return (support[block * PLANES + plane] > 0).astype(F32)


def lane_neighbours(tile, lane):
    axis = tile.ndim - 1
    low = jnp.where(lane == 0, 0.0, pltpu.roll(tile, 1, axis))
    high = jnp.where(lane == DEPTH - 1, 0.0, pltpu.roll(tile, DEPTH - 1, axis))
    return low + high


def split_rows(pairs, gram, core, mine, theirs):
    @pl.loop(0, PAIRS)
    def _(k):
        i, j = pairs[2 * k], pairs[2 * k + 1]
        group, member = k // 8, lax.rem(k, 8)
        for x in range(XD):
            mine[x, group, member] = gram[j, pl.ds(i * W + 2 * x + core, ZD, stride=8), :]
            theirs[x, group, member] = gram[j, pl.ds(i * W + 2 * x + 1 - core, ZD, stride=8), :]


def gram_blocks(left, right, gram):
    @pl.loop(0, NB // 2)
    def _(n):
        cols = pl.ds(pl.multiple_of(n * 2 * W, 2 * W), 2 * W)
        product = lax.dot_general(left[...], right[cols, :], (((1,), (1,)), ((), ())),
                                  preferred_element_type=F32)
        gram[2 * n] = product[:, 0:W]
        gram[2 * n + 1] = product[:, W:]


def overlap_kernel(pairs, support, where, own, conf, mine, theirs, gram):
    plane, core = where[0], where[1]

    @pl.loop(0, NB)
    def _(block):
        live = flag(support, block, plane)
        for y in range(ROWS):
            tile = own[pl.ds(block * 16, 16), y].astype(F32).reshape(W, DEPTH) * live
            conf[pl.ds(pl.multiple_of(block * W, W), W), y * DEPTH : (y + 1) * DEPTH] = tile.astype(BF16)

    gram_blocks(conf, conf, gram)
    split_rows(pairs, gram, core, mine, theirs)


def hamiltonian_kernel(pairs, support, where, conf, ahead, behind, above, pot,
                       mine, theirs, left, right, gram):
    plane, core = where[0], where[1]
    nxt = lax.rem(plane + 1, PLANES)
    prv = lax.rem(plane + PLANES - 1, PLANES)
    lane = lax.broadcasted_iota(jnp.int32, (64, DEPTH), 1)
    full = ROWS * DEPTH

    @pl.loop(0, 2 * NB)
    def _(half):
        block = half // 2
        live = flag(support, block, plane)
        live_next = flag(support, block, nxt)
        live_prev = flag(support, block, prv)
        src = pl.ds(pl.multiple_of(half * 8, 8), 8)
        rows = pl.ds(pl.multiple_of(half * 64, 64), 64)

        def row_of(y):
            return conf[rows, y * DEPTH : (y + 1) * DEPTH].astype(F32)

        def tile(ref, *index):
            return ref[(src,) + index].astype(F32).reshape(64, DEPTH)

        edge = tile(above) * live
        for y in range(ROWS):
            cols = slice(y * DEPTH, (y + 1) * DEPTH)
            more = slice(full + y * DEPTH, full + (y + 1) * DEPTH)
            centre = row_of(y)
            if y < ROWS // 2:
                beside, live_there = tile(ahead, y) * live_next, live_next
            else:
                beside, live_there = tile(behind, y - ROWS // 2) * live_prev, live_prev
            around = lane_neighbours(centre, lane) + beside * live
            around = around + (row_of(y + 1) if y < ROWS - 1 else edge)
            if y > 0:
                around = around + row_of(y - 1)
            applied = (3.0 + pot[y : y + 1, :]) * centre - 0.5 * around
            left[rows, cols] = centre.astype(BF16)
            left[rows, more] = beside.astype(BF16)
            right[rows, cols] = applied.astype(BF16)
            right[rows, more] = (centre * (-0.5 * live_there)).astype(BF16)
        last = slice(2 * full, 2 * full + DEPTH)
        left[rows, last] = edge.astype(BF16)
        right[rows, last] = (row_of(ROWS - 1) * -0.5).astype(BF16)

    gram_blocks(left, right, gram)
    split_rows(pairs, gram, core, mine, theirs)


VMEM = pl.BlockSpec(memory_space=pltpu.VMEM)
SMEM = pl.BlockSpec(memory_space=pltpu.SMEM)
SHARE = jax.ShapeDtypeStruct((XD, YD, 8, ZD, W), F32)
CELLS = ROWS * DEPTH


def overlap_products(pair_flat, support_flat, where, own):
    return pl.pallas_call(
        overlap_kernel,
        out_shape=(jax.ShapeDtypeStruct((NB * W, CELLS), BF16), SHARE, SHARE),
        in_specs=[SMEM] * 3 + [VMEM],
        out_specs=(VMEM,) * 3,
        scratch_shapes=[pltpu.VMEM((NB, NB * W, W), F32)],
        compiler_params=pltpu.CompilerParams(vmem_limit_bytes=20 << 20),
        name="overlap_products",
    )(pair_flat, support_flat, where, own)


def hamiltonian_products(pair_flat, support_flat, where, conf, ahead, behind, above, pot):
    return pl.pallas_call(
        hamiltonian_kernel,
        out_shape=(SHARE, SHARE),
        in_specs=[SMEM] * 3 + [VMEM] * 5,
        out_specs=(VMEM,) * 2,
        scratch_shapes=[
            pltpu.VMEM((NB * W, 2 * CELLS + DEPTH), BF16),
            pltpu.VMEM((NB * W, 2 * CELLS + DEPTH), BF16),
            pltpu.VMEM((NB, NB * W, W), F32),
        ],
        compiler_params=pltpu.CompilerParams(vmem_limit_bytes=32 << 20),
        name="hamiltonian_products",
    )(pair_flat, support_flat, where, conf, ahead, behind, above, pot)


def orbital_kernel(support, where, phi, below, above, pot, out):
    block, row_z = where[2], where[0] // 8
    lane = lax.broadcasted_iota(jnp.int32, (8, ROWS, DEPTH), 2)
    row = lax.broadcasted_iota(jnp.int32, (8, ROWS, DEPTH), 1)

    def masked(x):
        return phi[:, x].astype(F32) * flag(support, block, x)

    def step(x, carry):
        before, _ = carry
        centre = phi[:, x].astype(F32)
        after = masked(lax.rem(x + 1, PLANES))
        low = jnp.where(row == 0, below[:, x].astype(F32), pltpu.roll(centre, 1, 1))
        high = jnp.where(row == ROWS - 1, above[:, x].astype(F32), pltpu.roll(centre, ROWS - 1, 1))
        around = lane_neighbours(centre, lane) + low + high + before + after
        live = flag(support, block, x)
        applied = ((3.0 + pot[lax.rem(x, 8), lax.rem(x // 8 + ZD - row_z, ZD)])[None] * centre - 0.5 * around) * live
        out[:, x] = applied.astype(BF16)
        return centre * live, 0

    lax.fori_loop(0, PLANES, step, (masked(PLANES - 1), 0))


def orbital_apply(support_flat, where, phi, below, above, pot):
    return pl.pallas_call(
        orbital_kernel,
        out_shape=jax.ShapeDtypeStruct(phi.shape, BF16),
        in_specs=[SMEM] * 2 + [VMEM] * 4,
        out_specs=VMEM,
        compiler_params=pltpu.CompilerParams(vmem_limit_bytes=24 << 20),
        name="orbital_apply",
    )(support_flat, where, phi, below, above, pot)


def ring(count, shift):
    return [(i, (i + shift) % count) for i in range(count)]


def local(phi, potential, pair_list, support):
    region = lax.axis_index(REGION)
    core = lax.axis_index("c")
    where = jnp.stack([region, core, region // 16]).astype(jnp.int32)
    pair_flat = pair_list.reshape(-1)
    support_flat = support.reshape(-1)

    own = lax.all_to_all(phi.transpose(1, 2, 0, 3), REGION, split_axis=0, concat_axis=0, tiled=True)

    column = potential
    for step in (1, 2, 4, 8):
        column = jnp.concatenate([column, lax.ppermute(column, "z", ring(ZD, -step))], axis=0)
    pot_all = lax.all_gather(column[None], ("x", "c"), axis=0, tiled=True)
    row_below = lax.ppermute(phi[:, :, 7:], "y", ring(YD, 1))
    row_above = lax.ppermute(phi[:, :, :1], "y", ring(YD, -1))
    hphi = orbital_apply(support_flat, where, phi, row_below, row_above, pot_all)
    own, hphi = lax.optimization_barrier((own, hphi))

    ahead = lax.ppermute(own[:, :4], REGION, ring(PLANES, -1))
    behind = lax.ppermute(own[:, 4:], REGION, ring(PLANES, 1))
    above = lax.ppermute(own[:, 0], "y", ring(YD, -1))
    conf, mine_s, theirs_s = overlap_products(pair_flat, support_flat, where, own)
    swap = [(0, 1), (1, 0)]
    total_s = mine_s + lax.ppermute(theirs_s, "c", swap)
    mine_h, theirs_h = hamiltonian_products(pair_flat, support_flat, where, conf, ahead, behind, above,
                                            potential[0])
    total_h = mine_h + lax.ppermute(theirs_h, "c", swap)
    total = jnp.stack([total_s, total_h], axis=2).reshape(XD * YD, 2, 8, ZD, W)
    shares = lax.all_to_all(total, ("x", "y"), split_axis=0, concat_axis=0, tiled=True)
    partial = jnp.sum(shares, axis=0).transpose(2, 0, 1, 3)
    shares = lax.all_to_all(partial, ("z",), split_axis=0, concat_axis=0, tiled=True)
    result = jnp.sum(shares, axis=0)
    return result[0], result[1], hphi


def solution(mesh):
    fine = Mesh(mesh.devices.reshape(ZD, XD, CD, YD), ("z", "x", "c", "y"))
    in_specs = (P(REGION, None, "y", None), P(REGION, "y", None), P(), P())
    out_specs = (P("y", REGION), P("y", REGION), P(REGION, None, "y", None))
    return jax.shard_map(local, mesh=fine, in_specs=in_specs, out_specs=out_specs, check_vma=False)
```

time: 278 us -> 282 us (1.014)
  blocking collectives: 176 us -> 77.3 us
  waiting for transfers between devices: 12.5 us -> 81 us
  starting transfers between devices: 40.5 us -> 74.8 us
    all_gather x1 -> x0, blocking collectives: 104 us -> none  [local(): column = lax.all_gather(potential, 'z', axis=0, tiled=True)]
    ppermute x2 -> x6, waiting for transfers between devices: 9.45 us -> 81 us  [the longest x4 78.5 us: local(): lax.ppermute(column, 'z', ring(ZD, -step))]
    ppermute x2 -> x6, starting transfers between devices: 3.84 us -> 39.1 us  [the longest x4 31.8 us: local(): lax.ppermute(column, 'z', ring(ZD, -step))]
    all_to_all x1, blocking collectives: 33.5 us -> 38 us  [local(): lax.all_to_all(total, ('x', 'y'), split_axis=0, concat_axis=0, tiled=True)]
    ppermute x1, waiting for transfers between devices: 3 us -> 0.01 us  [local(): above = lax.ppermute(own[:, 0], 'y', ring(YD, -1))]
    pallas_call x1 -> x2, Pallas kernels: 17.2 us -> 15.8 us  [the longest x1 11 us: hamiltonian_products(): pl.pallas_call(hamiltonian_kernel, out_shape=(SHARE, SHARE), in_specs=[SM...]
    unnamed x10 -> x14, local copies, waits for them, and re-layouts: 7.05 us -> 7.05 us
  transfers between devices with their start and end apart: 8 -> 12, of which waited for: 3 -> 5; matrix products, arithmetic and copies ran while one was open for 2% -> 2% of each run, Pallas kernels for 5% -> 10%
where the time goes in v3:
time: 282 us; the launch traced here: 280 us
  waiting for transfers between devices  81 us (29%)
  blocking collectives  77.3 us (27%)
  starting transfers between devices  74.8 us (27%)
  Pallas kernels  29.4 us (10%)
  local copies, waits for them, and re-layouts  14.6 us (5%)
    ppermute x4, waiting for transfers between devices, local(): lax.ppermute(column, 'z', ring(ZD, -step))  78.5 us
    all_to_all x1, blocking collectives, local(): lax.all_to_all(total, ('x', 'y'), split_axis=0, concat_axis=0, tiled=True)  38 us
    ppermute x4, starting transfers between devices, local(): lax.ppermute(column, 'z', ring(ZD, -step))  31.8 us
    all_to_all x1, blocking collectives, local(): lax.all_to_all(partial, ('z',), split_axis=0, concat_axis=0, tiled=True)  26.3 us
    all_to_all x1, starting transfers between devices, local(): lax.all_to_all(phi.transpose(1, 2, 0, 3), REGION, split_axis=0, concat_ax...  19.5 us
    pallas_call x1, Pallas kernels, orbital_apply(): pl.pallas_call(orbital_kernel, out_shape=jax.ShapeDtypeStruct(phi.shape,...  13.6 us
    all_gather x1, blocking collectives, local(): pot_all = lax.all_gather(column[None], ('x', 'c'), axis=0, tiled=True)  13.1 us
    pallas_call x1, Pallas kernels, hamiltonian_products(): pl.pallas_call(hamiltonian_kernel, out_shape=(SHARE, SHARE), in_specs=[SM...  11 us
  transfers between devices with their start and end apart: 12, of which 5 were waited for; matrix products, arithmetic and copies ran while one was open for 2% of the time, Pallas kernels for 10%

profile of v3, /device:TPU:6, one launch (start us, length us, event | category | flops | bytes accessed | tf_op | source)
XLA Modules:
  0.0 280.3 jit_solution(9323983153959142570)
XLA Ops:
  0.6 5.4 %copy.31 = bf16[8,128,8,128]{3,0,2,1:T(8,128)(2,1)} copy(bf16[8,128,8,128]{3,2,1,0:T(8,128)(2,1)} %phi.1) | data formatting | bytes 4194304 | tf_op args[0]
  6.0 19.5 %all-to-all-start = ((bf16[128,8,8,128]{3,2,1,0:T(8,128)(2,1)}), bf16[128,8,8,128]{3,2,1,0:T(8,128)(2,1)S(1)}, u32[]{:S(2)}, u32[]{:S(2)}) async-start(bf16[128,8,8,128]{3,2,1,0:T(8,128)(2,1)} %bitcast.27), calls=%async_computation | async-start | bytes 4194304 | tf_op jit(solution)/shard_map/all_to_all | solution.py:195
  25.5 0.0 copy-done.1
  25.5 0.0 copy-start.2
  25.5 5.3 %collective-permute-start.2 = (f32[1,8,128]{2,1,0:T(8,128)S(1)}, f32[1,8,128]{2,1,0:T(8,128)S(1)}, u32[]{:S(2)}, u32[]{:S(2)}) collective-permute-start(f32[1,8,128]{2,1,0:T(8,128)S(1)} %copy-done.1), channel_id=1, source_target_pairs={{0,480},{32,0},{64,32},{96,64},{128,96},{160,128},{192,160},{224,1... | collective-permute-start | bytes 12296 | tf_op jit(solution)/shard_map/ppermute | solution.py:199
  30.8 4.3 %fusion.1 = (bf16[8,128,1,128]{3,2,1,0:T(2,128)(2,1)}, bf16[8,128,1,128]{3,2,1,0:T(2,128)(2,1)}) fusion(bf16[8,128,8,128]{3,2,1,0:T(8,128)(2,1)} %phi.1), kind=kLoop, calls=%fused_computation.15 | loop fusion | bytes 1048576 | tf_op jit(solution)/shard_map/slice | solution.py:202
  35.1 3.5 %collective-permute-start = (bf16[8,128,1,128]{3,2,1,0:T(2,128)(2,1)}, bf16[8,128,1,128]{3,2,1,0:T(2,128)(2,1)S(1)}, u32[]{:S(2)}, u32[]{:S(2)}) collective-permute-start(bf16[8,128,1,128]{3,2,1,0:T(2,128)(2,1)} %get-tuple-element.20), channel_id=1, source_target_pairs={{0,1},{1,2},{2,3},{3,0},{4,5},{5,6},{6,7},{7,4},{8,9},{9,10},{10,1... | collective-permute-start | bytes 786440 | tf_op jit(solution)/shard_map/ppermute | solution.py:201
  38.6 3.6 %collective-permute-start.1 = (bf16[8,128,1,128]{3,2,1,0:T(2,128)(2,1)}, bf16[8,128,1,128]{3,2,1,0:T(2,128)(2,1)S(1)}, u32[]{:S(2)}, u32[]{:S(2)}) collective-permute-start(bf16[8,128,1,128]{3,2,1,0:T(2,128)(2,1)} %get-tuple-element.19), channel_id=1, source_target_pairs={{0,3},{1,0},{2,1},{3,2},{4,7},{5,4},{6,5},{7,6},{8,11},{9,8},{10,9... | collective-permute-start | bytes 786440 | tf_op jit(solution)/shard_map/ppermute | solution.py:202
  42.2 0.1 pad_add_fusion.where
  42.3 73.2 %collective-permute-done.2 = f32[1,8,128]{2,1,0:T(8,128)S(1)} collective-permute-done((f32[1,8,128]{2,1,0:T(8,128)S(1)}, f32[1,8,128]{2,1,0:T(8,128)S(1)}, u32[]{:S(2)}, u32[]{:S(2)}) %collective-permute-start.2) | collective-permute-done | bytes 4128 | tf_op jit(solution)/shard_map/ppermute | solution.py:199
  115.5 5.7 %collective-permute-start.3 = (f32[2,8,128]{2,1,0:T(8,128)S(1)}, f32[2,8,128]{2,1,0:T(8,128)S(1)}, u32[]{:S(2)}, u32[]{:S(2)}) collective-permute-start(f32[2,8,128]{2,1,0:T(8,128)S(1)} %pad_maximum_fusion.3), channel_id=1, source_target_pairs={{0,448},{32,480},{64,0},{96,32},{128,64},{160,96},{192,128},{224,1... | collective-permute-start | bytes 24584 | tf_op jit(solution)/shard_map/ppermute | solution.py:199
  121.2 1.3 collective-permute-done.3
  122.6 8.1 %collective-permute-start.4 = (f32[4,8,128]{2,1,0:T(8,128)S(1)}, f32[4,8,128]{2,1,0:T(8,128)S(1)}, u32[]{:S(2)}, u32[]{:S(2)}) collective-permute-start(f32[4,8,128]{2,1,0:T(8,128)S(1)} %pad_maximum_fusion.2), channel_id=1, source_target_pairs={{0,384},{32,416},{64,448},{96,480},{128,0},{160,32},{192,64},{224,... | collective-permute-start | bytes 49160 | tf_op jit(solution)/shard_map/ppermute | solution.py:199
  130.7 1.6 collective-permute-done.4
  132.3 12.7 %collective-permute-start.5 = (f32[8,8,128]{2,1,0:T(8,128)S(1)}, f32[8,8,128]{2,1,0:T(8,128)S(1)}, u32[]{:S(2)}, u32[]{:S(2)}) collective-permute-start(f32[8,8,128]{2,1,0:T(8,128)S(1)} %pad_maximum_fusion.1), channel_id=1, source_target_pairs={{0,256},{32,288},{64,320},{96,352},{128,384},{160,416},{192,448},{... | collective-permute-start | bytes 98312 | tf_op jit(solution)/shard_map/ppermute | solution.py:199
  145.0 2.3 collective-permute-done.5
  147.4 13.1 %all-gather = f32[128,8,128]{2,1,0:T(8,128)S(1)} all-gather(f32[16,8,128]{2,1,0:T(8,128)S(1)} %constant_dynamic-update-slice_fusion), channel_id=2, replica_groups=mesh['z'=16,'x'=4,'c'=2,'y'=4] {'x','c'}, dimensions={0}, use_global_device_ids=true | all-gather | bytes 589824 | tf_op jit(solution)/shard_map/all_gather | solution.py:200
  160.5 0.0 collective-permute-done.below
  160.5 0.0 collective-permute-done.1.above
  160.5 0.0 copy-done.2
  160.5 0.0 copy-start
  160.5 1.6 copy-done
  162.1 13.6 %orbital_apply.1 = bf16[8,128,8,128]{3,2,1,0:T(8,128)(2,1)} custom-call(s32[1024]{0:T(1024)S(1)} %bitcast.24, s32[3]{0:T(128)S(1)} %pad_add_fusion.where, bf16[8,128,8,128]{3,2,1,0:T(8,128)(2,1)S(1)} %copy-done, bf16[8,128,1,128]{3,2,1,0:T(2,128)(2,1)S(1)} %collective-permute-done.below, bf16[8,128,1,128]{3,2,1,0:T(2,128)(2,1)S(1)} %collective-permute-done.1.above, ...), custom_call_target="tpu_custom_call" | custom-call | tf_op jit(solution)/shard_map/orbital_apply/pallas_call | solution.py:174
  175.7 0.0 all-to-all-done.own
  175.7 1.7 fusion
  177.4 1.9 collective-permute-start.7
  179.3 2.4 collective-permute-start.8
  181.7 0.8 slice_bitcast_fusion
  182.5 4.9 %collective-permute-start.9 = (bf16[128,8,128]{2,1,0:T(8,128)(2,1)}, bf16[128,8,128]{2,1,0:T(8,128)(2,1)S(1)}, u32[]{:S(2)}, u32[]{:S(2)}) collective-permute-start(bf16[128,8,128]{2,1,0:T(8,128)(2,1)} %slice_bitcast_fusion), channel_id=1, source_target_pairs={{0,3},{1,0},{2,1},{3,2},{4,7},{5,4},{6,5},{7,6},{8,11},{9,8},{10,9... | collective-permute-start | bytes 786440 | tf_op jit(solution)/shard_map/ppermute | solution.py:208
  187.4 0.0 copy-done.3
  187.4 0.1 copy.22
  187.5 0.1 reshape.17.pairs
  187.6 4.8 %overlap_products.1 = (bf16[1024,1024]{1,0:T(8,128)(2,1)S(1)}, f32[4,4,8,16,128]{4,3,2,1,0:T(8,128)S(1)}, f32[4,4,8,16,128]{4,3,2,1,0:T(8,128)S(1)}) custom-call(s32[64]{0:T(128)S(1)} %reshape.17.pairs, s32[1024]{0:T(1024)S(1)} %bitcast.25, s32[3]{0:T(128)S(1)} %pad_add_fusion.where, bf16[128,8,8,128]{3,2,1,0:T(8,128)(2,1)S(1)} %all-to-all-done.own), custom_call_target="tpu_custom_call" | custom-call | tf_op jit(solution)/shard_map/overlap_products/pallas_call | solution.py:123
  192.4 5.3 %collective-permute-start.6 = (f32[4,4,8,16,128]{4,3,2,1,0:T(8,128)S(1)}, f32[4,4,8,16,128]{4,3,2,1,0:T(8,128)S(1)}, u32[]{:S(2)}, u32[]{:S(2)}) collective-permute-start(f32[4,4,8,16,128]{4,3,2,1,0:T(8,128)S(1)} %get-tuple-element.12), channel_id=1, source_target_pairs={{0,4},{4,0},{1,5},{5,1},{2,6},{6,2},{3,7},{7,3},{8,12},{12,8},{9,1... | collective-permute-start | bytes 3145736 | tf_op jit(solution)/shard_map/ppermute | solution.py:211
  197.8 0.0 collective-permute-done.9.above
  197.8 0.0 collective-permute-done.7.ahead
  197.8 0.0 collective-permute-done.8.behind
  197.8 11.0 %hamiltonian_products.1 = (f32[4,4,8,16,128]{4,3,2,1,0:T(8,128)S(1)}, f32[4,4,8,16,128]{4,3,2,1,0:T(8,128)S(1)}) custom-call(s32[64]{0:T(128)S(1)} %reshape.17.pairs, s32[1024]{0:T(1024)S(1)} %bitcast.26, s32[3]{0:T(128)S(1)} %pad_add_fusion.where, bf16[1024,1024]{1,0:T(8,128)(2,1)S(1)} %get-tuple-element.13.conf, ...), custom_call_target="tpu_custom_call" | custom-call | tf_op jit(solution)/shard_map/hamiltonian_products/pallas_call | solution.py:135
  208.8 1.9 collective-permute-start.10
  210.8 0.0 collective-permute-done.6
  210.8 0.1 add.15
  210.9 2.5 collective-permute-done.10
  213.4 0.1 add.16
  213.5 0.1 pad_maximum_fusion
  213.7 38.0 %all_to_all.15 = f32[16,2,8,16,128]{4,3,2,1,0:T(8,128)} all-to-all(f32[16,2,8,16,128]{4,3,2,1,0:T(8,128)S(1)} %pad_maximum_fusion), channel_id=1, replica_groups=mesh['z'=16,'x'=4,'c'=2,'y'=4] {'x','y'}, dimensions={0} | all-to-all | bytes 4194304 | tf_op jit(solution)/shard_map/all_to_all | solution.py:216
  251.6 1.7 reduce_sum.18
  253.4 26.3 %all_to_all.16 = f32[16,2,8,128]{3,2,1,0:T(8,128)S(1)} all-to-all(f32[16,2,8,128]{3,2,1,0:T(8,128)S(1)} %copy.27), channel_id=1, replica_groups=mesh['z'=16,'x'=4,'c'=2,'y'=4] {'z'}, dimensions={0} | all-to-all | bytes 262144 | tf_op jit(solution)/shard_map/all_to_all | solution.py:218
  279.7 0.6 slice_bitcast_fusion.1
  (12 shorter events, 0.1 us)
Async XLA Ops:
  6.0 19.5 %copy-start.1 = (f32[1,8,128]{2,1,0:T(8,128)S(1)}, f32[1,8,128]{2,1,0:T(8,128)}, u32[]{:S(2)}) copy-start(f32[1,8,128]{2,1,0:T(8,128)} %param.5) | copy-start | bytes 12292
  6.0 169.7 %all-to-all-start = ((bf16[128,8,8,128]{3,2,1,0:T(8,128)(2,1)}), bf16[128,8,8,128]{3,2,1,0:T(8,128)(2,1)S(1)}, u32[]{:S(2)}, u32[]{:S(2)}) async-start(bf16[128,8,8,128]{3,2,1,0:T(8,128)(2,1)} %bitcast.27), calls=%async_computation | async-start | bytes 4194304 | tf_op jit(solution)/shard_map/all_to_all | solution.py:195
  25.5 135.0 %copy-start.2 = (s32[8,128]{1,0:T(8,128)S(1)}, s32[8,128]{1,0:T(8,128)}, u32[]{:S(2)}) copy-start(s32[8,128]{1,0:T(8,128)} %param.7) | copy-start | bytes 12292
  25.5 90.0 %collective-permute-start.2 = (f32[1,8,128]{2,1,0:T(8,128)S(1)}, f32[1,8,128]{2,1,0:T(8,128)S(1)}, u32[]{:S(2)}, u32[]{:S(2)}) collective-permute-start(f32[1,8,128]{2,1,0:T(8,128)S(1)} %copy-done.1), channel_id=1, source_target_pairs={{0,480},{32,0},{64,32},{96,64},{128,96},{160,128},{192,160},{224,1... | collective-permute-start | bytes 12296 | tf_op jit(solution)/shard_map/ppermute | solution.py:199
  35.1 125.3 %collective-permute-start = (bf16[8,128,1,128]{3,2,1,0:T(2,128)(2,1)}, bf16[8,128,1,128]{3,2,1,0:T(2,128)(2,1)S(1)}, u32[]{:S(2)}, u32[]{:S(2)}) collective-permute-start(bf16[8,128,1,128]{3,2,1,0:T(2,128)(2,1)} %get-tuple-element.20), channel_id=1, source_target_pairs={{0,1},{1,2},{2,3},{3,0},{4,5},{5,6},{6,7},{7,4},{8,9},{9,10},{10,1... | collective-permute-start | bytes 786440 | tf_op jit(solution)/shard_map/ppermute | solution.py:201
  38.6 121.9 %collective-permute-start.1 = (bf16[8,128,1,128]{3,2,1,0:T(2,128)(2,1)}, bf16[8,128,1,128]{3,2,1,0:T(2,128)(2,1)S(1)}, u32[]{:S(2)}, u32[]{:S(2)}) collective-permute-start(bf16[8,128,1,128]{3,2,1,0:T(2,128)(2,1)} %get-tuple-element.19), channel_id=1, source_target_pairs={{0,3},{1,0},{2,1},{3,2},{4,7},{5,4},{6,5},{7,6},{8,11},{9,8},{10,9... | collective-permute-start | bytes 786440 | tf_op jit(solution)/shard_map/ppermute | solution.py:202
  115.5 7.1 %collective-permute-start.3 = (f32[2,8,128]{2,1,0:T(8,128)S(1)}, f32[2,8,128]{2,1,0:T(8,128)S(1)}, u32[]{:S(2)}, u32[]{:S(2)}) collective-permute-start(f32[2,8,128]{2,1,0:T(8,128)S(1)} %pad_maximum_fusion.3), channel_id=1, source_target_pairs={{0,448},{32,480},{64,0},{96,32},{128,64},{160,96},{192,128},{224,1... | collective-permute-start | bytes 24584 | tf_op jit(solution)/shard_map/ppermute | solution.py:199
  122.6 9.7 %collective-permute-start.4 = (f32[4,8,128]{2,1,0:T(8,128)S(1)}, f32[4,8,128]{2,1,0:T(8,128)S(1)}, u32[]{:S(2)}, u32[]{:S(2)}) collective-permute-start(f32[4,8,128]{2,1,0:T(8,128)S(1)} %pad_maximum_fusion.2), channel_id=1, source_target_pairs={{0,384},{32,416},{64,448},{96,480},{128,0},{160,32},{192,64},{224,... | collective-permute-start | bytes 49160 | tf_op jit(solution)/shard_map/ppermute | solution.py:199
  132.3 15.1 %collective-permute-start.5 = (f32[8,8,128]{2,1,0:T(8,128)S(1)}, f32[8,8,128]{2,1,0:T(8,128)S(1)}, u32[]{:S(2)}, u32[]{:S(2)}) collective-permute-start(f32[8,8,128]{2,1,0:T(8,128)S(1)} %pad_maximum_fusion.1), channel_id=1, source_target_pairs={{0,256},{32,288},{64,320},{96,352},{128,384},{160,416},{192,448},{... | collective-permute-start | bytes 98312 | tf_op jit(solution)/shard_map/ppermute | solution.py:199
  160.5 1.6 copy-start
  175.7 11.7 %copy-start.3 = (s32[32,2]{0,1:T(2,128)S(1)}, s32[32,2]{0,1:T(2,128)}, u32[]{:S(2)}) copy-start(s32[32,2]{0,1:T(2,128)} %param.6) | copy-start | bytes 772
  177.4 20.4 %collective-permute-start.7 = (bf16[128,4,8,128]{3,2,1,0:T(8,128)(2,1)}, bf16[128,4,8,128]{3,2,1,0:T(8,128)(2,1)S(1)}, u32[]{:S(2)}, u32[]{:S(2)}) collective-permute-start(bf16[128,4,8,128]{3,2,1,0:T(8,128)(2,1)} %get-tuple-element.18), channel_id=1, source_target_pairs={{0,508},{4,0},{8,4},{12,8},{16,12},{20,16},{24,20},{28,24},{32,28}... | collective-permute-start | bytes 3145736 | tf_op jit(solution)/shard_map/ppermute | solution.py:206
  179.3 18.5 %collective-permute-start.8 = (bf16[128,4,8,128]{3,2,1,0:T(8,128)(2,1)}, bf16[128,4,8,128]{3,2,1,0:T(8,128)(2,1)}, u32[]{:S(2)}, u32[]{:S(2)}) collective-permute-start(bf16[128,4,8,128]{3,2,1,0:T(8,128)(2,1)} %get-tuple-element.17), channel_id=1, source_target_pairs={{0,4},{4,8},{8,12},{12,16},{16,20},{20,24},{24,28},{28,32},{32,36}... | collective-permute-start | bytes 3145736 | tf_op jit(solution)/shard_map/ppermute | solution.py:207
  182.5 15.3 %collective-permute-start.9 = (bf16[128,8,128]{2,1,0:T(8,128)(2,1)}, bf16[128,8,128]{2,1,0:T(8,128)(2,1)S(1)}, u32[]{:S(2)}, u32[]{:S(2)}) collective-permute-start(bf16[128,8,128]{2,1,0:T(8,128)(2,1)} %slice_bitcast_fusion), channel_id=1, source_target_pairs={{0,3},{1,0},{2,1},{3,2},{4,7},{5,4},{6,5},{7,6},{8,11},{9,8},{10,9... | collective-permute-start | bytes 786440 | tf_op jit(solution)/shard_map/ppermute | solution.py:208
  192.4 18.3 %collective-permute-start.6 = (f32[4,4,8,16,128]{4,3,2,1,0:T(8,128)S(1)}, f32[4,4,8,16,128]{4,3,2,1,0:T(8,128)S(1)}, u32[]{:S(2)}, u32[]{:S(2)}) collective-permute-start(f32[4,4,8,16,128]{4,3,2,1,0:T(8,128)S(1)} %get-tuple-element.12), channel_id=1, source_target_pairs={{0,4},{4,0},{1,5},{5,1},{2,6},{6,2},{3,7},{7,3},{8,12},{12,8},{9,1... | collective-permute-start | bytes 3145736 | tf_op jit(solution)/shard_map/ppermute | solution.py:211
  208.8 4.6 %collective-permute-start.10 = (f32[4,4,8,16,128]{4,3,2,1,0:T(8,128)S(1)}, f32[4,4,8,16,128]{4,3,2,1,0:T(8,128)S(1)}, u32[]{:S(2)}, u32[]{:S(2)}) collective-permute-start(f32[4,4,8,16,128]{4,3,2,1,0:T(8,128)S(1)} %get-tuple-element.15), channel_id=1, source_target_pairs={{0,4},{4,0},{1,5},{5,1},{2,6},{6,2},{3,7},{7,3},{8,12},{12,8},{9,1... | collective-permute-start | bytes 3145736 | tf_op jit(solution)/shard_map/ppermute | solution.py:214

commit v4 on v3

--- a/solution.py
+++ b/solution.py
@@ -126,7 +126,7 @@
         in_specs=[SMEM] * 3 + [VMEM],
         out_specs=(VMEM,) * 3,
         scratch_shapes=[pltpu.VMEM((NB, NB * W, W), F32)],
-        compiler_params=pltpu.CompilerParams(vmem_limit_bytes=20 << 20),
+        compiler_params=pltpu.CompilerParams(vmem_limit_bytes=16 << 20),
         name="overlap_products",
     )(pair_flat, support_flat, where, own)
 
@@ -142,13 +142,13 @@
             pltpu.VMEM((NB * W, 2 * CELLS + DEPTH), BF16),
             pltpu.VMEM((NB, NB * W, W), F32),
         ],
-        compiler_params=pltpu.CompilerParams(vmem_limit_bytes=32 << 20),
+        compiler_params=pltpu.CompilerParams(vmem_limit_bytes=26 << 20),
         name="hamiltonian_products",
     )(pair_flat, support_flat, where, conf, ahead, behind, above, pot)
 
 
-def orbital_kernel(support, where, phi, below, above, pot, out):
-    block, row_z = where[2], where[0] // 8
+def kinetic_kernel(support, where, phi, below, above, out):
+    block = where[2]
     lane = lax.broadcasted_iota(jnp.int32, (8, ROWS, DEPTH), 2)
     row = lax.broadcasted_iota(jnp.int32, (8, ROWS, DEPTH), 1)
 
@@ -156,29 +156,47 @@
         return phi[:, x].astype(F32) * flag(support, block, x)
 
     def step(x, carry):
-        before, _ = carry
-        centre = phi[:, x].astype(F32)
+        before, centre = carry
         after = masked(lax.rem(x + 1, PLANES))
         low = jnp.where(row == 0, below[:, x].astype(F32), pltpu.roll(centre, 1, 1))
         high = jnp.where(row == ROWS - 1, above[:, x].astype(F32), pltpu.roll(centre, ROWS - 1, 1))
         around = lane_neighbours(centre, lane) + low + high + before + after
         live = flag(support, block, x)
-        applied = ((3.0 + pot[lax.rem(x, 8), lax.rem(x // 8 + ZD - row_z, ZD)])[None] * centre - 0.5 * around) * live
-        out[:, x] = applied.astype(BF16)
-        return centre * live, 0
-
-    lax.fori_loop(0, PLANES, step, (masked(PLANES - 1), 0))
-
-
-def orbital_apply(support_flat, where, phi, below, above, pot):
-    return pl.pallas_call(
-        orbital_kernel,
+        out[x] = (3.0 * centre - 0.5 * around) * live
+        return centre, after
+
+    lax.fori_loop(0, PLANES, step, (masked(PLANES - 1), masked(0)))
+
+
+def potential_kernel(support, where, kinetic, phi, pot, out):
+    block = where[2]
+
+    @pl.loop(0, PLANES)
+    def _(x):
+        values = pot[x // 8, 0, lax.rem(x, 8)] * flag(support, block, x)
+        out[:, x] = (kinetic[x] + values[None] * phi[:, x].astype(F32)).astype(BF16)
+
+
+def kinetic_part(support_flat, where, phi, below, above):
+    return pl.pallas_call(
+        kinetic_kernel,
+        out_shape=jax.ShapeDtypeStruct((PLANES, 8, ROWS, DEPTH), F32),
+        in_specs=[SMEM] * 2 + [VMEM] * 3,
+        out_specs=VMEM,
+        compiler_params=pltpu.CompilerParams(vmem_limit_bytes=10 << 20),
+        name="kinetic_part",
+    )(support_flat, where, phi, below, above)
+
+
+def potential_part(support_flat, where, kinetic, phi, pot):
+    return pl.pallas_call(
+        potential_kernel,
         out_shape=jax.ShapeDtypeStruct(phi.shape, BF16),
-        in_specs=[SMEM] * 2 + [VMEM] * 4,
+        in_specs=[SMEM] * 2 + [VMEM] * 3,
         out_specs=VMEM,
-        compiler_params=pltpu.CompilerParams(vmem_limit_bytes=24 << 20),
-        name="orbital_apply",
-    )(support_flat, where, phi, below, above, pot)
+        compiler_params=pltpu.CompilerParams(vmem_limit_bytes=14 << 20),
+        name="potential_part",
+    )(support_flat, where, kinetic, phi, pot)
 
 
 def ring(count, shift):
@@ -194,14 +212,12 @@
 
     own = lax.all_to_all(phi.transpose(1, 2, 0, 3), REGION, split_axis=0, concat_axis=0, tiled=True)
 
-    column = potential
-    for step in (1, 2, 4, 8):
-        column = jnp.concatenate([column, lax.ppermute(column, "z", ring(ZD, -step))], axis=0)
-    pot_all = lax.all_gather(column[None], ("x", "c"), axis=0, tiled=True)
+    plane_row = lax.all_gather(potential, ("x", "c"), axis=0, tiled=True)
     row_below = lax.ppermute(phi[:, :, 7:], "y", ring(YD, 1))
     row_above = lax.ppermute(phi[:, :, :1], "y", ring(YD, -1))
-    hphi = orbital_apply(support_flat, where, phi, row_below, row_above, pot_all)
-    own, hphi = lax.optimization_barrier((own, hphi))
+    kinetic = kinetic_part(support_flat, where, phi, row_below, row_above)
+    own, plane_row, kinetic = lax.optimization_barrier((own, plane_row, kinetic))
+    pot_all = lax.all_gather(jnp.stack([plane_row, plane_row])[None], "z", axis=0, tiled=True)
 
     ahead = lax.ppermute(own[:, :4], REGION, ring(PLANES, -1))
     behind = lax.ppermute(own[:, 4:], REGION, ring(PLANES, 1))
@@ -212,9 +228,10 @@
     mine_h, theirs_h = hamiltonian_products(pair_flat, support_flat, where, conf, ahead, behind, above,
                                             potential[0])
     total_h = mine_h + lax.ppermute(theirs_h, "c", swap)
-    total = jnp.stack([total_s, total_h], axis=2).reshape(XD * YD, 2, 8, ZD, W)
+    total = jnp.stack([total_s, total_h], axis=2).reshape(XD * YD, 2, 8, ZD, W).astype(BF16)
     shares = lax.all_to_all(total, ("x", "y"), split_axis=0, concat_axis=0, tiled=True)
-    partial = jnp.sum(shares, axis=0).transpose(2, 0, 1, 3)
+    partial = jnp.sum(shares.astype(F32), axis=0).transpose(2, 0, 1, 3)
+    hphi = potential_part(support_flat, where, kinetic, phi, pot_all)
     shares = lax.all_to_all(partial, ("z",), split_axis=0, concat_axis=0, tiled=True)
     result = jnp.sum(shares, axis=0)
     return result[0], result[1], hphi

time: 282 us -> 263 us (0.933)
  blocking collectives: 77.3 us -> 37.8 us
  starting transfers between devices: 74.8 us -> 48.7 us
  waiting for transfers between devices: 81 us -> 101 us
  between operations: 0.91 us -> 14.2 us
  Pallas kernels: 29.4 us -> 35.5 us
  local copies, waits for them, and re-layouts: 14.6 us -> 20.4 us
    ppermute x4 -> x0, waiting for transfers between devices: 78.5 us -> none  [local(): lax.ppermute(column, 'z', ring(ZD, -step))]
    all_to_all x1, waiting for transfers between devices: 0.01 us -> 58.1 us  [local(): lax.all_to_all(phi.transpose(1, 2, 0, 3), REGION, split_axis=0, concat_ax...]
    all_gather x0 -> x1, waiting for transfers between devices: none -> 34.8 us  [local(): lax.all_gather(jnp.stack([plane_row, plane_row])[None], 'z', axis=0, tile...]
    ppermute x4 -> x0, starting transfers between devices: 31.8 us -> none  [local(): lax.ppermute(column, 'z', ring(ZD, -step))]
    all_to_all x1 -> x0, blocking collectives: 26.3 us -> none  [local(): lax.all_to_all(partial, ('z',), split_axis=0, concat_axis=0, tiled=True)]
    all_to_all x1, blocking collectives: 38 us -> 25.1 us  [local(): lax.all_to_all(total, ('x', 'y'), split_axis=0, concat_axis=0, tiled=True)]
    all_to_all x0 -> x1, starting transfers between devices: none -> 6.34 us  [local(): lax.all_to_all(partial, ('z',), split_axis=0, concat_axis=0, tiled=True)]
    unnamed x14 -> x22, local copies, waits for them, and re-layouts: 7.05 us -> 12.8 us
  transfers between devices with their start and end apart: 12 -> 10, of which waited for: 5 -> 5; matrix products, arithmetic and copies ran while one was open for 2% -> 3% of each run, Pallas kernels for 10% -> 14%
where the time goes in v4:
time: 263 us; the launch traced here: 262 us
  waiting for transfers between devices  101 us (38%)
  starting transfers between devices  48.7 us (19%)
  blocking collectives  37.8 us (14%)
  Pallas kernels  35.5 us (13%)
  local copies, waits for them, and re-layouts  20.4 us (8%)
  between operations  14.2 us (5%)
  other arithmetic  4.03 us (2%)
    all_to_all x1, waiting for transfers between devices, local(): lax.all_to_all(phi.transpose(1, 2, 0, 3), REGION, split_axis=0, concat_ax...  58.1 us
    all_gather x1, waiting for transfers between devices, local(): lax.all_gather(jnp.stack([plane_row, plane_row])[None], 'z', axis=0, tile...  34.8 us
    all_to_all x1, blocking collectives, local(): lax.all_to_all(total, ('x', 'y'), split_axis=0, concat_axis=0, tiled=True)  25.1 us
    all_to_all x1, starting transfers between devices, local(): lax.all_to_all(phi.transpose(1, 2, 0, 3), REGION, split_axis=0, concat_ax...  20 us
    unnamed x22, local copies, waits for them, and re-layouts  12.8 us
    all_gather x1, blocking collectives, local(): plane_row = lax.all_gather(potential, ('x', 'c'), axis=0, tiled=True)  12.8 us
    pallas_call x1, Pallas kernels, kinetic_part(): pl.pallas_call(kinetic_kernel, out_shape=jax.ShapeDtypeStruct((PLANES, 8,...  12.5 us
    pallas_call x1, Pallas kernels, hamiltonian_products(): pl.pallas_call(hamiltonian_kernel, out_shape=(SHARE, SHARE), in_specs=[SM...  12.1 us
  transfers between devices with their start and end apart: 10, of which 5 were waited for; matrix products, arithmetic and copies ran while one was open for 3% of the time, Pallas kernels for 14%

profile of v4, /device:TPU:6, one launch (start us, length us, event | category | flops | bytes accessed | tf_op | source)
XLA Modules:
  0.0 262.1 jit_solution(4773963758640828512)
XLA Ops:
  7.2 5.3 %copy.31 = bf16[8,128,8,128]{3,0,2,1:T(8,128)(2,1)} copy(bf16[8,128,8,128]{3,2,1,0:T(8,128)(2,1)} %phi.3) | data formatting | bytes 4194304 | tf_op args[0]
  12.5 20.0 %all-to-all-start = ((bf16[128,8,8,128]{3,2,1,0:T(8,128)(2,1)}), bf16[128,8,8,128]{3,2,1,0:T(8,128)(2,1)}, u32[]{:S(2)}, u32[]{:S(2)}) async-start(bf16[128,8,8,128]{3,2,1,0:T(8,128)(2,1)} %bitcast.29), calls=%async_computation | async-start | bytes 4194304 | tf_op jit(solution)/shard_map/all_to_all | solution.py:213
  32.5 0.0 copy-start.8
  32.5 0.0 copy-start.7
  32.5 0.0 all-gather.3.cloned.1.call-start
  32.6 1.9 fusion.1
  34.5 4.9 %collective-permute-start.1 = (bf16[8,128,1,128]{3,2,1,0:T(2,128)(2,1)}, bf16[8,128,1,128]{3,2,1,0:T(2,128)(2,1)S(1)}, u32[]{:S(2)}, u32[]{:S(2)}) collective-permute-start(bf16[8,128,1,128]{3,2,1,0:T(2,128)(2,1)} %get-tuple-element.21), channel_id=1, source_target_pairs={{0,3},{1,0},{2,1},{3,2},{4,7},{5,4},{6,5},{7,6},{8,11},{9,8},{10,9... | collective-permute-start | bytes 786440 | tf_op jit(solution)/shard_map/ppermute | solution.py:217
  39.4 1.9 collective-permute-start
  41.4 12.8 %all_gather.6 = f32[8,8,128]{2,1,0:T(8,128)S(1)} all-gather(f32[1,8,128]{2,1,0:T(8,128)S(1)} %copy-done.8), channel_id=1, replica_groups=mesh['z'=16,'x'=4,'c'=2,'y'=4] {'x','c'}, dimensions={0}, use_global_device_ids=true | all-gather | bytes 36864 | tf_op jit(solution)/shard_map/all_gather | solution.py:215
  54.2 0.1 pad_add_fusion.where
  54.3 0.0 collective-permute-done.1.above
  54.3 2.2 collective-permute-done.below
  56.4 12.5 %kinetic_part.1.kinetic = f32[128,8,8,128]{3,2,1,0:T(8,128)S(1)} custom-call(s32[1024]{0:T(1024)S(1)} %bitcast.24, s32[3]{0:T(128)S(1)} %pad_add_fusion.where, bf16[8,128,8,128]{3,2,1,0:T(8,128)(2,1)S(1)} %copy-done, bf16[8,128,1,128]{3,2,1,0:T(2,128)(2,1)S(1)} %collective-permute-done.below, bf16[8,128,1,128]{3,2,1,0:T(2,128)(2,1)S(1)} %collective-permute-done.1.above), custom_call_target="tpu_custom_call" | custom-call | tf_op jit(solution)/shard_map/kinetic_part/pallas_call | solution.py:181
  69.0 1.9 copy-done.1
  70.9 58.1 %all-to-all-done.own = bf16[128,8,8,128]{3,2,1,0:T(8,128)(2,1)} async-done(((bf16[128,8,8,128]{3,2,1,0:T(8,128)(2,1)}), bf16[128,8,8,128]{3,2,1,0:T(8,128)(2,1)}, u32[]{:S(2)}, u32[]{:S(2)}) %all-to-all-start) | async-done | bytes 2097184 | tf_op jit(solution)/shard_map/all_to_all | solution.py:213
  129.1 3.2 %fusion = (bf16[128,4,8,128]{3,2,1,0:T(8,128)(2,1)}, bf16[128,4,8,128]{3,2,1,0:T(8,128)(2,1)}) fusion(bf16[128,8,8,128]{3,2,1,0:T(8,128)(2,1)} %all-to-all-done.own), kind=kLoop, calls=%fused_computation.10 | loop fusion | bytes 4194304 | tf_op jit(solution)/shard_map/slice | solution.py:223
  132.3 2.8 %collective-permute-start.4 = (bf16[128,4,8,128]{3,2,1,0:T(8,128)(2,1)}, bf16[128,4,8,128]{3,2,1,0:T(8,128)(2,1)S(1)}, u32[]{:S(2)}, u32[]{:S(2)}) collective-permute-start(bf16[128,4,8,128]{3,2,1,0:T(8,128)(2,1)} %get-tuple-element.19), channel_id=1, source_target_pairs={{0,4},{4,8},{8,12},{12,16},{16,20},{20,24},{24,28},{28,32},{32,36}... | collective-permute-start | bytes 3145736 | tf_op jit(solution)/shard_map/ppermute | solution.py:223
  135.1 2.8 %collective-permute-start.3 = (bf16[128,4,8,128]{3,2,1,0:T(8,128)(2,1)}, bf16[128,4,8,128]{3,2,1,0:T(8,128)(2,1)}, u32[]{:S(2)}, u32[]{:S(2)}) collective-permute-start(bf16[128,4,8,128]{3,2,1,0:T(8,128)(2,1)} %get-tuple-element.20), channel_id=1, source_target_pairs={{0,508},{4,0},{8,4},{12,8},{16,12},{20,16},{24,20},{28,24},{32,28}... | collective-permute-start | bytes 3145736 | tf_op jit(solution)/shard_map/ppermute | solution.py:222
  137.9 0.1 copy.22
  138.0 0.1 reshape.19.pairs
  138.1 6.8 %overlap_products.1 = (bf16[1024,1024]{1,0:T(8,128)(2,1)S(1)}, f32[4,4,8,16,128]{4,3,2,1,0:T(8,128)S(1)}, f32[4,4,8,16,128]{4,3,2,1,0:T(8,128)}) custom-call(s32[64]{0:T(128)S(1)} %reshape.19.pairs, s32[1024]{0:T(1024)S(1)} %bitcast.25, s32[3]{0:T(128)S(1)} %pad_add_fusion.where, bf16[128,8,8,128]{3,2,1,0:T(8,128)(2,1)} %all-to-all-done.own), custom_call_target="tpu_custom_call" | custom-call | tf_op jit(solution)/shard_map/overlap_products/pallas_call | solution.py:123
  144.9 1.0 copy-done.4
  145.8 3.0 %collective-permute-start.2 = (f32[4,4,8,16,128]{4,3,2,1,0:T(8,128)}, f32[4,4,8,16,128]{4,3,2,1,0:T(8,128)}, u32[]{:S(2)}, u32[]{:S(2)}) collective-permute-start(f32[4,4,8,16,128]{4,3,2,1,0:T(8,128)} %get-tuple-element.13), channel_id=1, source_target_pairs={{0,4},{4,0},{1,5},{5,1},{2,6},{6,2},{3,7},{7,3},{8,12},{12,8},{9,1... | collective-permute-start | bytes 3145736 | tf_op jit(solution)/shard_map/ppermute | solution.py:227
  148.9 1.0 slice_bitcast_fusion
  149.8 4.9 %collective-permute-start.5 = (bf16[128,8,128]{2,1,0:T(8,128)(2,1)S(1)}, bf16[128,8,128]{2,1,0:T(8,128)(2,1)S(1)}, u32[]{:S(2)}, u32[]{:S(2)}) collective-permute-start(bf16[128,8,128]{2,1,0:T(8,128)(2,1)S(1)} %slice_bitcast_fusion), channel_id=1, source_target_pairs={{0,3},{1,0},{2,1},{3,2},{4,7},{5,4},{6,5},{7,6},{8,11},{9,8},{10,9... | collective-permute-start | bytes 786440 | tf_op jit(solution)/shard_map/ppermute | solution.py:224
  154.8 5.7 %collective-permute-done.5.above = bf16[128,8,128]{2,1,0:T(8,128)(2,1)S(1)} collective-permute-done((bf16[128,8,128]{2,1,0:T(8,128)(2,1)S(1)}, bf16[128,8,128]{2,1,0:T(8,128)(2,1)S(1)}, u32[]{:S(2)}, u32[]{:S(2)}) %collective-permute-start.5) | collective-permute-done | bytes 262176 | tf_op jit(solution)/shard_map/ppermute | solution.py:224
  160.5 0.0 collective-permute-done.4.behind
  160.5 0.0 collective-permute-done.3.ahead
  160.5 12.1 %hamiltonian_products.1 = (f32[4,4,8,16,128]{4,3,2,1,0:T(8,128)S(1)}, f32[4,4,8,16,128]{4,3,2,1,0:T(8,128)}) custom-call(s32[64]{0:T(128)S(1)} %reshape.19.pairs, s32[1024]{0:T(1024)S(1)} %bitcast.26, s32[3]{0:T(128)S(1)} %pad_add_fusion.where, bf16[1024,1024]{1,0:T(8,128)(2,1)S(1)} %get-tuple-element.14.conf, ...), custom_call_target="tpu_custom_call" | custom-call | tf_op jit(solution)/shard_map/hamiltonian_products/pallas_call | solution.py:135
  172.6 1.1 copy-done.5
  173.6 2.0 collective-permute-start.6
  175.7 0.6 pad_maximum_fusion.1
  176.3 0.0 all-gather.3.cloned.1.call-update
  176.3 0.0 collective-permute-done.2
  176.3 1.7 add_convert_fusion.1
  178.0 0.6 collective-permute-done.6
  178.7 1.4 add_convert_fusion
  180.0 0.1 pad_maximum_fusion
  180.1 25.1 %all_to_all.15 = bf16[16,2,8,16,128]{4,3,2,1,0:T(8,128)(2,1)S(1)} all-to-all(bf16[16,2,8,16,128]{4,3,2,1,0:T(8,128)(2,1)S(1)} %pad_maximum_fusion), channel_id=1, replica_groups=mesh['z'=16,'x'=4,'c'=2,'y'=4] {'x','y'}, dimensions={0} | all-to-all | bytes 2097152 | tf_op jit(solution)/shard_map/all_to_all | solution.py:232
  205.2 0.1 convert_reduce_fusion
  205.3 0.7 copy.27
  206.0 6.3 %all-to-all-start.2 = ((f32[16,2,8,128]{3,2,1,0:T(8,128)}), f32[16,2,8,128]{3,2,1,0:T(8,128)S(1)}, u32[]{:S(2)}, u32[]{:S(2)}) async-start(f32[16,2,8,128]{3,2,1,0:T(8,128)} %copy.27), calls=%async_computation.2 | async-start | bytes 262144 | tf_op jit(solution)/shard_map/all_to_all | solution.py:235
  212.4 34.8 %all-gather.3.cloned.1.call-done = f32[32,8,8,128]{3,2,1,0:T(8,128)} async-done(((f32[2,8,8,128]{3,2,1,0:T(8,128)}), f32[32,8,8,128]{3,2,1,0:T(8,128)}) %all-gather.3.cloned.1.call-update) | async-done | bytes 1048592 | tf_op jit(solution)/shard_map/all_gather | solution.py:220
  247.2 2.2 copy-done.2
  249.4 1.2 copy-done.3
  250.6 4.1 %potential_part.1 = bf16[8,128,8,128]{3,2,1,0:T(8,128)(2,1)} custom-call(s32[1024]{0:T(1024)S(1)} %bitcast.27, s32[3]{0:T(128)S(1)} %pad_add_fusion.where, f32[128,8,8,128]{3,2,1,0:T(8,128)S(1)} %copy-done.2, bf16[8,128,8,128]{3,2,1,0:T(8,128)(2,1)S(1)} %copy-done, f32[16,2,8,8,128]{4,3,2,1,0:T(8,128)S(1)} %bitcast.23), custom_call_target="tpu_custom_call" | custom-call | tf_op jit(solution)/shard_map/potential_part/pallas_call | solution.py:192
  254.7 0.0 all-to-all-done.2
  254.7 0.6 slice_bitcast_fusion.1
  (14 shorter events, 0.0 us)
Async XLA Ops:
  12.5 20.0 %copy-start = (bf16[8,128,8,128]{3,2,1,0:T(8,128)(2,1)S(1)}, bf16[8,128,8,128]{3,2,1,0:T(8,128)(2,1)}, u32[]{:S(2)}) copy-start(bf16[8,128,8,128]{3,2,1,0:T(8,128)(2,1)} %phi.3) | copy-start | bytes 6291460
  12.5 116.6 %all-to-all-start = ((bf16[128,8,8,128]{3,2,1,0:T(8,128)(2,1)}), bf16[128,8,8,128]{3,2,1,0:T(8,128)(2,1)}, u32[]{:S(2)}, u32[]{:S(2)}) async-start(bf16[128,8,8,128]{3,2,1,0:T(8,128)(2,1)} %bitcast.29), calls=%async_computation | async-start | bytes 4194304 | tf_op jit(solution)/shard_map/all_to_all | solution.py:213
  32.5 8.9 %copy-start.8 = (f32[1,8,128]{2,1,0:T(8,128)S(1)}, f32[1,8,128]{2,1,0:T(8,128)}, u32[]{:S(2)}) copy-start(f32[1,8,128]{2,1,0:T(8,128)} %param.5) | copy-start | bytes 12292
  32.5 23.9 %copy-start.7 = (s32[8,128]{1,0:T(8,128)S(1)}, s32[8,128]{1,0:T(8,128)}, u32[]{:S(2)}) copy-start(s32[8,128]{1,0:T(8,128)} %param.7) | copy-start | bytes 12292
  32.5 214.7 %all-gather.3.cloned.1.call-start = ((), (), s32[]{:S(2)}) async-start(), calls=%async_computation.3 | async-start | bytes 1114112 | tf_op jit(solution)/shard_map/all_gather | solution.py:220
  34.5 19.8 %collective-permute-start.1 = (bf16[8,128,1,128]{3,2,1,0:T(2,128)(2,1)}, bf16[8,128,1,128]{3,2,1,0:T(2,128)(2,1)S(1)}, u32[]{:S(2)}, u32[]{:S(2)}) collective-permute-start(bf16[8,128,1,128]{3,2,1,0:T(2,128)(2,1)} %get-tuple-element.21), channel_id=1, source_target_pairs={{0,3},{1,0},{2,1},{3,2},{4,7},{5,4},{6,5},{7,6},{8,11},{9,8},{10,9... | collective-permute-start | bytes 786440 | tf_op jit(solution)/shard_map/ppermute | solution.py:217
  39.4 17.0 %collective-permute-start = (bf16[8,128,1,128]{3,2,1,0:T(2,128)(2,1)}, bf16[8,128,1,128]{3,2,1,0:T(2,128)(2,1)S(1)}, u32[]{:S(2)}, u32[]{:S(2)}) collective-permute-start(bf16[8,128,1,128]{3,2,1,0:T(2,128)(2,1)} %get-tuple-element.22), channel_id=1, source_target_pairs={{0,1},{1,2},{2,3},{3,0},{4,5},{5,6},{6,7},{7,4},{8,9},{9,10},{10,1... | collective-permute-start | bytes 786440 | tf_op jit(solution)/shard_map/ppermute | solution.py:216
  69.0 1.9 copy-start.1
  70.9 67.0 %copy-start.9 = (s32[32,2]{0,1:T(2,128)S(1)}, s32[32,2]{0,1:T(2,128)}, u32[]{:S(2)}) copy-start(s32[32,2]{0,1:T(2,128)} %param.6) | copy-start | bytes 772
  132.3 28.2 %collective-permute-start.4 = (bf16[128,4,8,128]{3,2,1,0:T(8,128)(2,1)}, bf16[128,4,8,128]{3,2,1,0:T(8,128)(2,1)S(1)}, u32[]{:S(2)}, u32[]{:S(2)}) collective-permute-start(bf16[128,4,8,128]{3,2,1,0:T(8,128)(2,1)} %get-tuple-element.19), channel_id=1, source_target_pairs={{0,4},{4,8},{8,12},{12,16},{16,20},{20,24},{24,28},{28,32},{32,36}... | collective-permute-start | bytes 3145736 | tf_op jit(solution)/shard_map/ppermute | solution.py:223
  135.1 25.4 %collective-permute-start.3 = (bf16[128,4,8,128]{3,2,1,0:T(8,128)(2,1)}, bf16[128,4,8,128]{3,2,1,0:T(8,128)(2,1)}, u32[]{:S(2)}, u32[]{:S(2)}) collective-permute-start(bf16[128,4,8,128]{3,2,1,0:T(8,128)(2,1)} %get-tuple-element.20), channel_id=1, source_target_pairs={{0,508},{4,0},{8,4},{12,8},{16,12},{20,16},{24,20},{28,24},{32,28}... | collective-permute-start | bytes 3145736 | tf_op jit(solution)/shard_map/ppermute | solution.py:222
  144.9 1.0 copy-start.4
  145.8 30.5 %collective-permute-start.2 = (f32[4,4,8,16,128]{4,3,2,1,0:T(8,128)}, f32[4,4,8,16,128]{4,3,2,1,0:T(8,128)}, u32[]{:S(2)}, u32[]{:S(2)}) collective-permute-start(f32[4,4,8,16,128]{4,3,2,1,0:T(8,128)} %get-tuple-element.13), channel_id=1, source_target_pairs={{0,4},{4,0},{1,5},{5,1},{2,6},{6,2},{3,7},{7,3},{8,12},{12,8},{9,1... | collective-permute-start | bytes 3145736 | tf_op jit(solution)/shard_map/ppermute | solution.py:227
  149.8 10.7 %collective-permute-start.5 = (bf16[128,8,128]{2,1,0:T(8,128)(2,1)S(1)}, bf16[128,8,128]{2,1,0:T(8,128)(2,1)S(1)}, u32[]{:S(2)}, u32[]{:S(2)}) collective-permute-start(bf16[128,8,128]{2,1,0:T(8,128)(2,1)S(1)} %slice_bitcast_fusion), channel_id=1, source_target_pairs={{0,3},{1,0},{2,1},{3,2},{4,7},{5,4},{6,5},{7,6},{8,11},{9,8},{10,9... | collective-permute-start | bytes 786440 | tf_op jit(solution)/shard_map/ppermute | solution.py:224
  172.6 1.1 copy-start.5
  173.6 5.0 %copy-start.6 = (f32[4,4,8,16,128]{4,3,2,1,0:T(8,128)S(1)}, f32[4,4,8,16,128]{4,3,2,1,0:T(8,128)}, u32[]{:S(2)}) copy-start(f32[4,4,8,16,128]{4,3,2,1,0:T(8,128)} %copy-done.5) | copy-start | bytes 3145732
  173.6 5.0 %collective-permute-start.6 = (f32[4,4,8,16,128]{4,3,2,1,0:T(8,128)}, f32[4,4,8,16,128]{4,3,2,1,0:T(8,128)}, u32[]{:S(2)}, u32[]{:S(2)}) collective-permute-start(f32[4,4,8,16,128]{4,3,2,1,0:T(8,128)} %get-tuple-element.16), channel_id=1, source_target_pairs={{0,4},{4,0},{1,5},{5,1},{2,6},{6,2},{3,7},{7,3},{8,12},{12,8},{9,1... | collective-permute-start | bytes 3145736 | tf_op jit(solution)/shard_map/ppermute | solution.py:230
  206.0 48.6 %all-to-all-start.2 = ((f32[16,2,8,128]{3,2,1,0:T(8,128)}), f32[16,2,8,128]{3,2,1,0:T(8,128)S(1)}, u32[]{:S(2)}, u32[]{:S(2)}) async-start(f32[16,2,8,128]{3,2,1,0:T(8,128)} %copy.27), calls=%async_computation.2 | async-start | bytes 262144 | tf_op jit(solution)/shard_map/all_to_all | solution.py:235
  247.2 2.2 copy-start.2
  249.4 1.2 copy-start.3
Sparse Core Ops, SparseCore 0:
  176.5 70.6 all-gather.2

commit v5 on v3

--- a/solution.py
+++ b/solution.py
@@ -15,6 +15,7 @@
 PAIRS = 32
 ZD, XD, CD, YD = 16, 4, 2, 4
 REGION = ("z", "x", "c")
+NEAR = 6
 F32 = jnp.float32
 BF16 = jnp.bfloat16
 
@@ -126,7 +127,7 @@
         in_specs=[SMEM] * 3 + [VMEM],
         out_specs=(VMEM,) * 3,
         scratch_shapes=[pltpu.VMEM((NB, NB * W, W), F32)],
-        compiler_params=pltpu.CompilerParams(vmem_limit_bytes=20 << 20),
+        compiler_params=pltpu.CompilerParams(vmem_limit_bytes=16 << 20),
         name="overlap_products",
     )(pair_flat, support_flat, where, own)
 
@@ -142,13 +143,15 @@
             pltpu.VMEM((NB * W, 2 * CELLS + DEPTH), BF16),
             pltpu.VMEM((NB, NB * W, W), F32),
         ],
-        compiler_params=pltpu.CompilerParams(vmem_limit_bytes=32 << 20),
+        compiler_params=pltpu.CompilerParams(vmem_limit_bytes=26 << 20),
         name="hamiltonian_products",
     )(pair_flat, support_flat, where, conf, ahead, behind, above, pot)
 
 
-def orbital_kernel(support, where, phi, below, above, pot, out):
+def orbital_kernel(support, where, phi, below, above, pot_low, pot_mid, pot_high, out, pot):
     block, row_z = where[2], where[0] // 8
+    for step, piece in enumerate((pot_low, pot_mid, pot_high)):
+        pot[step * NEAR : (step + 1) * NEAR] = piece[...]
     lane = lax.broadcasted_iota(jnp.int32, (8, ROWS, DEPTH), 2)
     row = lax.broadcasted_iota(jnp.int32, (8, ROWS, DEPTH), 1)
 
@@ -163,22 +166,24 @@
         high = jnp.where(row == ROWS - 1, above[:, x].astype(F32), pltpu.roll(centre, ROWS - 1, 1))
         around = lane_neighbours(centre, lane) + low + high + before + after
         live = flag(support, block, x)
-        applied = ((3.0 + pot[lax.rem(x, 8), lax.rem(x // 8 + ZD - row_z, ZD)])[None] * centre - 0.5 * around) * live
+        values = pot[lax.rem(x // 8 - row_z + 3 * ZD // 2, ZD), lax.rem(x, 8)]
+        applied = ((3.0 + values)[None] * centre - 0.5 * around) * live
         out[:, x] = applied.astype(BF16)
         return centre * live, 0
 
     lax.fori_loop(0, PLANES, step, (masked(PLANES - 1), 0))
 
 
-def orbital_apply(support_flat, where, phi, below, above, pot):
+def orbital_apply(support_flat, where, phi, below, above, pieces):
     return pl.pallas_call(
         orbital_kernel,
         out_shape=jax.ShapeDtypeStruct(phi.shape, BF16),
-        in_specs=[SMEM] * 2 + [VMEM] * 4,
+        in_specs=[SMEM] * 2 + [VMEM] * 6,
         out_specs=VMEM,
-        compiler_params=pltpu.CompilerParams(vmem_limit_bytes=24 << 20),
+        scratch_shapes=[pltpu.VMEM((3 * NEAR, 8, ROWS, DEPTH), F32)],
+        compiler_params=pltpu.CompilerParams(vmem_limit_bytes=14 << 20),
         name="orbital_apply",
-    )(support_flat, where, phi, below, above, pot)
+    )(support_flat, where, phi, below, above, *pieces)
 
 
 def ring(count, shift):
@@ -194,14 +199,13 @@
 
     own = lax.all_to_all(phi.transpose(1, 2, 0, 3), REGION, split_axis=0, concat_axis=0, tiled=True)
 
-    column = potential
-    for step in (1, 2, 4, 8):
-        column = jnp.concatenate([column, lax.ppermute(column, "z", ring(ZD, -step))], axis=0)
-    pot_all = lax.all_gather(column[None], ("x", "c"), axis=0, tiled=True)
+    plane_row = lax.all_gather(potential, ("x", "c"), axis=0, tiled=True)
     row_below = lax.ppermute(phi[:, :, 7:], "y", ring(YD, 1))
     row_above = lax.ppermute(phi[:, :, :1], "y", ring(YD, -1))
-    hphi = orbital_apply(support_flat, where, phi, row_below, row_above, pot_all)
-    own, hphi = lax.optimization_barrier((own, hphi))
+    plane_row, row_below, row_above = lax.optimization_barrier((plane_row, row_below, row_above))
+    near = [plane_row if s == 0 else lax.ppermute(plane_row, "z", ring(ZD, -s))
+            for s in range(-2, NEAR - 2)]
+    own, near = lax.optimization_barrier((own, near))
 
     ahead = lax.ppermute(own[:, :4], REGION, ring(PLANES, -1))
     behind = lax.ppermute(own[:, 4:], REGION, ring(PLANES, 1))
@@ -212,9 +216,15 @@
     mine_h, theirs_h = hamiltonian_products(pair_flat, support_flat, where, conf, ahead, behind, above,
                                             potential[0])
     total_h = mine_h + lax.ppermute(theirs_h, "c", swap)
-    total = jnp.stack([total_s, total_h], axis=2).reshape(XD * YD, 2, 8, ZD, W)
+    total = jnp.stack([total_s, total_h], axis=2).reshape(XD * YD, 2, 8, ZD, W).astype(BF16)
+    total, near = lax.optimization_barrier((total, near))
+    column = jnp.stack(near)
+    pieces = [lax.ppermute(column, "z", ring(ZD, NEAR)), column,
+              lax.ppermute(column, "z", ring(ZD, -NEAR))]
     shares = lax.all_to_all(total, ("x", "y"), split_axis=0, concat_axis=0, tiled=True)
-    partial = jnp.sum(shares, axis=0).transpose(2, 0, 1, 3)
+    partial = jnp.sum(shares.astype(F32), axis=0).transpose(2, 0, 1, 3)
+    partial, pieces = lax.optimization_barrier((partial, pieces))
+    hphi = orbital_apply(support_flat, where, phi, row_below, row_above, pieces)
     shares = lax.all_to_all(partial, ("z",), split_axis=0, concat_axis=0, tiled=True)
     result = jnp.sum(shares, axis=0)
     return result[0], result[1], hphi

time: 282 us -> 240 us (0.85)
  blocking collectives: 77.3 us -> 12.8 us
  starting transfers between devices: 74.8 us -> 94.1 us
  waiting for transfers between devices: 81 us -> 84.5 us
    all_to_all x2 -> x0, blocking collectives: 64.2 us -> none  [the longest x1 38 us: local(): lax.all_to_all(total, ('x', 'y'), split_axis=0, concat_axis=0, tiled=True)]
    all_to_all x0 -> x2, starting transfers between devices: none -> 17.3 us  [the longest x1 9.35 us: local(): lax.all_to_all(partial, ('z',), split_axis=0, concat_axis=0, tiled=True)]
    ppermute x4 -> x7, waiting for transfers between devices: 78.5 us -> 71.8 us  [the longest x5 49.8 us: local(): lax.ppermute(plane_row, 'z', ring(ZD, -s))]
    ppermute x1, waiting for transfers between devices: 0.01 us -> 5.72 us  [local(): above = lax.ppermute(own[:, 0], 'y', ring(YD, -1))]
    all_to_all x0 -> x2, waiting for transfers between devices: none -> 2.93 us  [the longest x1 2.93 us: local(): lax.all_to_all(total, ('x', 'y'), split_axis=0, concat_axis=0, tiled=True)]
    ppermute x4 -> x7, starting transfers between devices: 31.8 us -> 33.6 us  [the longest x5 20.9 us: local(): lax.ppermute(plane_row, 'z', ring(ZD, -s))]
    unnamed x14 -> x23, local copies, waits for them, and re-layouts: 7.05 us -> 7.07 us
  transfers between devices with their start and end apart: 12 -> 17, of which waited for: 5 -> 7; matrix products, arithmetic and copies ran while one was open for 2% -> 2% of each run, Pallas kernels for 10% -> 12%
where the time goes in v5:
time: 240 us; the launch traced here: 239 us
  starting transfers between devices  94.1 us (39%)
  waiting for transfers between devices  84.5 us (35%)
  Pallas kernels  29.8 us (12%)
  local copies, waits for them, and re-layouts  13.5 us (6%)
  blocking collectives  12.8 us (5%)
  other arithmetic  3.74 us (2%)
    ppermute x5, waiting for transfers between devices, local(): lax.ppermute(plane_row, 'z', ring(ZD, -s))  49.8 us
    ppermute x5, starting transfers between devices, local(): lax.ppermute(plane_row, 'z', ring(ZD, -s))  20.9 us
    all_to_all x1, starting transfers between devices, local(): lax.all_to_all(phi.transpose(1, 2, 0, 3), REGION, split_axis=0, concat_ax...  19.4 us
    ppermute x1, waiting for transfers between devices, local(): lax.ppermute(column, 'z', ring(ZD, -NEAR))  16.3 us
    pallas_call x1, Pallas kernels, orbital_apply(): pl.pallas_call(orbital_kernel, out_shape=jax.ShapeDtypeStruct(phi.shape,...  14 us
    all_gather x1, blocking collectives, local(): plane_row = lax.all_gather(potential, ('x', 'c'), axis=0, tiled=True)  12.8 us
    pallas_call x1, Pallas kernels, hamiltonian_products(): pl.pallas_call(hamiltonian_kernel, out_shape=(SHARE, SHARE), in_specs=[SM...  11 us
    ppermute x1, starting transfers between devices, local(): lax.ppermute(column, 'z', ring(ZD, NEAR))  9.96 us
  transfers between devices with their start and end apart: 17, of which 7 were waited for; matrix products, arithmetic and copies ran while one was open for 2% of the time, Pallas kernels for 12%

profile of v5, /device:TPU:6, one launch (start us, length us, event | category | flops | bytes accessed | tf_op | source)
XLA Modules:
  0.0 239.4 jit_solution(11242771319749317879)
XLA Ops:
  0.6 5.3 %copy.31 = bf16[8,128,8,128]{3,0,2,1:T(8,128)(2,1)} copy(bf16[8,128,8,128]{3,2,1,0:T(8,128)(2,1)} %phi.1) | data formatting | bytes 4194304 | tf_op args[0]
  6.0 19.4 %all-to-all-start = ((bf16[128,8,8,128]{3,2,1,0:T(8,128)(2,1)}), bf16[128,8,8,128]{3,2,1,0:T(8,128)(2,1)S(1)}, u32[]{:S(2)}, u32[]{:S(2)}) async-start(bf16[128,8,8,128]{3,2,1,0:T(8,128)(2,1)} %bitcast.37), calls=%async_computation | async-start | bytes 4194304 | tf_op jit(solution)/shard_map/all_to_all | solution.py:200
  25.3 0.0 copy-start.6
  25.4 3.3 %fusion.1 = (bf16[8,128,1,128]{3,2,1,0:T(2,128)(2,1)S(1)}, bf16[8,128,1,128]{3,2,1,0:T(2,128)(2,1)S(1)}) fusion(bf16[8,128,8,128]{3,2,1,0:T(8,128)(2,1)} %phi.1), kind=kLoop, calls=%fused_computation.16 | loop fusion | bytes 1048576 | tf_op jit(solution)/shard_map/slice | solution.py:204
  28.6 3.5 %collective-permute-start = (bf16[8,128,1,128]{3,2,1,0:T(2,128)(2,1)S(1)}, bf16[8,128,1,128]{3,2,1,0:T(2,128)(2,1)S(1)}, u32[]{:S(2)}, u32[]{:S(2)}) collective-permute-start(bf16[8,128,1,128]{3,2,1,0:T(2,128)(2,1)S(1)} %get-tuple-element.58), channel_id=1, source_target_pairs={{0,1},{1,2},{2,3},{3,0},{4,5},{5,6},{6,7},{7,4},{8,9},{9,10},{10,1... | collective-permute-start | bytes 786440 | tf_op jit(solution)/shard_map/ppermute | solution.py:203
  32.1 3.6 %collective-permute-start.1 = (bf16[8,128,1,128]{3,2,1,0:T(2,128)(2,1)S(1)}, bf16[8,128,1,128]{3,2,1,0:T(2,128)(2,1)S(1)}, u32[]{:S(2)}, u32[]{:S(2)}) collective-permute-start(bf16[8,128,1,128]{3,2,1,0:T(2,128)(2,1)S(1)} %get-tuple-element.57), channel_id=1, source_target_pairs={{0,3},{1,0},{2,1},{3,2},{4,7},{5,4},{6,5},{7,6},{8,11},{9,8},{10,9... | collective-permute-start | bytes 786440 | tf_op jit(solution)/shard_map/ppermute | solution.py:204
  35.7 12.8 %all_gather.3 = f32[8,8,128]{2,1,0:T(8,128)S(1)} all-gather(f32[1,8,128]{2,1,0:T(8,128)S(1)} %copy-done.6), channel_id=1, replica_groups=mesh['z'=16,'x'=4,'c'=2,'y'=4] {'x','c'}, dimensions={0}, use_global_device_ids=true | all-gather | bytes 36864 | tf_op jit(solution)/shard_map/all_gather | solution.py:202
  48.5 0.0 collective-permute-done.below
  48.5 0.8 copy-done.1
  49.3 0.0 collective-permute-done.1.above
  49.3 0.8 copy-done.3
  50.1 4.3 %collective-permute-start.2 = (f32[8,8,128]{2,1,0:T(8,128)S(1)}, f32[8,8,128]{2,1,0:T(8,128)S(1)}, u32[]{:S(2)}, u32[]{:S(2)}) collective-permute-start(f32[8,8,128]{2,1,0:T(8,128)S(1)} %all_gather.3), channel_id=1, source_target_pairs={{0,64},{32,96},{64,128},{96,160},{128,192},{160,224},{192,256},{22... | collective-permute-start | bytes 98312 | tf_op jit(solution)/shard_map/ppermute | solution.py:206
  54.4 3.4 %collective-permute-start.3 = (f32[8,8,128]{2,1,0:T(8,128)S(1)}, f32[8,8,128]{2,1,0:T(8,128)S(1)}, u32[]{:S(2)}, u32[]{:S(2)}) collective-permute-start(f32[8,8,128]{2,1,0:T(8,128)S(1)} %all_gather.3), channel_id=1, source_target_pairs={{0,32},{32,64},{64,96},{96,128},{128,160},{160,192},{192,224},{224... | collective-permute-start | bytes 98312 | tf_op jit(solution)/shard_map/ppermute | solution.py:206
  57.9 3.6 %collective-permute-start.4 = (f32[8,8,128]{2,1,0:T(8,128)S(1)}, f32[8,8,128]{2,1,0:T(8,128)S(1)}, u32[]{:S(2)}, u32[]{:S(2)}) collective-permute-start(f32[8,8,128]{2,1,0:T(8,128)S(1)} %all_gather.3), channel_id=1, source_target_pairs={{0,480},{32,0},{64,32},{96,64},{128,96},{160,128},{192,160},{224,1... | collective-permute-start | bytes 98312 | tf_op jit(solution)/shard_map/ppermute | solution.py:206
  61.5 2.6 %collective-permute-start.5 = (f32[8,8,128]{2,1,0:T(8,128)S(1)}, f32[8,8,128]{2,1,0:T(8,128)S(1)}, u32[]{:S(2)}, u32[]{:S(2)}) collective-permute-start(f32[8,8,128]{2,1,0:T(8,128)S(1)} %all_gather.3), channel_id=1, source_target_pairs={{0,448},{32,480},{64,0},{96,32},{128,64},{160,96},{192,128},{224,1... | collective-permute-start | bytes 98312 | tf_op jit(solution)/shard_map/ppermute | solution.py:206
  64.1 6.9 %collective-permute-start.6 = (f32[8,8,128]{2,1,0:T(8,128)S(1)}, f32[8,8,128]{2,1,0:T(8,128)S(1)}, u32[]{:S(2)}, u32[]{:S(2)}) collective-permute-start(f32[8,8,128]{2,1,0:T(8,128)S(1)} %all_gather.3), channel_id=1, source_target_pairs={{0,416},{32,448},{64,480},{96,0},{128,32},{160,64},{192,96},{224,1... | collective-permute-start | bytes 98312 | tf_op jit(solution)/shard_map/ppermute | solution.py:206
  71.1 49.8 %collective-permute-done.2 = f32[8,8,128]{2,1,0:T(8,128)S(1)} collective-permute-done((f32[8,8,128]{2,1,0:T(8,128)S(1)}, f32[8,8,128]{2,1,0:T(8,128)S(1)}, u32[]{:S(2)}, u32[]{:S(2)}) %collective-permute-start.2) | collective-permute-done | bytes 32800 | tf_op jit(solution)/shard_map/ppermute | solution.py:206
  120.9 0.0 collective-permute-done.5
  120.9 1.6 all-to-all-done.own
  122.4 1.7 fusion
  124.2 3.1 %collective-permute-start.8 = (bf16[128,4,8,128]{3,2,1,0:T(8,128)(2,1)}, bf16[128,4,8,128]{3,2,1,0:T(8,128)(2,1)S(1)}, u32[]{:S(2)}, u32[]{:S(2)}) collective-permute-start(bf16[128,4,8,128]{3,2,1,0:T(8,128)(2,1)} %get-tuple-element.56), channel_id=1, source_target_pairs={{0,508},{4,0},{8,4},{12,8},{16,12},{20,16},{24,20},{28,24},{32,28}... | collective-permute-start | bytes 3145736 | tf_op jit(solution)/shard_map/ppermute | solution.py:210
  127.3 1.9 collective-permute-start.9
  129.3 0.1 copy.22
  129.4 0.1 reshape.19.pairs
  129.5 0.1 pad_add_fusion.where
  129.6 4.8 %overlap_products.1 = (bf16[1024,1024]{1,0:T(8,128)(2,1)S(1)}, f32[4,4,8,16,128]{4,3,2,1,0:T(8,128)S(1)}, f32[4,4,8,16,128]{4,3,2,1,0:T(8,128)S(1)}) custom-call(s32[64]{0:T(128)S(1)} %reshape.19.pairs, s32[1024]{0:T(1024)S(1)} %bitcast.33, s32[3]{0:T(128)S(1)} %pad_add_fusion.where, bf16[128,8,8,128]{3,2,1,0:T(8,128)(2,1)S(1)} %all-to-all-done.own), custom_call_target="tpu_custom_call" | custom-call | tf_op jit(solution)/shard_map/overlap_products/pallas_call | solution.py:124
  134.4 4.9 %collective-permute-start.7 = (f32[4,4,8,16,128]{4,3,2,1,0:T(8,128)S(1)}, f32[4,4,8,16,128]{4,3,2,1,0:T(8,128)S(1)}, u32[]{:S(2)}, u32[]{:S(2)}) collective-permute-start(f32[4,4,8,16,128]{4,3,2,1,0:T(8,128)S(1)} %get-tuple-element.32), channel_id=1, source_target_pairs={{0,4},{4,0},{1,5},{5,1},{2,6},{6,2},{3,7},{7,3},{8,12},{12,8},{9,1... | collective-permute-start | bytes 3145736 | tf_op jit(solution)/shard_map/ppermute | solution.py:215
  139.2 0.1 slice_bitcast_fusion
  139.3 4.9 %collective-permute-start.10 = (bf16[128,8,128]{2,1,0:T(8,128)(2,1)S(1)}, bf16[128,8,128]{2,1,0:T(8,128)(2,1)S(1)}, u32[]{:S(2)}, u32[]{:S(2)}) collective-permute-start(bf16[128,8,128]{2,1,0:T(8,128)(2,1)S(1)} %slice_bitcast_fusion), channel_id=1, source_target_pairs={{0,3},{1,0},{2,1},{3,2},{4,7},{5,4},{6,5},{7,6},{8,11},{9,8},{10,9... | collective-permute-start | bytes 786440 | tf_op jit(solution)/shard_map/ppermute | solution.py:212
  144.3 5.7 %collective-permute-done.10.above = bf16[128,8,128]{2,1,0:T(8,128)(2,1)S(1)} collective-permute-done((bf16[128,8,128]{2,1,0:T(8,128)(2,1)S(1)}, bf16[128,8,128]{2,1,0:T(8,128)(2,1)S(1)}, u32[]{:S(2)}, u32[]{:S(2)}) %collective-permute-start.10) | collective-permute-done | bytes 262176 | tf_op jit(solution)/shard_map/ppermute | solution.py:212
  150.0 11.0 %hamiltonian_products.1 = (f32[4,4,8,16,128]{4,3,2,1,0:T(8,128)S(1)}, f32[4,4,8,16,128]{4,3,2,1,0:T(8,128)S(1)}) custom-call(s32[64]{0:T(128)S(1)} %reshape.19.pairs, s32[1024]{0:T(1024)S(1)} %bitcast.34, s32[3]{0:T(128)S(1)} %pad_add_fusion.where, bf16[1024,1024]{1,0:T(8,128)(2,1)S(1)} %get-tuple-element.33.conf, ...), custom_call_target="tpu_custom_call" | custom-call | tf_op jit(solution)/shard_map/hamiltonian_products/pallas_call | solution.py:136
  161.0 1.9 collective-permute-start.11
  163.0 0.1 add_convert_fusion.1
  163.1 2.5 %collective-permute-done.11 = f32[4,4,8,16,128]{4,3,2,1,0:T(8,128)S(1)} collective-permute-done((f32[4,4,8,16,128]{4,3,2,1,0:T(8,128)S(1)}, f32[4,4,8,16,128]{4,3,2,1,0:T(8,128)S(1)}, u32[]{:S(2)}, u32[]{:S(2)}) %collective-permute-start.11) | collective-permute-done | bytes 1048608 | tf_op jit(solution)/shard_map/ppermute | solution.py:218
  165.6 0.1 add_convert_fusion
  165.7 1.1 pad_maximum_fusion
  166.8 7.9 %all-to-all-start.1 = ((bf16[16,2,8,16,128]{4,3,2,1,0:T(8,128)(2,1)}), bf16[16,2,8,16,128]{4,3,2,1,0:T(8,128)(2,1)}, u32[]{:S(2)}, u32[]{:S(2)}) async-start(bf16[16,2,8,16,128]{4,3,2,1,0:T(8,128)(2,1)} %pad_maximum_fusion), calls=%async_computation.1 | async-start | bytes 2097152 | tf_op jit(solution)/shard_map/all_to_all | solution.py:224
  174.8 10.0 %collective-permute-start.12 = (f32[6,8,8,128]{3,2,1,0:T(8,128)S(1)}, f32[6,8,8,128]{3,2,1,0:T(8,128)S(1)}, u32[]{:S(2)}, u32[]{:S(2)}) collective-permute-start(f32[6,8,8,128]{3,2,1,0:T(8,128)S(1)} %bitcast_dynamic-update-slice_fusion.pot_mid), channel_id=1, source_target_pairs={{0,192},{32,224},{64,256},{96,288},{128,320},{160,352},{192,384},{... | collective-permute-start | bytes 589832 | tf_op jit(solution)/shard_map/ppermute | solution.py:222
  184.8 2.8 %collective-permute-start.13 = (f32[6,8,8,128]{3,2,1,0:T(8,128)S(1)}, f32[6,8,8,128]{3,2,1,0:T(8,128)}, u32[]{:S(2)}, u32[]{:S(2)}) collective-permute-start(f32[6,8,8,128]{3,2,1,0:T(8,128)S(1)} %bitcast_dynamic-update-slice_fusion.pot_mid), channel_id=1, source_target_pairs={{0,320},{32,352},{64,384},{96,416},{128,448},{160,480},{192,0},{22... | collective-permute-start | bytes 589832 | tf_op jit(solution)/shard_map/ppermute | solution.py:223
  187.6 2.9 %all-to-all-done.1 = bf16[16,2,8,16,128]{4,3,2,1,0:T(8,128)(2,1)} async-done(((bf16[16,2,8,16,128]{4,3,2,1,0:T(8,128)(2,1)}), bf16[16,2,8,16,128]{4,3,2,1,0:T(8,128)(2,1)}, u32[]{:S(2)}, u32[]{:S(2)}) %all-to-all-start.1) | async-done | bytes 1048608 | tf_op jit(solution)/shard_map/all_to_all | solution.py:224
  190.5 1.4 convert_reduce_fusion
  191.9 5.6 %collective-permute-done.12.pot_low = f32[6,8,8,128]{3,2,1,0:T(8,128)S(1)} collective-permute-done((f32[6,8,8,128]{3,2,1,0:T(8,128)S(1)}, f32[6,8,8,128]{3,2,1,0:T(8,128)S(1)}, u32[]{:S(2)}, u32[]{:S(2)}) %collective-permute-start.12) | collective-permute-done | bytes 196640 | tf_op jit(solution)/shard_map/ppermute | solution.py:222
  197.5 16.3 %collective-permute-done.13.pot_high = f32[6,8,8,128]{3,2,1,0:T(8,128)} collective-permute-done((f32[6,8,8,128]{3,2,1,0:T(8,128)S(1)}, f32[6,8,8,128]{3,2,1,0:T(8,128)}, u32[]{:S(2)}, u32[]{:S(2)}) %collective-permute-start.13) | collective-permute-done | bytes 196640 | tf_op jit(solution)/shard_map/ppermute | solution.py:223
  213.8 0.7 copy.27
  214.5 9.3 %all-to-all-start.2 = ((f32[16,2,8,128]{3,2,1,0:T(8,128)}), f32[16,2,8,128]{3,2,1,0:T(8,128)}, u32[]{:S(2)}, u32[]{:S(2)}) async-start(f32[16,2,8,128]{3,2,1,0:T(8,128)} %copy.27), calls=%async_computation.2 | async-start | bytes 262144 | tf_op jit(solution)/shard_map/all_to_all | solution.py:228
  223.9 14.0 %orbital_apply.1 = bf16[8,128,8,128]{3,2,1,0:T(8,128)(2,1)} custom-call(s32[1024]{0:T(1024)S(1)} %bitcast.35, s32[3]{0:T(128)S(1)} %pad_add_fusion.where, bf16[8,128,8,128]{3,2,1,0:T(8,128)(2,1)S(1)} %copy-done, bf16[8,128,1,128]{3,2,1,0:T(2,128)(2,1)S(1)} %copy-done.2, bf16[8,128,1,128]{3,2,1,0:T(2,128)(2,1)S(1)} %copy-done.4, ...), custom_call_target="tpu_custom_call" | custom-call | tf_op jit(solution)/shard_map/orbital_apply/pallas_call | solution.py:178
  237.9 0.9 reduce_sum.19
  238.8 0.6 slice_bitcast_fusion.1
  (26 shorter events, 0.1 us)
Async XLA Ops:
  6.0 116.5 %all-to-all-start = ((bf16[128,8,8,128]{3,2,1,0:T(8,128)(2,1)}), bf16[128,8,8,128]{3,2,1,0:T(8,128)(2,1)S(1)}, u32[]{:S(2)}, u32[]{:S(2)}) async-start(bf16[128,8,8,128]{3,2,1,0:T(8,128)(2,1)} %bitcast.37), calls=%async_computation | async-start | bytes 4194304 | tf_op jit(solution)/shard_map/all_to_all | solution.py:200
  25.3 10.4 %copy-start.6 = (f32[1,8,128]{2,1,0:T(8,128)S(1)}, f32[1,8,128]{2,1,0:T(8,128)}, u32[]{:S(2)}) copy-start(f32[1,8,128]{2,1,0:T(8,128)} %param.5) | copy-start | bytes 12292
  28.6 19.9 %collective-permute-start = (bf16[8,128,1,128]{3,2,1,0:T(2,128)(2,1)S(1)}, bf16[8,128,1,128]{3,2,1,0:T(2,128)(2,1)S(1)}, u32[]{:S(2)}, u32[]{:S(2)}) collective-permute-start(bf16[8,128,1,128]{3,2,1,0:T(2,128)(2,1)S(1)} %get-tuple-element.58), channel_id=1, source_target_pairs={{0,1},{1,2},{2,3},{3,0},{4,5},{5,6},{6,7},{7,4},{8,9},{9,10},{10,1... | collective-permute-start | bytes 786440 | tf_op jit(solution)/shard_map/ppermute | solution.py:203
  32.1 17.2 %collective-permute-start.1 = (bf16[8,128,1,128]{3,2,1,0:T(2,128)(2,1)S(1)}, bf16[8,128,1,128]{3,2,1,0:T(2,128)(2,1)S(1)}, u32[]{:S(2)}, u32[]{:S(2)}) collective-permute-start(bf16[8,128,1,128]{3,2,1,0:T(2,128)(2,1)S(1)} %get-tuple-element.57), channel_id=1, source_target_pairs={{0,3},{1,0},{2,1},{3,2},{4,7},{5,4},{6,5},{7,6},{8,11},{9,8},{10,9... | collective-permute-start | bytes 786440 | tf_op jit(solution)/shard_map/ppermute | solution.py:204
  48.5 80.8 %copy-start.7 = (s32[32,2]{0,1:T(2,128)S(1)}, s32[32,2]{0,1:T(2,128)}, u32[]{:S(2)}) copy-start(s32[32,2]{0,1:T(2,128)} %param.6) | copy-start | bytes 772
  48.5 81.1 %copy-start.5 = (s32[8,128]{1,0:T(8,128)S(1)}, s32[8,128]{1,0:T(8,128)}, u32[]{:S(2)}) copy-start(s32[8,128]{1,0:T(8,128)} %param.7) | copy-start | bytes 12292
  48.5 0.8 copy-start.1
  49.3 0.8 copy-start.3
  50.1 70.7 %collective-permute-start.2 = (f32[8,8,128]{2,1,0:T(8,128)S(1)}, f32[8,8,128]{2,1,0:T(8,128)S(1)}, u32[]{:S(2)}, u32[]{:S(2)}) collective-permute-start(f32[8,8,128]{2,1,0:T(8,128)S(1)} %all_gather.3), channel_id=1, source_target_pairs={{0,64},{32,96},{64,128},{96,160},{128,192},{160,224},{192,256},{22... | collective-permute-start | bytes 98312 | tf_op jit(solution)/shard_map/ppermute | solution.py:206
  54.4 66.4 %collective-permute-start.3 = (f32[8,8,128]{2,1,0:T(8,128)S(1)}, f32[8,8,128]{2,1,0:T(8,128)S(1)}, u32[]{:S(2)}, u32[]{:S(2)}) collective-permute-start(f32[8,8,128]{2,1,0:T(8,128)S(1)} %all_gather.3), channel_id=1, source_target_pairs={{0,32},{32,64},{64,96},{96,128},{128,160},{160,192},{192,224},{224... | collective-permute-start | bytes 98312 | tf_op jit(solution)/shard_map/ppermute | solution.py:206
  57.9 63.0 %collective-permute-start.4 = (f32[8,8,128]{2,1,0:T(8,128)S(1)}, f32[8,8,128]{2,1,0:T(8,128)S(1)}, u32[]{:S(2)}, u32[]{:S(2)}) collective-permute-start(f32[8,8,128]{2,1,0:T(8,128)S(1)} %all_gather.3), channel_id=1, source_target_pairs={{0,480},{32,0},{64,32},{96,64},{128,96},{160,128},{192,160},{224,1... | collective-permute-start | bytes 98312 | tf_op jit(solution)/shard_map/ppermute | solution.py:206
  61.5 59.4 %collective-permute-start.5 = (f32[8,8,128]{2,1,0:T(8,128)S(1)}, f32[8,8,128]{2,1,0:T(8,128)S(1)}, u32[]{:S(2)}, u32[]{:S(2)}) collective-permute-start(f32[8,8,128]{2,1,0:T(8,128)S(1)} %all_gather.3), channel_id=1, source_target_pairs={{0,448},{32,480},{64,0},{96,32},{128,64},{160,96},{192,128},{224,1... | collective-permute-start | bytes 98312 | tf_op jit(solution)/shard_map/ppermute | solution.py:206
  64.1 56.7 %collective-permute-start.6 = (f32[8,8,128]{2,1,0:T(8,128)S(1)}, f32[8,8,128]{2,1,0:T(8,128)S(1)}, u32[]{:S(2)}, u32[]{:S(2)}) collective-permute-start(f32[8,8,128]{2,1,0:T(8,128)S(1)} %all_gather.3), channel_id=1, source_target_pairs={{0,416},{32,448},{64,480},{96,0},{128,32},{160,64},{192,96},{224,1... | collective-permute-start | bytes 98312 | tf_op jit(solution)/shard_map/ppermute | solution.py:206
  124.2 25.8 %collective-permute-start.8 = (bf16[128,4,8,128]{3,2,1,0:T(8,128)(2,1)}, bf16[128,4,8,128]{3,2,1,0:T(8,128)(2,1)S(1)}, u32[]{:S(2)}, u32[]{:S(2)}) collective-permute-start(bf16[128,4,8,128]{3,2,1,0:T(8,128)(2,1)} %get-tuple-element.56), channel_id=1, source_target_pairs={{0,508},{4,0},{8,4},{12,8},{16,12},{20,16},{24,20},{28,24},{32,28}... | collective-permute-start | bytes 3145736 | tf_op jit(solution)/shard_map/ppermute | solution.py:210
  127.3 22.7 %collective-permute-start.9 = (bf16[128,4,8,128]{3,2,1,0:T(8,128)(2,1)}, bf16[128,4,8,128]{3,2,1,0:T(8,128)(2,1)}, u32[]{:S(2)}, u32[]{:S(2)}) collective-permute-start(bf16[128,4,8,128]{3,2,1,0:T(8,128)(2,1)} %get-tuple-element.55), channel_id=1, source_target_pairs={{0,4},{4,8},{8,12},{12,16},{16,20},{20,24},{24,28},{28,32},{32,36}... | collective-permute-start | bytes 3145736 | tf_op jit(solution)/shard_map/ppermute | solution.py:211
  134.4 28.6 %collective-permute-start.7 = (f32[4,4,8,16,128]{4,3,2,1,0:T(8,128)S(1)}, f32[4,4,8,16,128]{4,3,2,1,0:T(8,128)S(1)}, u32[]{:S(2)}, u32[]{:S(2)}) collective-permute-start(f32[4,4,8,16,128]{4,3,2,1,0:T(8,128)S(1)} %get-tuple-element.32), channel_id=1, source_target_pairs={{0,4},{4,0},{1,5},{5,1},{2,6},{6,2},{3,7},{7,3},{8,12},{12,8},{9,1... | collective-permute-start | bytes 3145736 | tf_op jit(solution)/shard_map/ppermute | solution.py:215
  139.3 10.7 %collective-permute-start.10 = (bf16[128,8,128]{2,1,0:T(8,128)(2,1)S(1)}, bf16[128,8,128]{2,1,0:T(8,128)(2,1)S(1)}, u32[]{:S(2)}, u32[]{:S(2)}) collective-permute-start(bf16[128,8,128]{2,1,0:T(8,128)(2,1)S(1)} %slice_bitcast_fusion), channel_id=1, source_target_pairs={{0,3},{1,0},{2,1},{3,2},{4,7},{5,4},{6,5},{7,6},{8,11},{9,8},{10,9... | collective-permute-start | bytes 786440 | tf_op jit(solution)/shard_map/ppermute | solution.py:212
  161.0 4.6 %collective-permute-start.11 = (f32[4,4,8,16,128]{4,3,2,1,0:T(8,128)S(1)}, f32[4,4,8,16,128]{4,3,2,1,0:T(8,128)S(1)}, u32[]{:S(2)}, u32[]{:S(2)}) collective-permute-start(f32[4,4,8,16,128]{4,3,2,1,0:T(8,128)S(1)} %get-tuple-element.35), channel_id=1, source_target_pairs={{0,4},{4,0},{1,5},{5,1},{2,6},{6,2},{3,7},{7,3},{8,12},{12,8},{9,1... | collective-permute-start | bytes 3145736 | tf_op jit(solution)/shard_map/ppermute | solution.py:218
  166.8 57.1 %copy-start = (bf16[8,128,8,128]{3,2,1,0:T(8,128)(2,1)S(1)}, bf16[8,128,8,128]{3,2,1,0:T(8,128)(2,1)}, u32[]{:S(2)}) copy-start(bf16[8,128,8,128]{3,2,1,0:T(8,128)(2,1)} %phi.1) | copy-start | bytes 6291460
  166.8 57.1 %copy-start.2 = (bf16[8,128,1,128]{3,2,1,0:T(2,128)(2,1)S(1)}, bf16[8,128,1,128]{3,2,1,0:T(2,128)(2,1)}, u32[]{:S(2)}) copy-start(bf16[8,128,1,128]{3,2,1,0:T(2,128)(2,1)} %copy-done.1) | copy-start | bytes 786436
  166.8 57.1 %copy-start.4 = (bf16[8,128,1,128]{3,2,1,0:T(2,128)(2,1)S(1)}, bf16[8,128,1,128]{3,2,1,0:T(2,128)(2,1)}, u32[]{:S(2)}) copy-start(bf16[8,128,1,128]{3,2,1,0:T(2,128)(2,1)} %copy-done.3) | copy-start | bytes 786436
  166.8 23.7 %all-to-all-start.1 = ((bf16[16,2,8,16,128]{4,3,2,1,0:T(8,128)(2,1)}), bf16[16,2,8,16,128]{4,3,2,1,0:T(8,128)(2,1)}, u32[]{:S(2)}, u32[]{:S(2)}) async-start(bf16[16,2,8,16,128]{4,3,2,1,0:T(8,128)(2,1)} %pad_maximum_fusion), calls=%async_computation.1 | async-start | bytes 2097152 | tf_op jit(solution)/shard_map/all_to_all | solution.py:224
  174.8 22.7 %collective-permute-start.12 = (f32[6,8,8,128]{3,2,1,0:T(8,128)S(1)}, f32[6,8,8,128]{3,2,1,0:T(8,128)S(1)}, u32[]{:S(2)}, u32[]{:S(2)}) collective-permute-start(f32[6,8,8,128]{3,2,1,0:T(8,128)S(1)} %bitcast_dynamic-update-slice_fusion.pot_mid), channel_id=1, source_target_pairs={{0,192},{32,224},{64,256},{96,288},{128,320},{160,352},{192,384},{... | collective-permute-start | bytes 589832 | tf_op jit(solution)/shard_map/ppermute | solution.py:222
  184.8 29.1 %collective-permute-start.13 = (f32[6,8,8,128]{3,2,1,0:T(8,128)S(1)}, f32[6,8,8,128]{3,2,1,0:T(8,128)}, u32[]{:S(2)}, u32[]{:S(2)}) collective-permute-start(f32[6,8,8,128]{3,2,1,0:T(8,128)S(1)} %bitcast_dynamic-update-slice_fusion.pot_mid), channel_id=1, source_target_pairs={{0,320},{32,352},{64,384},{96,416},{128,448},{160,480},{192,0},{22... | collective-permute-start | bytes 589832 | tf_op jit(solution)/shard_map/ppermute | solution.py:223
  214.5 23.3 %all-to-all-start.2 = ((f32[16,2,8,128]{3,2,1,0:T(8,128)}), f32[16,2,8,128]{3,2,1,0:T(8,128)}, u32[]{:S(2)}, u32[]{:S(2)}) async-start(f32[16,2,8,128]{3,2,1,0:T(8,128)} %copy.27), calls=%async_computation.2 | async-start | bytes 262144 | tf_op jit(solution)/shard_map/all_to_all | solution.py:228

commit v6 on v5

--- a/solution.py
+++ b/solution.py
@@ -15,7 +15,7 @@
 PAIRS = 32
 ZD, XD, CD, YD = 16, 4, 2, 4
 REGION = ("z", "x", "c")
-NEAR = 6
+STRIDE = (0, 3, 6, 9, 12, 15)
 F32 = jnp.float32
 BF16 = jnp.bfloat16
 
@@ -150,8 +150,9 @@
 
 def orbital_kernel(support, where, phi, below, above, pot_low, pot_mid, pot_high, out, pot):
     block, row_z = where[2], where[0] // 8
+    core = where[1]
     for step, piece in enumerate((pot_low, pot_mid, pot_high)):
-        pot[step * NEAR : (step + 1) * NEAR] = piece[...]
+        pot[step] = piece[...]
     lane = lax.broadcasted_iota(jnp.int32, (8, ROWS, DEPTH), 2)
     row = lax.broadcasted_iota(jnp.int32, (8, ROWS, DEPTH), 1)
 
@@ -166,7 +167,8 @@
         high = jnp.where(row == ROWS - 1, above[:, x].astype(F32), pltpu.roll(centre, ROWS - 1, 1))
         around = lane_neighbours(centre, lane) + low + high + before + after
         live = flag(support, block, x)
-        values = pot[lax.rem(x // 8 - row_z + 3 * ZD // 2, ZD), lax.rem(x, 8)]
+        ahead_by = lax.rem(x // 8 - row_z + ZD, ZD) + 1
+        values = pot[lax.rem(ahead_by, 3), lax.rem(x + core, CD), ahead_by // 3, lax.rem(x // 2, XD)]
         applied = ((3.0 + values)[None] * centre - 0.5 * around) * live
         out[:, x] = applied.astype(BF16)
         return centre * live, 0
@@ -180,7 +182,7 @@
         out_shape=jax.ShapeDtypeStruct(phi.shape, BF16),
         in_specs=[SMEM] * 2 + [VMEM] * 6,
         out_specs=VMEM,
-        scratch_shapes=[pltpu.VMEM((3 * NEAR, 8, ROWS, DEPTH), F32)],
+        scratch_shapes=[pltpu.VMEM((3, CD, len(STRIDE), XD, ROWS, DEPTH), F32)],
         compiler_params=pltpu.CompilerParams(vmem_limit_bytes=14 << 20),
         name="orbital_apply",
     )(support_flat, where, phi, below, above, *pieces)
@@ -199,17 +201,18 @@
 
     own = lax.all_to_all(phi.transpose(1, 2, 0, 3), REGION, split_axis=0, concat_axis=0, tiled=True)
 
-    plane_row = lax.all_gather(potential, ("x", "c"), axis=0, tiled=True)
+    planes = lax.all_gather(potential, "x", axis=0, tiled=True)
     row_below = lax.ppermute(phi[:, :, 7:], "y", ring(YD, 1))
     row_above = lax.ppermute(phi[:, :, :1], "y", ring(YD, -1))
-    plane_row, row_below, row_above = lax.optimization_barrier((plane_row, row_below, row_above))
-    near = [plane_row if s == 0 else lax.ppermute(plane_row, "z", ring(ZD, -s))
-            for s in range(-2, NEAR - 2)]
-    own, near = lax.optimization_barrier((own, near))
-
-    ahead = lax.ppermute(own[:, :4], REGION, ring(PLANES, -1))
-    behind = lax.ppermute(own[:, 4:], REGION, ring(PLANES, 1))
-    above = lax.ppermute(own[:, 0], "y", ring(YD, -1))
+    planes, row_below, row_above = lax.optimization_barrier((planes, row_below, row_above))
+    strided = [lax.ppermute(planes, "z", ring(ZD, -s)) if s else planes for s in STRIDE]
+    own, strided = lax.optimization_barrier((own, strided))
+
+    own, low_half, high_half, edge = lax.optimization_barrier((own, own[:, :4], own[:, 4:], own[:, 0]))
+    ahead = lax.ppermute(low_half, REGION, ring(PLANES, -1))
+    behind = lax.ppermute(high_half, REGION, ring(PLANES, 1))
+    above = lax.ppermute(edge, "y", ring(YD, -1))
+    own, above = lax.optimization_barrier((own, above))
     conf, mine_s, theirs_s = overlap_products(pair_flat, support_flat, where, own)
     swap = [(0, 1), (1, 0)]
     total_s = mine_s + lax.ppermute(theirs_s, "c", swap)
@@ -217,10 +220,10 @@
                                             potential[0])
     total_h = mine_h + lax.ppermute(theirs_h, "c", swap)
     total = jnp.stack([total_s, total_h], axis=2).reshape(XD * YD, 2, 8, ZD, W).astype(BF16)
-    total, near = lax.optimization_barrier((total, near))
-    column = jnp.stack(near)
-    pieces = [lax.ppermute(column, "z", ring(ZD, NEAR)), column,
-              lax.ppermute(column, "z", ring(ZD, -NEAR))]
+    total, strided = lax.optimization_barrier((total, strided))
+    column = jnp.stack(strided)
+    column = jnp.stack([column, lax.ppermute(column, "c", swap)])
+    pieces = [lax.ppermute(column, "z", ring(ZD, 1)), column, lax.ppermute(column, "z", ring(ZD, -1))]
     shares = lax.all_to_all(total, ("x", "y"), split_axis=0, concat_axis=0, tiled=True)
     partial = jnp.sum(shares.astype(F32), axis=0).transpose(2, 0, 1, 3)
     partial, pieces = lax.optimization_barrier((partial, pieces))

time: 240 us -> 219 us (0.912)
  waiting for transfers between devices: 84.5 us -> 66.5 us
  starting transfers between devices: 94.1 us -> 89.4 us
    ppermute x10 -> x11, waiting for transfers between devices: 77.5 us -> 56.6 us  [the longest x5 48.7 us: local(): lax.ppermute(planes, 'z', ring(ZD, -s))]
    all_to_all x1, starting transfers between devices: 9.35 us -> 4.17 us  [local(): lax.all_to_all(partial, ('z',), split_axis=0, concat_axis=0, tiled=True)]
    all_to_all x1, waiting for transfers between devices: 2.93 us -> 5.37 us  [local(): lax.all_to_all(total, ('x', 'y'), split_axis=0, concat_axis=0, tiled=True)]
    ppermute x10 -> x11, starting transfers between devices: 43.6 us -> 45.1 us  [the longest x5 26.9 us: local(): lax.ppermute(planes, 'z', ring(ZD, -s))]
  transfers between devices with their start and end apart: 17 -> 18, of which waited for: 7 -> 9; matrix products, arithmetic and copies ran while one was open for 2% -> 2% of each run, Pallas kernels for 12% -> 14%
where the time goes in v6:
time: 219 us; the launch traced here: 217 us
  starting transfers between devices  89.4 us (41%)
  waiting for transfers between devices  66.5 us (30%)
  Pallas kernels  29.8 us (14%)
  local copies, waits for them, and re-layouts  14.3 us (7%)
  blocking collectives  11.9 us (5%)
  other arithmetic  3.76 us (2%)
    ppermute x5, waiting for transfers between devices, local(): lax.ppermute(planes, 'z', ring(ZD, -s))  48.7 us
    ppermute x5, starting transfers between devices, local(): lax.ppermute(planes, 'z', ring(ZD, -s))  26.9 us
    all_to_all x1, starting transfers between devices, local(): lax.all_to_all(phi.transpose(1, 2, 0, 3), REGION, split_axis=0, concat_ax...  19.4 us
    pallas_call x1, Pallas kernels, orbital_apply(): pl.pallas_call(orbital_kernel, out_shape=jax.ShapeDtypeStruct(phi.shape,...  14 us
    all_gather x1, blocking collectives, local(): planes = lax.all_gather(potential, 'x', axis=0, tiled=True)  11.9 us
    pallas_call x1, Pallas kernels, hamiltonian_products(): pl.pallas_call(hamiltonian_kernel, out_shape=(SHARE, SHARE), in_specs=[SM...  11 us
    all_to_all x1, starting transfers between devices, local(): lax.all_to_all(total, ('x', 'y'), split_axis=0, concat_axis=0, tiled=True)  8.64 us
    unnamed x23, local copies, waits for them, and re-layouts  7.09 us
  transfers between devices with their start and end apart: 18, of which 9 were waited for; matrix products, arithmetic and copies ran while one was open for 2% of the time, Pallas kernels for 14%

profile of v6, /device:TPU:6, one launch (start us, length us, event | category | flops | bytes accessed | tf_op | source)
XLA Modules:
  0.0 216.6 jit_solution(474748366405496115)
XLA Ops:
  0.6 5.3 %copy.31 = bf16[8,128,8,128]{3,0,2,1:T(8,128)(2,1)} copy(bf16[8,128,8,128]{3,2,1,0:T(8,128)(2,1)} %phi.1) | data formatting | bytes 4194304 | tf_op args[0]
  6.0 19.4 %all-to-all-start = ((bf16[128,8,8,128]{3,2,1,0:T(8,128)(2,1)}), bf16[128,8,8,128]{3,2,1,0:T(8,128)(2,1)S(1)}, u32[]{:S(2)}, u32[]{:S(2)}) async-start(bf16[128,8,8,128]{3,2,1,0:T(8,128)(2,1)} %bitcast.39), calls=%async_computation | async-start | bytes 4194304 | tf_op jit(solution)/shard_map/all_to_all | solution.py:202
  25.4 3.3 %fusion.1 = (bf16[8,128,1,128]{3,2,1,0:T(2,128)(2,1)S(1)}, bf16[8,128,1,128]{3,2,1,0:T(2,128)(2,1)S(1)}) fusion(bf16[8,128,8,128]{3,2,1,0:T(8,128)(2,1)} %phi.1), kind=kLoop, calls=%fused_computation.17 | loop fusion | bytes 1048576 | tf_op jit(solution)/shard_map/slice | solution.py:206
  28.6 4.9 %collective-permute-start.1 = (bf16[8,128,1,128]{3,2,1,0:T(2,128)(2,1)S(1)}, bf16[8,128,1,128]{3,2,1,0:T(2,128)(2,1)S(1)}, u32[]{:S(2)}, u32[]{:S(2)}) collective-permute-start(bf16[8,128,1,128]{3,2,1,0:T(2,128)(2,1)S(1)} %get-tuple-element.69), channel_id=1, source_target_pairs={{0,3},{1,0},{2,1},{3,2},{4,7},{5,4},{6,5},{7,6},{8,11},{9,8},{10,9... | collective-permute-start | bytes 786440 | tf_op jit(solution)/shard_map/ppermute | solution.py:206
  33.6 1.9 collective-permute-start
  35.5 11.9 %all_gather.3 = f32[4,8,128]{2,1,0:T(8,128)S(1)} all-gather(f32[1,8,128]{2,1,0:T(8,128)S(1)} %copy-done.6), channel_id=1, replica_groups=mesh['z'=16,'x'=4,'c'=2,'y'=4] {'x'}, dimensions={0}, use_global_device_ids=true | all-gather | bytes 20480 | tf_op jit(solution)/shard_map/all_gather | solution.py:204
  47.5 0.8 copy-done.1
  48.3 2.1 collective-permute-done.below
  50.4 0.8 copy-done.3
  51.2 3.4 %collective-permute-start.6 = (f32[4,8,128]{2,1,0:T(8,128)S(1)}, f32[4,8,128]{2,1,0:T(8,128)S(1)}, u32[]{:S(2)}, u32[]{:S(2)}) collective-permute-start(f32[4,8,128]{2,1,0:T(8,128)S(1)} %all_gather.3), channel_id=1, source_target_pairs={{0,32},{32,64},{64,96},{96,128},{128,160},{160,192},{192,224},{224... | collective-permute-start | bytes 49160 | tf_op jit(solution)/shard_map/ppermute | solution.py:208
  54.6 7.5 %collective-permute-start.5 = (f32[4,8,128]{2,1,0:T(8,128)S(1)}, f32[4,8,128]{2,1,0:T(8,128)S(1)}, u32[]{:S(2)}, u32[]{:S(2)}) collective-permute-start(f32[4,8,128]{2,1,0:T(8,128)S(1)} %all_gather.3), channel_id=1, source_target_pairs={{0,128},{32,160},{64,192},{96,224},{128,256},{160,288},{192,320},{... | collective-permute-start | bytes 49160 | tf_op jit(solution)/shard_map/ppermute | solution.py:208
  62.0 6.8 %collective-permute-start.4 = (f32[4,8,128]{2,1,0:T(8,128)S(1)}, f32[4,8,128]{2,1,0:T(8,128)S(1)}, u32[]{:S(2)}, u32[]{:S(2)}) collective-permute-start(f32[4,8,128]{2,1,0:T(8,128)S(1)} %all_gather.3), channel_id=1, source_target_pairs={{0,224},{32,256},{64,288},{96,320},{128,352},{160,384},{192,416},{... | collective-permute-start | bytes 49160 | tf_op jit(solution)/shard_map/ppermute | solution.py:208
  68.8 6.9 %collective-permute-start.3 = (f32[4,8,128]{2,1,0:T(8,128)S(1)}, f32[4,8,128]{2,1,0:T(8,128)S(1)}, u32[]{:S(2)}, u32[]{:S(2)}) collective-permute-start(f32[4,8,128]{2,1,0:T(8,128)S(1)} %all_gather.3), channel_id=1, source_target_pairs={{0,320},{32,352},{64,384},{96,416},{128,448},{160,480},{192,0},{22... | collective-permute-start | bytes 49160 | tf_op jit(solution)/shard_map/ppermute | solution.py:208
  75.8 2.3 %collective-permute-start.2 = (f32[4,8,128]{2,1,0:T(8,128)S(1)}, f32[4,8,128]{2,1,0:T(8,128)S(1)}, u32[]{:S(2)}, u32[]{:S(2)}) collective-permute-start(f32[4,8,128]{2,1,0:T(8,128)S(1)} %all_gather.3), channel_id=1, source_target_pairs={{0,416},{32,448},{64,480},{96,0},{128,32},{160,64},{192,96},{224,1... | collective-permute-start | bytes 49160 | tf_op jit(solution)/shard_map/ppermute | solution.py:208
  78.1 42.3 %collective-permute-done.6 = f32[4,8,128]{2,1,0:T(8,128)S(1)} collective-permute-done((f32[4,8,128]{2,1,0:T(8,128)S(1)}, f32[4,8,128]{2,1,0:T(8,128)S(1)}, u32[]{:S(2)}, u32[]{:S(2)}) %collective-permute-start.6) | collective-permute-done | bytes 16416 | tf_op jit(solution)/shard_map/ppermute | solution.py:208
  120.4 0.3 collective-permute-done.5
  120.7 6.0 %collective-permute-done.4 = f32[4,8,128]{2,1,0:T(8,128)S(1)} collective-permute-done((f32[4,8,128]{2,1,0:T(8,128)S(1)}, f32[4,8,128]{2,1,0:T(8,128)S(1)}, u32[]{:S(2)}, u32[]{:S(2)}) %collective-permute-start.4) | collective-permute-done | bytes 16416 | tf_op jit(solution)/shard_map/ppermute | solution.py:208
  126.8 0.8 slice_bitcast_fusion
  127.6 1.7 fusion
  129.3 1.9 collective-permute-start.9
  131.2 2.4 %collective-permute-start.10 = (bf16[128,4,8,128]{3,2,1,0:T(8,128)(2,1)}, bf16[128,4,8,128]{3,2,1,0:T(8,128)(2,1)}, u32[]{:S(2)}, u32[]{:S(2)}) collective-permute-start(bf16[128,4,8,128]{3,2,1,0:T(8,128)(2,1)} %get-tuple-element.44), channel_id=1, source_target_pairs={{0,4},{4,8},{8,12},{12,16},{16,20},{20,24},{24,28},{28,32},{32,36}... | collective-permute-start | bytes 3145736 | tf_op jit(solution)/shard_map/ppermute | solution.py:213
  133.6 4.9 %collective-permute-start.7 = (bf16[128,8,128]{2,1,0:T(8,128)(2,1)}, bf16[128,8,128]{2,1,0:T(8,128)(2,1)S(1)}, u32[]{:S(2)}, u32[]{:S(2)}) collective-permute-start(bf16[128,8,128]{2,1,0:T(8,128)(2,1)} %slice_bitcast_fusion), channel_id=1, source_target_pairs={{0,3},{1,0},{2,1},{3,2},{4,7},{5,4},{6,5},{7,6},{8,11},{9,8},{10,9... | collective-permute-start | bytes 786440 | tf_op jit(solution)/shard_map/ppermute | solution.py:214
  138.6 0.1 copy.22
  138.7 0.1 reshape.19.pairs
  138.8 0.1 pad_add_fusion.where
  138.9 5.4 %collective-permute-done.7.above = bf16[128,8,128]{2,1,0:T(8,128)(2,1)S(1)} collective-permute-done((bf16[128,8,128]{2,1,0:T(8,128)(2,1)}, bf16[128,8,128]{2,1,0:T(8,128)(2,1)S(1)}, u32[]{:S(2)}, u32[]{:S(2)}) %collective-permute-start.7) | collective-permute-done | bytes 262176 | tf_op jit(solution)/shard_map/ppermute | solution.py:214
  144.3 4.8 %overlap_products.1 = (bf16[1024,1024]{1,0:T(8,128)(2,1)S(1)}, f32[4,4,8,16,128]{4,3,2,1,0:T(8,128)S(1)}, f32[4,4,8,16,128]{4,3,2,1,0:T(8,128)S(1)}) custom-call(s32[64]{0:T(128)S(1)} %reshape.19.pairs, s32[1024]{0:T(1024)S(1)} %bitcast.35, s32[3]{0:T(128)S(1)} %pad_add_fusion.where, bf16[128,8,8,128]{3,2,1,0:T(8,128)(2,1)S(1)} %all-to-all-done.own), custom_call_target="tpu_custom_call" | custom-call | tf_op jit(solution)/shard_map/overlap_products/pallas_call | solution.py:124
  149.1 3.3 %collective-permute-start.8 = (f32[4,4,8,16,128]{4,3,2,1,0:T(8,128)S(1)}, f32[4,4,8,16,128]{4,3,2,1,0:T(8,128)S(1)}, u32[]{:S(2)}, u32[]{:S(2)}) collective-permute-start(f32[4,4,8,16,128]{4,3,2,1,0:T(8,128)S(1)} %get-tuple-element.41), channel_id=1, source_target_pairs={{0,4},{4,0},{1,5},{5,1},{2,6},{6,2},{3,7},{7,3},{8,12},{12,8},{9,1... | collective-permute-start | bytes 3145736 | tf_op jit(solution)/shard_map/ppermute | solution.py:218
  152.4 11.0 %hamiltonian_products.1 = (f32[4,4,8,16,128]{4,3,2,1,0:T(8,128)S(1)}, f32[4,4,8,16,128]{4,3,2,1,0:T(8,128)S(1)}) custom-call(s32[64]{0:T(128)S(1)} %reshape.19.pairs, s32[1024]{0:T(1024)S(1)} %bitcast.36, s32[3]{0:T(128)S(1)} %pad_add_fusion.where, bf16[1024,1024]{1,0:T(8,128)(2,1)S(1)} %get-tuple-element.42.conf, ...), custom_call_target="tpu_custom_call" | custom-call | tf_op jit(solution)/shard_map/hamiltonian_products/pallas_call | solution.py:136
  163.5 1.9 collective-permute-start.11
  165.4 0.1 add_convert_fusion.1
  165.6 2.5 %collective-permute-done.11 = f32[4,4,8,16,128]{4,3,2,1,0:T(8,128)S(1)} collective-permute-done((f32[4,4,8,16,128]{4,3,2,1,0:T(8,128)S(1)}, f32[4,4,8,16,128]{4,3,2,1,0:T(8,128)S(1)}, u32[]{:S(2)}, u32[]{:S(2)}) %collective-permute-start.11) | collective-permute-done | bytes 1048608 | tf_op jit(solution)/shard_map/ppermute | solution.py:221
  168.0 0.1 add_convert_fusion
  168.2 1.1 pad_maximum_fusion
  169.3 8.6 %all-to-all-start.1 = ((bf16[16,2,8,16,128]{4,3,2,1,0:T(8,128)(2,1)}), bf16[16,2,8,16,128]{4,3,2,1,0:T(8,128)(2,1)}, u32[]{:S(2)}, u32[]{:S(2)}) async-start(bf16[16,2,8,16,128]{4,3,2,1,0:T(8,128)(2,1)} %pad_maximum_fusion), calls=%async_computation.1 | async-start | bytes 2097152 | tf_op jit(solution)/shard_map/all_to_all | solution.py:227
  178.0 1.9 collective-permute-start.12
  179.9 1.3 collective-permute-done.12
  181.2 5.2 %collective-permute-start.14 = (f32[2,6,4,8,128]{4,3,2,1,0:T(8,128)S(1)}, f32[2,6,4,8,128]{4,3,2,1,0:T(8,128)S(1)}, u32[]{:S(2)}, u32[]{:S(2)}) collective-permute-start(f32[2,6,4,8,128]{4,3,2,1,0:T(8,128)S(1)} %pad_maximum_fusion.1.pot_mid), channel_id=1, source_target_pairs={{0,480},{32,0},{64,32},{96,64},{128,96},{160,128},{192,160},{224,1... | collective-permute-start | bytes 589832 | tf_op jit(solution)/shard_map/ppermute | solution.py:226
  186.4 1.9 collective-permute-start.13
  188.3 5.4 %all-to-all-done.1 = bf16[16,2,8,16,128]{4,3,2,1,0:T(8,128)(2,1)} async-done(((bf16[16,2,8,16,128]{4,3,2,1,0:T(8,128)(2,1)}), bf16[16,2,8,16,128]{4,3,2,1,0:T(8,128)(2,1)}, u32[]{:S(2)}, u32[]{:S(2)}) %all-to-all-start.1) | async-done | bytes 1048608 | tf_op jit(solution)/shard_map/all_to_all | solution.py:227
  193.7 1.4 convert_reduce_fusion
  195.1 1.2 collective-permute-done.13.pot_low
  196.2 0.7 copy.27
  196.9 4.2 %all-to-all-start.2 = ((f32[16,2,8,128]{3,2,1,0:T(8,128)}), f32[16,2,8,128]{3,2,1,0:T(8,128)}, u32[]{:S(2)}, u32[]{:S(2)}) async-start(f32[16,2,8,128]{3,2,1,0:T(8,128)} %copy.27), calls=%async_computation.2 | async-start | bytes 262144 | tf_op jit(solution)/shard_map/all_to_all | solution.py:231
  201.1 14.0 %orbital_apply.1 = bf16[8,128,8,128]{3,2,1,0:T(8,128)(2,1)} custom-call(s32[1024]{0:T(1024)S(1)} %bitcast.37, s32[3]{0:T(128)S(1)} %pad_add_fusion.where, bf16[8,128,8,128]{3,2,1,0:T(8,128)(2,1)S(1)} %copy-done, bf16[8,128,1,128]{3,2,1,0:T(2,128)(2,1)S(1)} %copy-done.4, bf16[8,128,1,128]{3,2,1,0:T(2,128)(2,1)S(1)} %copy-done.2, ...), custom_call_target="tpu_custom_call" | custom-call | tf_op jit(solution)/shard_map/orbital_apply/pallas_call | solution.py:180
  215.1 0.0 all-to-all-done.2
  215.1 0.9 reduce_sum.19
  216.0 0.6 slice_bitcast_fusion.1
  (29 shorter events, 0.1 us)
Async XLA Ops:
  6.0 120.8 %all-to-all-start = ((bf16[128,8,8,128]{3,2,1,0:T(8,128)(2,1)}), bf16[128,8,8,128]{3,2,1,0:T(8,128)(2,1)S(1)}, u32[]{:S(2)}, u32[]{:S(2)}) async-start(bf16[128,8,8,128]{3,2,1,0:T(8,128)(2,1)} %bitcast.39), calls=%async_computation | async-start | bytes 4194304 | tf_op jit(solution)/shard_map/all_to_all | solution.py:202
  25.3 10.2 %copy-start.6 = (f32[1,8,128]{2,1,0:T(8,128)S(1)}, f32[1,8,128]{2,1,0:T(8,128)}, u32[]{:S(2)}) copy-start(f32[1,8,128]{2,1,0:T(8,128)} %param.5) | copy-start | bytes 12292
  28.6 18.8 %collective-permute-start.1 = (bf16[8,128,1,128]{3,2,1,0:T(2,128)(2,1)S(1)}, bf16[8,128,1,128]{3,2,1,0:T(2,128)(2,1)S(1)}, u32[]{:S(2)}, u32[]{:S(2)}) collective-permute-start(bf16[8,128,1,128]{3,2,1,0:T(2,128)(2,1)S(1)} %get-tuple-element.69), channel_id=1, source_target_pairs={{0,3},{1,0},{2,1},{3,2},{4,7},{5,4},{6,5},{7,6},{8,11},{9,8},{10,9... | collective-permute-start | bytes 786440 | tf_op jit(solution)/shard_map/ppermute | solution.py:206
  33.6 16.8 %collective-permute-start = (bf16[8,128,1,128]{3,2,1,0:T(2,128)(2,1)S(1)}, bf16[8,128,1,128]{3,2,1,0:T(2,128)(2,1)S(1)}, u32[]{:S(2)}, u32[]{:S(2)}) collective-permute-start(bf16[8,128,1,128]{3,2,1,0:T(2,128)(2,1)S(1)} %get-tuple-element.70), channel_id=1, source_target_pairs={{0,1},{1,2},{2,3},{3,0},{4,5},{5,6},{6,7},{7,4},{8,9},{9,10},{10,1... | collective-permute-start | bytes 786440 | tf_op jit(solution)/shard_map/ppermute | solution.py:205
  47.5 0.8 copy-start.1
  50.4 0.8 copy-start.3
  51.2 69.2 %collective-permute-start.6 = (f32[4,8,128]{2,1,0:T(8,128)S(1)}, f32[4,8,128]{2,1,0:T(8,128)S(1)}, u32[]{:S(2)}, u32[]{:S(2)}) collective-permute-start(f32[4,8,128]{2,1,0:T(8,128)S(1)} %all_gather.3), channel_id=1, source_target_pairs={{0,32},{32,64},{64,96},{96,128},{128,160},{160,192},{192,224},{224... | collective-permute-start | bytes 49160 | tf_op jit(solution)/shard_map/ppermute | solution.py:208
  54.6 66.2 %collective-permute-start.5 = (f32[4,8,128]{2,1,0:T(8,128)S(1)}, f32[4,8,128]{2,1,0:T(8,128)S(1)}, u32[]{:S(2)}, u32[]{:S(2)}) collective-permute-start(f32[4,8,128]{2,1,0:T(8,128)S(1)} %all_gather.3), channel_id=1, source_target_pairs={{0,128},{32,160},{64,192},{96,224},{128,256},{160,288},{192,320},{... | collective-permute-start | bytes 49160 | tf_op jit(solution)/shard_map/ppermute | solution.py:208
  62.0 64.7 %collective-permute-start.4 = (f32[4,8,128]{2,1,0:T(8,128)S(1)}, f32[4,8,128]{2,1,0:T(8,128)S(1)}, u32[]{:S(2)}, u32[]{:S(2)}) collective-permute-start(f32[4,8,128]{2,1,0:T(8,128)S(1)} %all_gather.3), channel_id=1, source_target_pairs={{0,224},{32,256},{64,288},{96,320},{128,352},{160,384},{192,416},{... | collective-permute-start | bytes 49160 | tf_op jit(solution)/shard_map/ppermute | solution.py:208
  68.8 58.0 %collective-permute-start.3 = (f32[4,8,128]{2,1,0:T(8,128)S(1)}, f32[4,8,128]{2,1,0:T(8,128)S(1)}, u32[]{:S(2)}, u32[]{:S(2)}) collective-permute-start(f32[4,8,128]{2,1,0:T(8,128)S(1)} %all_gather.3), channel_id=1, source_target_pairs={{0,320},{32,352},{64,384},{96,416},{128,448},{160,480},{192,0},{22... | collective-permute-start | bytes 49160 | tf_op jit(solution)/shard_map/ppermute | solution.py:208
  75.8 51.0 %collective-permute-start.2 = (f32[4,8,128]{2,1,0:T(8,128)S(1)}, f32[4,8,128]{2,1,0:T(8,128)S(1)}, u32[]{:S(2)}, u32[]{:S(2)}) collective-permute-start(f32[4,8,128]{2,1,0:T(8,128)S(1)} %all_gather.3), channel_id=1, source_target_pairs={{0,416},{32,448},{64,480},{96,0},{128,32},{160,64},{192,96},{224,1... | collective-permute-start | bytes 49160 | tf_op jit(solution)/shard_map/ppermute | solution.py:208
  127.6 11.0 %copy-start.7 = (s32[32,2]{0,1:T(2,128)S(1)}, s32[32,2]{0,1:T(2,128)}, u32[]{:S(2)}) copy-start(s32[32,2]{0,1:T(2,128)} %param.6) | copy-start | bytes 772
  127.6 16.7 %copy-start.5 = (s32[8,128]{1,0:T(8,128)S(1)}, s32[8,128]{1,0:T(8,128)}, u32[]{:S(2)}) copy-start(s32[8,128]{1,0:T(8,128)} %param.7) | copy-start | bytes 12292
  129.3 23.1 %collective-permute-start.9 = (bf16[128,4,8,128]{3,2,1,0:T(8,128)(2,1)}, bf16[128,4,8,128]{3,2,1,0:T(8,128)(2,1)S(1)}, u32[]{:S(2)}, u32[]{:S(2)}) collective-permute-start(bf16[128,4,8,128]{3,2,1,0:T(8,128)(2,1)} %get-tuple-element.43), channel_id=1, source_target_pairs={{0,508},{4,0},{8,4},{12,8},{16,12},{20,16},{24,20},{28,24},{32,28}... | collective-permute-start | bytes 3145736 | tf_op jit(solution)/shard_map/ppermute | solution.py:212
  131.2 21.2 %collective-permute-start.10 = (bf16[128,4,8,128]{3,2,1,0:T(8,128)(2,1)}, bf16[128,4,8,128]{3,2,1,0:T(8,128)(2,1)}, u32[]{:S(2)}, u32[]{:S(2)}) collective-permute-start(bf16[128,4,8,128]{3,2,1,0:T(8,128)(2,1)} %get-tuple-element.44), channel_id=1, source_target_pairs={{0,4},{4,8},{8,12},{12,16},{16,20},{20,24},{24,28},{28,32},{32,36}... | collective-permute-start | bytes 3145736 | tf_op jit(solution)/shard_map/ppermute | solution.py:213
  133.6 10.6 %collective-permute-start.7 = (bf16[128,8,128]{2,1,0:T(8,128)(2,1)}, bf16[128,8,128]{2,1,0:T(8,128)(2,1)S(1)}, u32[]{:S(2)}, u32[]{:S(2)}) collective-permute-start(bf16[128,8,128]{2,1,0:T(8,128)(2,1)} %slice_bitcast_fusion), channel_id=1, source_target_pairs={{0,3},{1,0},{2,1},{3,2},{4,7},{5,4},{6,5},{7,6},{8,11},{9,8},{10,9... | collective-permute-start | bytes 786440 | tf_op jit(solution)/shard_map/ppermute | solution.py:214
  149.1 16.3 %collective-permute-start.8 = (f32[4,4,8,16,128]{4,3,2,1,0:T(8,128)S(1)}, f32[4,4,8,16,128]{4,3,2,1,0:T(8,128)S(1)}, u32[]{:S(2)}, u32[]{:S(2)}) collective-permute-start(f32[4,4,8,16,128]{4,3,2,1,0:T(8,128)S(1)} %get-tuple-element.41), channel_id=1, source_target_pairs={{0,4},{4,0},{1,5},{5,1},{2,6},{6,2},{3,7},{7,3},{8,12},{12,8},{9,1... | collective-permute-start | bytes 3145736 | tf_op jit(solution)/shard_map/ppermute | solution.py:218
  163.5 4.6 %collective-permute-start.11 = (f32[4,4,8,16,128]{4,3,2,1,0:T(8,128)S(1)}, f32[4,4,8,16,128]{4,3,2,1,0:T(8,128)S(1)}, u32[]{:S(2)}, u32[]{:S(2)}) collective-permute-start(f32[4,4,8,16,128]{4,3,2,1,0:T(8,128)S(1)} %get-tuple-element.47), channel_id=1, source_target_pairs={{0,4},{4,0},{1,5},{5,1},{2,6},{6,2},{3,7},{7,3},{8,12},{12,8},{9,1... | collective-permute-start | bytes 3145736 | tf_op jit(solution)/shard_map/ppermute | solution.py:221
  169.2 31.9 %copy-start = (bf16[8,128,8,128]{3,2,1,0:T(8,128)(2,1)S(1)}, bf16[8,128,8,128]{3,2,1,0:T(8,128)(2,1)}, u32[]{:S(2)}) copy-start(bf16[8,128,8,128]{3,2,1,0:T(8,128)(2,1)} %phi.1) | copy-start | bytes 6291460
  169.3 31.9 %copy-start.2 = (bf16[8,128,1,128]{3,2,1,0:T(2,128)(2,1)S(1)}, bf16[8,128,1,128]{3,2,1,0:T(2,128)(2,1)}, u32[]{:S(2)}) copy-start(bf16[8,128,1,128]{3,2,1,0:T(2,128)(2,1)} %copy-done.1) | copy-start | bytes 786436
  169.3 31.9 %copy-start.4 = (bf16[8,128,1,128]{3,2,1,0:T(2,128)(2,1)S(1)}, bf16[8,128,1,128]{3,2,1,0:T(2,128)(2,1)}, u32[]{:S(2)}) copy-start(bf16[8,128,1,128]{3,2,1,0:T(2,128)(2,1)} %copy-done.3) | copy-start | bytes 786436
  169.3 24.4 %all-to-all-start.1 = ((bf16[16,2,8,16,128]{4,3,2,1,0:T(8,128)(2,1)}), bf16[16,2,8,16,128]{4,3,2,1,0:T(8,128)(2,1)}, u32[]{:S(2)}, u32[]{:S(2)}) async-start(bf16[16,2,8,16,128]{4,3,2,1,0:T(8,128)(2,1)} %pad_maximum_fusion), calls=%async_computation.1 | async-start | bytes 2097152 | tf_op jit(solution)/shard_map/all_to_all | solution.py:227
  178.0 3.2 %collective-permute-start.12 = (f32[6,4,8,128]{3,2,1,0:T(8,128)S(1)}, f32[6,4,8,128]{3,2,1,0:T(8,128)S(1)}, u32[]{:S(2)}, u32[]{:S(2)}) collective-permute-start(f32[6,4,8,128]{3,2,1,0:T(8,128)S(1)} %bitcast_dynamic-update-slice_fusion), channel_id=1, source_target_pairs={{0,4},{4,0},{1,5},{5,1},{2,6},{6,2},{3,7},{7,3},{8,12},{12,8},{9,1... | collective-permute-start | bytes 294920 | tf_op jit(solution)/shard_map/ppermute | solution.py:225
  181.2 13.9 %collective-permute-start.14 = (f32[2,6,4,8,128]{4,3,2,1,0:T(8,128)S(1)}, f32[2,6,4,8,128]{4,3,2,1,0:T(8,128)S(1)}, u32[]{:S(2)}, u32[]{:S(2)}) collective-permute-start(f32[2,6,4,8,128]{4,3,2,1,0:T(8,128)S(1)} %pad_maximum_fusion.1.pot_mid), channel_id=1, source_target_pairs={{0,480},{32,0},{64,32},{96,64},{128,96},{160,128},{192,160},{224,1... | collective-permute-start | bytes 589832 | tf_op jit(solution)/shard_map/ppermute | solution.py:226
  186.4 9.9 %collective-permute-start.13 = (f32[2,6,4,8,128]{4,3,2,1,0:T(8,128)S(1)}, f32[2,6,4,8,128]{4,3,2,1,0:T(8,128)}, u32[]{:S(2)}, u32[]{:S(2)}) collective-permute-start(f32[2,6,4,8,128]{4,3,2,1,0:T(8,128)S(1)} %pad_maximum_fusion.1.pot_mid), channel_id=1, source_target_pairs={{0,32},{32,64},{64,96},{96,128},{128,160},{160,192},{192,224},{224... | collective-permute-start | bytes 589832 | tf_op jit(solution)/shard_map/ppermute | solution.py:226
  196.9 18.2 %all-to-all-start.2 = ((f32[16,2,8,128]{3,2,1,0:T(8,128)}), f32[16,2,8,128]{3,2,1,0:T(8,128)}, u32[]{:S(2)}, u32[]{:S(2)}) async-start(f32[16,2,8,128]{3,2,1,0:T(8,128)} %copy.27), calls=%async_computation.2 | async-start | bytes 262144 | tf_op jit(solution)/shard_map/all_to_all | solution.py:231

commit v7 on v6

--- a/solution.py
+++ b/solution.py
@@ -42,13 +42,13 @@
 
 
 def gram_blocks(left, right, gram):
-    @pl.loop(0, NB // 2)
+    @pl.loop(0, NB // 4)
     def _(n):
-        cols = pl.ds(pl.multiple_of(n * 2 * W, 2 * W), 2 * W)
+        cols = pl.ds(pl.multiple_of(n * 4 * W, 4 * W), 4 * W)
         product = lax.dot_general(left[...], right[cols, :], (((1,), (1,)), ((), ())),
                                   preferred_element_type=F32)
-        gram[2 * n] = product[:, 0:W]
-        gram[2 * n + 1] = product[:, W:]
+        for part in range(4):
+            gram[4 * n + part] = product[:, part * W : (part + 1) * W]
 
 
 def overlap_kernel(pairs, support, where, own, conf, mine, theirs, gram):
@@ -128,6 +128,7 @@
         out_specs=(VMEM,) * 3,
         scratch_shapes=[pltpu.VMEM((NB, NB * W, W), F32)],
         compiler_params=pltpu.CompilerParams(vmem_limit_bytes=16 << 20),
+        cost_estimate=pl.CostEstimate(flops=2 * 10**9, transcendentals=0, bytes_accessed=8 << 20),
         name="overlap_products",
     )(pair_flat, support_flat, where, own)
 
@@ -144,6 +145,7 @@
             pltpu.VMEM((NB, NB * W, W), F32),
         ],
         compiler_params=pltpu.CompilerParams(vmem_limit_bytes=26 << 20),
+        cost_estimate=pl.CostEstimate(flops=5 * 10**9, transcendentals=0, bytes_accessed=8 << 20),
         name="hamiltonian_products",
     )(pair_flat, support_flat, where, conf, ahead, behind, above, pot)
 
@@ -212,7 +214,6 @@
     ahead = lax.ppermute(low_half, REGION, ring(PLANES, -1))
     behind = lax.ppermute(high_half, REGION, ring(PLANES, 1))
     above = lax.ppermute(edge, "y", ring(YD, -1))
-    own, above = lax.optimization_barrier((own, above))
     conf, mine_s, theirs_s = overlap_products(pair_flat, support_flat, where, own)
     swap = [(0, 1), (1, 0)]
     total_s = mine_s + lax.ppermute(theirs_s, "c", swap)

time: 219 us -> 220 us (level)
  starting transfers between devices: 89.4 us -> 93.2 us
  local copies, waits for them, and re-layouts: 14.3 us -> 12.1 us
    ppermute x1, waiting for transfers between devices: 5.38 us -> 0.01 us  [local(): above = lax.ppermute(edge, 'y', ring(YD, -1))]
    all_to_all x1, starting transfers between devices: 8.64 us -> 12.6 us  [local(): lax.all_to_all(total, ('x', 'y'), split_axis=0, concat_axis=0, tiled=True)]
    ppermute x1, starting transfers between devices: 5.18 us -> 2.14 us  [local(): lax.ppermute(column, 'z', ring(ZD, -1))]
    ppermute x5, waiting for transfers between devices: 48.7 us -> 51.4 us  [local(): lax.ppermute(planes, 'z', ring(ZD, -s))]
    slice x1, local copies, waits for them, and re-layouts: 3.27 us -> 0.94 us  [local(): row_above = lax.ppermute(phi[:, :, :1], 'y', ring(YD, -1))]
    unnamed x23 -> x15, local copies, waits for them, and re-layouts: 7.09 us -> 5.47 us
  transfers between devices with their start and end apart: 18 -> 18, of which waited for: 9 -> 7; matrix products, arithmetic and copies ran while one was open for 2% -> 1% of each run, Pallas kernels for 14% -> 14%
where the time goes in v7:
time: 220 us; the launch traced here: 217 us
  starting transfers between devices  93.2 us (42%)
  waiting for transfers between devices  64.7 us (29%)
  Pallas kernels  30.3 us (14%)
  local copies, waits for them, and re-layouts  12.1 us (6%)
  blocking collectives  12 us (5%)
  other arithmetic  3.76 us (2%)
    ppermute x5, waiting for transfers between devices, local(): lax.ppermute(planes, 'z', ring(ZD, -s))  51.4 us
    ppermute x5, starting transfers between devices, local(): lax.ppermute(planes, 'z', ring(ZD, -s))  26.9 us
    all_to_all x1, starting transfers between devices, local(): lax.all_to_all(phi.transpose(1, 2, 0, 3), REGION, split_axis=0, concat_ax...  20 us
    pallas_call x1, Pallas kernels, orbital_apply(): pl.pallas_call(orbital_kernel, out_shape=jax.ShapeDtypeStruct(phi.shape,...  14 us
    all_to_all x1, starting transfers between devices, local(): lax.all_to_all(total, ('x', 'y'), split_axis=0, concat_axis=0, tiled=True)  12.6 us
    all_gather x1, blocking collectives, local(): planes = lax.all_gather(potential, 'x', axis=0, tiled=True)  12 us
    pallas_call x1, Pallas kernels, hamiltonian_products(): pl.pallas_call(hamiltonian_kernel, out_shape=(SHARE, SHARE), in_specs=[SM...  10.9 us
    all_to_all x1, waiting for transfers between devices, local(): lax.all_to_all(total, ('x', 'y'), split_axis=0, concat_axis=0, tiled=True)  6.63 us
  transfers between devices with their start and end apart: 18, of which 7 were waited for; matrix products, arithmetic and copies ran while one was open for 1% of the time, Pallas kernels for 14%

profile of v7, /device:TPU:6, one launch (start us, length us, event | category | flops | bytes accessed | tf_op | source)
XLA Modules:
  0.0 216.9 jit_solution(1565872954915778480)
XLA Ops:
  0.6 5.3 %copy.31 = bf16[8,128,8,128]{3,0,2,1:T(8,128)(2,1)} copy(bf16[8,128,8,128]{3,2,1,0:T(8,128)(2,1)} %phi.1) | data formatting | bytes 4194304 | tf_op args[0]
  6.0 20.0 %all-to-all-start = ((bf16[128,8,8,128]{3,2,1,0:T(8,128)(2,1)}), bf16[128,8,8,128]{3,2,1,0:T(8,128)(2,1)}, u32[]{:S(2)}, u32[]{:S(2)}) async-start(bf16[128,8,8,128]{3,2,1,0:T(8,128)(2,1)} %bitcast.39), calls=%async_computation | async-start | bytes 4194304 | tf_op jit(solution)/shard_map/all_to_all | solution.py:204
  26.0 0.0 copy-start.1
  26.0 0.9 fusion.1
  26.9 4.9 %collective-permute-start.1 = (bf16[8,128,1,128]{3,2,1,0:T(2,128)(2,1)S(1)}, bf16[8,128,1,128]{3,2,1,0:T(2,128)(2,1)S(1)}, u32[]{:S(2)}, u32[]{:S(2)}) collective-permute-start(bf16[8,128,1,128]{3,2,1,0:T(2,128)(2,1)S(1)} %get-tuple-element.65), channel_id=1, source_target_pairs={{0,3},{1,0},{2,1},{3,2},{4,7},{5,4},{6,5},{7,6},{8,11},{9,8},{10,9... | collective-permute-start | bytes 786440 | tf_op jit(solution)/shard_map/ppermute | solution.py:208
  31.8 1.9 collective-permute-start
  33.8 12.0 %all_gather.3 = f32[4,8,128]{2,1,0:T(8,128)S(1)} all-gather(f32[1,8,128]{2,1,0:T(8,128)S(1)} %copy-done.1), channel_id=1, replica_groups=mesh['z'=16,'x'=4,'c'=2,'y'=4] {'x'}, dimensions={0}, use_global_device_ids=true | all-gather | bytes 20480 | tf_op jit(solution)/shard_map/all_gather | solution.py:206
  45.7 0.0 collective-permute-done.1.above
  45.7 2.9 %collective-permute-done.below = bf16[8,128,1,128]{3,2,1,0:T(2,128)(2,1)S(1)} collective-permute-done((bf16[8,128,1,128]{3,2,1,0:T(2,128)(2,1)S(1)}, bf16[8,128,1,128]{3,2,1,0:T(2,128)(2,1)S(1)}, u32[]{:S(2)}, u32[]{:S(2)}) %collective-permute-start) | collective-permute-done | bytes 262176 | tf_op jit(solution)/shard_map/ppermute | solution.py:207
  48.6 3.4 %collective-permute-start.6 = (f32[4,8,128]{2,1,0:T(8,128)S(1)}, f32[4,8,128]{2,1,0:T(8,128)S(1)}, u32[]{:S(2)}, u32[]{:S(2)}) collective-permute-start(f32[4,8,128]{2,1,0:T(8,128)S(1)} %all_gather.3), channel_id=1, source_target_pairs={{0,32},{32,64},{64,96},{96,128},{128,160},{160,192},{192,224},{224... | collective-permute-start | bytes 49160 | tf_op jit(solution)/shard_map/ppermute | solution.py:210
  52.0 7.5 %collective-permute-start.5 = (f32[4,8,128]{2,1,0:T(8,128)S(1)}, f32[4,8,128]{2,1,0:T(8,128)S(1)}, u32[]{:S(2)}, u32[]{:S(2)}) collective-permute-start(f32[4,8,128]{2,1,0:T(8,128)S(1)} %all_gather.3), channel_id=1, source_target_pairs={{0,128},{32,160},{64,192},{96,224},{128,256},{160,288},{192,320},{... | collective-permute-start | bytes 49160 | tf_op jit(solution)/shard_map/ppermute | solution.py:210
  59.5 6.8 %collective-permute-start.4 = (f32[4,8,128]{2,1,0:T(8,128)S(1)}, f32[4,8,128]{2,1,0:T(8,128)S(1)}, u32[]{:S(2)}, u32[]{:S(2)}) collective-permute-start(f32[4,8,128]{2,1,0:T(8,128)S(1)} %all_gather.3), channel_id=1, source_target_pairs={{0,224},{32,256},{64,288},{96,320},{128,352},{160,384},{192,416},{... | collective-permute-start | bytes 49160 | tf_op jit(solution)/shard_map/ppermute | solution.py:210
  66.3 6.9 %collective-permute-start.3 = (f32[4,8,128]{2,1,0:T(8,128)S(1)}, f32[4,8,128]{2,1,0:T(8,128)S(1)}, u32[]{:S(2)}, u32[]{:S(2)}) collective-permute-start(f32[4,8,128]{2,1,0:T(8,128)S(1)} %all_gather.3), channel_id=1, source_target_pairs={{0,320},{32,352},{64,384},{96,416},{128,448},{160,480},{192,0},{22... | collective-permute-start | bytes 49160 | tf_op jit(solution)/shard_map/ppermute | solution.py:210
  73.2 2.3 %collective-permute-start.2 = (f32[4,8,128]{2,1,0:T(8,128)S(1)}, f32[4,8,128]{2,1,0:T(8,128)S(1)}, u32[]{:S(2)}, u32[]{:S(2)}) collective-permute-start(f32[4,8,128]{2,1,0:T(8,128)S(1)} %all_gather.3), channel_id=1, source_target_pairs={{0,416},{32,448},{64,480},{96,0},{128,32},{160,64},{192,96},{224,1... | collective-permute-start | bytes 49160 | tf_op jit(solution)/shard_map/ppermute | solution.py:210
  75.5 45.0 %collective-permute-done.6 = f32[4,8,128]{2,1,0:T(8,128)S(1)} collective-permute-done((f32[4,8,128]{2,1,0:T(8,128)S(1)}, f32[4,8,128]{2,1,0:T(8,128)S(1)}, u32[]{:S(2)}, u32[]{:S(2)}) %collective-permute-start.6) | collective-permute-done | bytes 16416 | tf_op jit(solution)/shard_map/ppermute | solution.py:210
  120.5 0.3 collective-permute-done.5
  120.9 6.0 %collective-permute-done.4 = f32[4,8,128]{2,1,0:T(8,128)S(1)} collective-permute-done((f32[4,8,128]{2,1,0:T(8,128)S(1)}, f32[4,8,128]{2,1,0:T(8,128)S(1)}, u32[]{:S(2)}, u32[]{:S(2)}) %collective-permute-start.4) | collective-permute-done | bytes 16416 | tf_op jit(solution)/shard_map/ppermute | solution.py:210
  126.9 0.0 collective-permute-done.3
  126.9 1.0 slice_bitcast_fusion
  127.9 0.0 copy-start.3
  127.9 0.0 copy-start.2
  127.9 3.3 %fusion = (bf16[128,4,8,128]{3,2,1,0:T(8,128)(2,1)}, bf16[128,4,8,128]{3,2,1,0:T(8,128)(2,1)}) fusion(bf16[128,8,8,128]{3,2,1,0:T(8,128)(2,1)} %all-to-all-done.own), kind=kLoop, calls=%fused_computation.16 | loop fusion | bytes 4194304 | tf_op jit(solution)/shard_map/slice | solution.py:213
  131.2 1.9 collective-permute-start.8
  133.1 2.4 %collective-permute-start.9 = (bf16[128,4,8,128]{3,2,1,0:T(8,128)(2,1)}, bf16[128,4,8,128]{3,2,1,0:T(8,128)(2,1)}, u32[]{:S(2)}, u32[]{:S(2)}) collective-permute-start(bf16[128,4,8,128]{3,2,1,0:T(8,128)(2,1)} %get-tuple-element.40), channel_id=1, source_target_pairs={{0,4},{4,8},{8,12},{12,16},{16,20},{20,24},{24,28},{28,32},{32,36}... | collective-permute-start | bytes 3145736 | tf_op jit(solution)/shard_map/ppermute | solution.py:215
  135.5 0.1 copy.22
  135.6 0.1 reshape.19.pairs
  135.8 4.9 %collective-permute-start.10 = (bf16[128,8,128]{2,1,0:T(8,128)(2,1)S(1)}, bf16[128,8,128]{2,1,0:T(8,128)(2,1)S(1)}, u32[]{:S(2)}, u32[]{:S(2)}) collective-permute-start(bf16[128,8,128]{2,1,0:T(8,128)(2,1)S(1)} %slice_bitcast_fusion), channel_id=1, source_target_pairs={{0,3},{1,0},{2,1},{3,2},{4,7},{5,4},{6,5},{7,6},{8,11},{9,8},{10,9... | collective-permute-start | bytes 786440 | tf_op jit(solution)/shard_map/ppermute | solution.py:216
  140.7 0.1 pad_add_fusion.where
  140.8 5.4 %overlap_products.1 = (bf16[1024,1024]{1,0:T(8,128)(2,1)S(1)}, f32[4,4,8,16,128]{4,3,2,1,0:T(8,128)S(1)}, f32[4,4,8,16,128]{4,3,2,1,0:T(8,128)S(1)}) custom-call(s32[64]{0:T(128)S(1)} %reshape.19.pairs, s32[1024]{0:T(1024)S(1)} %bitcast.36, s32[3]{0:T(128)S(1)} %pad_add_fusion.where, bf16[128,8,8,128]{3,2,1,0:T(8,128)(2,1)} %all-to-all-done.own), custom_call_target="tpu_custom_call" | custom-call | flops 2000000000 | bytes 8388608 | tf_op jit(solution)/shard_map/overlap_products/pallas_call | solution.py:124
  146.2 3.9 %collective-permute-start.7 = (f32[4,4,8,16,128]{4,3,2,1,0:T(8,128)S(1)}, f32[4,4,8,16,128]{4,3,2,1,0:T(8,128)S(1)}, u32[]{:S(2)}, u32[]{:S(2)}) collective-permute-start(f32[4,4,8,16,128]{4,3,2,1,0:T(8,128)S(1)} %get-tuple-element.37), channel_id=1, source_target_pairs={{0,4},{4,0},{1,5},{5,1},{2,6},{6,2},{3,7},{7,3},{8,12},{12,8},{9,1... | collective-permute-start | bytes 3145736 | tf_op jit(solution)/shard_map/ppermute | solution.py:219
  150.1 10.9 %hamiltonian_products.1 = (f32[4,4,8,16,128]{4,3,2,1,0:T(8,128)S(1)}, f32[4,4,8,16,128]{4,3,2,1,0:T(8,128)S(1)}) custom-call(s32[64]{0:T(128)S(1)} %reshape.19.pairs, s32[1024]{0:T(1024)S(1)} %bitcast.37, s32[3]{0:T(128)S(1)} %pad_add_fusion.where, bf16[1024,1024]{1,0:T(8,128)(2,1)S(1)} %get-tuple-element.38.conf, ...), custom_call_target="tpu_custom_call" | custom-call | flops 5000000000 | bytes 8388608 | tf_op jit(solution)/shard_map/hamiltonian_products/pallas_call | solution.py:137
  161.0 1.9 collective-permute-start.11
  163.0 0.1 add_convert_fusion.1
  163.1 2.5 %collective-permute-done.11 = f32[4,4,8,16,128]{4,3,2,1,0:T(8,128)S(1)} collective-permute-done((f32[4,4,8,16,128]{4,3,2,1,0:T(8,128)S(1)}, f32[4,4,8,16,128]{4,3,2,1,0:T(8,128)S(1)}, u32[]{:S(2)}, u32[]{:S(2)}) %collective-permute-start.11) | collective-permute-done | bytes 1048608 | tf_op jit(solution)/shard_map/ppermute | solution.py:222
  165.6 0.1 add_convert_fusion
  165.7 1.1 pad_maximum_fusion
  166.8 12.6 %all-to-all-start.1 = ((bf16[16,2,8,16,128]{4,3,2,1,0:T(8,128)(2,1)}), bf16[16,2,8,16,128]{4,3,2,1,0:T(8,128)(2,1)}, u32[]{:S(2)}, u32[]{:S(2)}) async-start(bf16[16,2,8,16,128]{4,3,2,1,0:T(8,128)(2,1)} %pad_maximum_fusion), calls=%async_computation.1 | async-start | bytes 2097152 | tf_op jit(solution)/shard_map/all_to_all | solution.py:228
  179.5 1.9 collective-permute-start.12
  181.4 1.3 collective-permute-done.12
  182.7 2.1 collective-permute-start.14
  184.8 3.7 %collective-permute-start.13 = (f32[2,6,4,8,128]{4,3,2,1,0:T(8,128)S(1)}, f32[2,6,4,8,128]{4,3,2,1,0:T(8,128)}, u32[]{:S(2)}, u32[]{:S(2)}) collective-permute-start(f32[2,6,4,8,128]{4,3,2,1,0:T(8,128)S(1)} %pad_maximum_fusion.1.pot_mid), channel_id=1, source_target_pairs={{0,32},{32,64},{64,96},{96,128},{128,160},{160,192},{192,224},{224... | collective-permute-start | bytes 589832 | tf_op jit(solution)/shard_map/ppermute | solution.py:227
  188.6 6.6 %all-to-all-done.1 = bf16[16,2,8,16,128]{4,3,2,1,0:T(8,128)(2,1)} async-done(((bf16[16,2,8,16,128]{4,3,2,1,0:T(8,128)(2,1)}), bf16[16,2,8,16,128]{4,3,2,1,0:T(8,128)(2,1)}, u32[]{:S(2)}, u32[]{:S(2)}) %all-to-all-start.1) | async-done | bytes 1048608 | tf_op jit(solution)/shard_map/all_to_all | solution.py:228
  195.2 1.4 convert_reduce_fusion
  196.6 0.7 copy.27
  197.3 4.2 %all-to-all-start.2 = ((f32[16,2,8,128]{3,2,1,0:T(8,128)}), f32[16,2,8,128]{3,2,1,0:T(8,128)}, u32[]{:S(2)}, u32[]{:S(2)}) async-start(f32[16,2,8,128]{3,2,1,0:T(8,128)} %copy.27), calls=%async_computation.2 | async-start | bytes 262144 | tf_op jit(solution)/shard_map/all_to_all | solution.py:232
  201.5 14.0 %orbital_apply.1 = bf16[8,128,8,128]{3,2,1,0:T(8,128)(2,1)} custom-call(s32[1024]{0:T(1024)S(1)} %bitcast.38, s32[3]{0:T(128)S(1)} %pad_add_fusion.where, bf16[8,128,8,128]{3,2,1,0:T(8,128)(2,1)S(1)} %copy-done, bf16[8,128,1,128]{3,2,1,0:T(2,128)(2,1)S(1)} %collective-permute-done.below, bf16[8,128,1,128]{3,2,1,0:T(2,128)(2,1)S(1)} %collective-permute-done.1.above, ...), custom_call_target="tpu_custom_call" | custom-call | tf_op jit(solution)/shard_map/orbital_apply/pallas_call | solution.py:182
  215.4 0.9 reduce_sum.19
  216.3 0.6 slice_bitcast_fusion.1
  (21 shorter events, 0.1 us)
Async XLA Ops:
  6.0 20.0 %copy-start = (bf16[8,128,8,128]{3,2,1,0:T(8,128)(2,1)S(1)}, bf16[8,128,8,128]{3,2,1,0:T(8,128)(2,1)}, u32[]{:S(2)}) copy-start(bf16[8,128,8,128]{3,2,1,0:T(8,128)(2,1)} %phi.1) | copy-start | bytes 6291460
  6.0 120.9 %all-to-all-start = ((bf16[128,8,8,128]{3,2,1,0:T(8,128)(2,1)}), bf16[128,8,8,128]{3,2,1,0:T(8,128)(2,1)}, u32[]{:S(2)}, u32[]{:S(2)}) async-start(bf16[128,8,8,128]{3,2,1,0:T(8,128)(2,1)} %bitcast.39), calls=%async_computation | async-start | bytes 4194304 | tf_op jit(solution)/shard_map/all_to_all | solution.py:204
  26.0 7.8 %copy-start.1 = (f32[1,8,128]{2,1,0:T(8,128)S(1)}, f32[1,8,128]{2,1,0:T(8,128)}, u32[]{:S(2)}) copy-start(f32[1,8,128]{2,1,0:T(8,128)} %param.5) | copy-start | bytes 12292
  26.9 18.8 %collective-permute-start.1 = (bf16[8,128,1,128]{3,2,1,0:T(2,128)(2,1)S(1)}, bf16[8,128,1,128]{3,2,1,0:T(2,128)(2,1)S(1)}, u32[]{:S(2)}, u32[]{:S(2)}) collective-permute-start(bf16[8,128,1,128]{3,2,1,0:T(2,128)(2,1)S(1)} %get-tuple-element.65), channel_id=1, source_target_pairs={{0,3},{1,0},{2,1},{3,2},{4,7},{5,4},{6,5},{7,6},{8,11},{9,8},{10,9... | collective-permute-start | bytes 786440 | tf_op jit(solution)/shard_map/ppermute | solution.py:208
  31.8 16.8 %collective-permute-start = (bf16[8,128,1,128]{3,2,1,0:T(2,128)(2,1)S(1)}, bf16[8,128,1,128]{3,2,1,0:T(2,128)(2,1)S(1)}, u32[]{:S(2)}, u32[]{:S(2)}) collective-permute-start(bf16[8,128,1,128]{3,2,1,0:T(2,128)(2,1)S(1)} %get-tuple-element.66), channel_id=1, source_target_pairs={{0,1},{1,2},{2,3},{3,0},{4,5},{5,6},{6,7},{7,4},{8,9},{9,10},{10,1... | collective-permute-start | bytes 786440 | tf_op jit(solution)/shard_map/ppermute | solution.py:207
  48.6 71.9 %collective-permute-start.6 = (f32[4,8,128]{2,1,0:T(8,128)S(1)}, f32[4,8,128]{2,1,0:T(8,128)S(1)}, u32[]{:S(2)}, u32[]{:S(2)}) collective-permute-start(f32[4,8,128]{2,1,0:T(8,128)S(1)} %all_gather.3), channel_id=1, source_target_pairs={{0,32},{32,64},{64,96},{96,128},{128,160},{160,192},{192,224},{224... | collective-permute-start | bytes 49160 | tf_op jit(solution)/shard_map/ppermute | solution.py:210
  52.0 68.8 %collective-permute-start.5 = (f32[4,8,128]{2,1,0:T(8,128)S(1)}, f32[4,8,128]{2,1,0:T(8,128)S(1)}, u32[]{:S(2)}, u32[]{:S(2)}) collective-permute-start(f32[4,8,128]{2,1,0:T(8,128)S(1)} %all_gather.3), channel_id=1, source_target_pairs={{0,128},{32,160},{64,192},{96,224},{128,256},{160,288},{192,320},{... | collective-permute-start | bytes 49160 | tf_op jit(solution)/shard_map/ppermute | solution.py:210
  59.5 67.4 %collective-permute-start.4 = (f32[4,8,128]{2,1,0:T(8,128)S(1)}, f32[4,8,128]{2,1,0:T(8,128)S(1)}, u32[]{:S(2)}, u32[]{:S(2)}) collective-permute-start(f32[4,8,128]{2,1,0:T(8,128)S(1)} %all_gather.3), channel_id=1, source_target_pairs={{0,224},{32,256},{64,288},{96,320},{128,352},{160,384},{192,416},{... | collective-permute-start | bytes 49160 | tf_op jit(solution)/shard_map/ppermute | solution.py:210
  66.3 60.6 %collective-permute-start.3 = (f32[4,8,128]{2,1,0:T(8,128)S(1)}, f32[4,8,128]{2,1,0:T(8,128)S(1)}, u32[]{:S(2)}, u32[]{:S(2)}) collective-permute-start(f32[4,8,128]{2,1,0:T(8,128)S(1)} %all_gather.3), channel_id=1, source_target_pairs={{0,320},{32,352},{64,384},{96,416},{128,448},{160,480},{192,0},{22... | collective-permute-start | bytes 49160 | tf_op jit(solution)/shard_map/ppermute | solution.py:210
  73.2 53.7 %collective-permute-start.2 = (f32[4,8,128]{2,1,0:T(8,128)S(1)}, f32[4,8,128]{2,1,0:T(8,128)S(1)}, u32[]{:S(2)}, u32[]{:S(2)}) collective-permute-start(f32[4,8,128]{2,1,0:T(8,128)S(1)} %all_gather.3), channel_id=1, source_target_pairs={{0,416},{32,448},{64,480},{96,0},{128,32},{160,64},{192,96},{224,1... | collective-permute-start | bytes 49160 | tf_op jit(solution)/shard_map/ppermute | solution.py:210
  127.9 7.6 %copy-start.3 = (s32[32,2]{0,1:T(2,128)S(1)}, s32[32,2]{0,1:T(2,128)}, u32[]{:S(2)}) copy-start(s32[32,2]{0,1:T(2,128)} %param.6) | copy-start | bytes 772
  127.9 12.9 %copy-start.2 = (s32[8,128]{1,0:T(8,128)S(1)}, s32[8,128]{1,0:T(8,128)}, u32[]{:S(2)}) copy-start(s32[8,128]{1,0:T(8,128)} %param.7) | copy-start | bytes 12292
  131.2 18.9 %collective-permute-start.8 = (bf16[128,4,8,128]{3,2,1,0:T(8,128)(2,1)}, bf16[128,4,8,128]{3,2,1,0:T(8,128)(2,1)}, u32[]{:S(2)}, u32[]{:S(2)}) collective-permute-start(bf16[128,4,8,128]{3,2,1,0:T(8,128)(2,1)} %get-tuple-element.39), channel_id=1, source_target_pairs={{0,508},{4,0},{8,4},{12,8},{16,12},{20,16},{24,20},{28,24},{32,28}... | collective-permute-start | bytes 3145736 | tf_op jit(solution)/shard_map/ppermute | solution.py:214
  133.1 17.0 %collective-permute-start.9 = (bf16[128,4,8,128]{3,2,1,0:T(8,128)(2,1)}, bf16[128,4,8,128]{3,2,1,0:T(8,128)(2,1)}, u32[]{:S(2)}, u32[]{:S(2)}) collective-permute-start(bf16[128,4,8,128]{3,2,1,0:T(8,128)(2,1)} %get-tuple-element.40), channel_id=1, source_target_pairs={{0,4},{4,8},{8,12},{12,16},{16,20},{20,24},{24,28},{28,32},{32,36}... | collective-permute-start | bytes 3145736 | tf_op jit(solution)/shard_map/ppermute | solution.py:215
  135.8 14.3 %collective-permute-start.10 = (bf16[128,8,128]{2,1,0:T(8,128)(2,1)S(1)}, bf16[128,8,128]{2,1,0:T(8,128)(2,1)S(1)}, u32[]{:S(2)}, u32[]{:S(2)}) collective-permute-start(bf16[128,8,128]{2,1,0:T(8,128)(2,1)S(1)} %slice_bitcast_fusion), channel_id=1, source_target_pairs={{0,3},{1,0},{2,1},{3,2},{4,7},{5,4},{6,5},{7,6},{8,11},{9,8},{10,9... | collective-permute-start | bytes 786440 | tf_op jit(solution)/shard_map/ppermute | solution.py:216
  146.2 16.8 %collective-permute-start.7 = (f32[4,4,8,16,128]{4,3,2,1,0:T(8,128)S(1)}, f32[4,4,8,16,128]{4,3,2,1,0:T(8,128)S(1)}, u32[]{:S(2)}, u32[]{:S(2)}) collective-permute-start(f32[4,4,8,16,128]{4,3,2,1,0:T(8,128)S(1)} %get-tuple-element.37), channel_id=1, source_target_pairs={{0,4},{4,0},{1,5},{5,1},{2,6},{6,2},{3,7},{7,3},{8,12},{12,8},{9,1... | collective-permute-start | bytes 3145736 | tf_op jit(solution)/shard_map/ppermute | solution.py:219
  161.0 4.6 %collective-permute-start.11 = (f32[4,4,8,16,128]{4,3,2,1,0:T(8,128)S(1)}, f32[4,4,8,16,128]{4,3,2,1,0:T(8,128)S(1)}, u32[]{:S(2)}, u32[]{:S(2)}) collective-permute-start(f32[4,4,8,16,128]{4,3,2,1,0:T(8,128)S(1)} %get-tuple-element.43), channel_id=1, source_target_pairs={{0,4},{4,0},{1,5},{5,1},{2,6},{6,2},{3,7},{7,3},{8,12},{12,8},{9,1... | collective-permute-start | bytes 3145736 | tf_op jit(solution)/shard_map/ppermute | solution.py:222
  166.8 28.4 %all-to-all-start.1 = ((bf16[16,2,8,16,128]{4,3,2,1,0:T(8,128)(2,1)}), bf16[16,2,8,16,128]{4,3,2,1,0:T(8,128)(2,1)}, u32[]{:S(2)}, u32[]{:S(2)}) async-start(bf16[16,2,8,16,128]{4,3,2,1,0:T(8,128)(2,1)} %pad_maximum_fusion), calls=%async_computation.1 | async-start | bytes 2097152 | tf_op jit(solution)/shard_map/all_to_all | solution.py:228
  179.5 3.2 %collective-permute-start.12 = (f32[6,4,8,128]{3,2,1,0:T(8,128)S(1)}, f32[6,4,8,128]{3,2,1,0:T(8,128)S(1)}, u32[]{:S(2)}, u32[]{:S(2)}) collective-permute-start(f32[6,4,8,128]{3,2,1,0:T(8,128)S(1)} %bitcast_dynamic-update-slice_fusion), channel_id=1, source_target_pairs={{0,4},{4,0},{1,5},{5,1},{2,6},{6,2},{3,7},{7,3},{8,12},{12,8},{9,1... | collective-permute-start | bytes 294920 | tf_op jit(solution)/shard_map/ppermute | solution.py:226
  182.7 13.9 %collective-permute-start.14 = (f32[2,6,4,8,128]{4,3,2,1,0:T(8,128)S(1)}, f32[2,6,4,8,128]{4,3,2,1,0:T(8,128)S(1)}, u32[]{:S(2)}, u32[]{:S(2)}) collective-permute-start(f32[2,6,4,8,128]{4,3,2,1,0:T(8,128)S(1)} %pad_maximum_fusion.1.pot_mid), channel_id=1, source_target_pairs={{0,480},{32,0},{64,32},{96,64},{128,96},{160,128},{192,160},{224,1... | collective-permute-start | bytes 589832 | tf_op jit(solution)/shard_map/ppermute | solution.py:227
  184.8 11.7 %collective-permute-start.13 = (f32[2,6,4,8,128]{4,3,2,1,0:T(8,128)S(1)}, f32[2,6,4,8,128]{4,3,2,1,0:T(8,128)}, u32[]{:S(2)}, u32[]{:S(2)}) collective-permute-start(f32[2,6,4,8,128]{4,3,2,1,0:T(8,128)S(1)} %pad_maximum_fusion.1.pot_mid), channel_id=1, source_target_pairs={{0,32},{32,64},{64,96},{96,128},{128,160},{160,192},{192,224},{224... | collective-permute-start | bytes 589832 | tf_op jit(solution)/shard_map/ppermute | solution.py:227
  197.3 18.1 %all-to-all-start.2 = ((f32[16,2,8,128]{3,2,1,0:T(8,128)}), f32[16,2,8,128]{3,2,1,0:T(8,128)}, u32[]{:S(2)}, u32[]{:S(2)}) async-start(f32[16,2,8,128]{3,2,1,0:T(8,128)} %copy.27), calls=%async_computation.2 | async-start | bytes 262144 | tf_op jit(solution)/shard_map/all_to_all | solution.py:232

commit v8 on v7

--- a/solution.py
+++ b/solution.py
@@ -15,7 +15,8 @@
 PAIRS = 32
 ZD, XD, CD, YD = 16, 4, 2, 4
 REGION = ("z", "x", "c")
-STRIDE = (0, 3, 6, 9, 12, 15)
+STRIDE = (0, 4, 8, 12)
+SHIFTS = (-1, 0, 1, 2)
 F32 = jnp.float32
 BF16 = jnp.bfloat16
 
@@ -150,10 +151,10 @@
     )(pair_flat, support_flat, where, conf, ahead, behind, above, pot)
 
 
-def orbital_kernel(support, where, phi, below, above, pot_low, pot_mid, pot_high, out, pot):
+def orbital_kernel(support, where, phi, below, above, pot_0, pot_1, pot_2, pot_3, out, pot):
     block, row_z = where[2], where[0] // 8
     core = where[1]
-    for step, piece in enumerate((pot_low, pot_mid, pot_high)):
+    for step, piece in enumerate((pot_0, pot_1, pot_2, pot_3)):
         pot[step] = piece[...]
     lane = lax.broadcasted_iota(jnp.int32, (8, ROWS, DEPTH), 2)
     row = lax.broadcasted_iota(jnp.int32, (8, ROWS, DEPTH), 1)
@@ -169,8 +170,8 @@
         high = jnp.where(row == ROWS - 1, above[:, x].astype(F32), pltpu.roll(centre, ROWS - 1, 1))
         around = lane_neighbours(centre, lane) + low + high + before + after
         live = flag(support, block, x)
-        ahead_by = lax.rem(x // 8 - row_z + ZD, ZD) + 1
-        values = pot[lax.rem(ahead_by, 3), lax.rem(x + core, CD), ahead_by // 3, lax.rem(x // 2, XD)]
+        ahead_by = lax.rem(x // 8 - row_z + ZD + 1, ZD)
+        values = pot[lax.rem(ahead_by, 4), lax.rem(x + core, CD), ahead_by // 4, lax.rem(x // 2, XD)]
         applied = ((3.0 + values)[None] * centre - 0.5 * around) * live
         out[:, x] = applied.astype(BF16)
         return centre * live, 0
@@ -182,9 +183,9 @@
     return pl.pallas_call(
         orbital_kernel,
         out_shape=jax.ShapeDtypeStruct(phi.shape, BF16),
-        in_specs=[SMEM] * 2 + [VMEM] * 6,
+        in_specs=[SMEM] * 2 + [VMEM] * 7,
         out_specs=VMEM,
-        scratch_shapes=[pltpu.VMEM((3, CD, len(STRIDE), XD, ROWS, DEPTH), F32)],
+        scratch_shapes=[pltpu.VMEM((len(SHIFTS), CD, len(STRIDE), XD, ROWS, DEPTH), F32)],
         compiler_params=pltpu.CompilerParams(vmem_limit_bytes=14 << 20),
         name="orbital_apply",
     )(support_flat, where, phi, below, above, *pieces)
@@ -224,7 +225,7 @@
     total, strided = lax.optimization_barrier((total, strided))
     column = jnp.stack(strided)
     column = jnp.stack([column, lax.ppermute(column, "c", swap)])
-    pieces = [lax.ppermute(column, "z", ring(ZD, 1)), column, lax.ppermute(column, "z", ring(ZD, -1))]
+    pieces = [lax.ppermute(column, "z", ring(ZD, -s)) if s else column for s in SHIFTS]
     shares = lax.all_to_all(total, ("x", "y"), split_axis=0, concat_axis=0, tiled=True)
     partial = jnp.sum(shares.astype(F32), axis=0).transpose(2, 0, 1, 3)
     partial, pieces = lax.optimization_barrier((partial, pieces))

time: 220 us -> 218 us (level)
  starting transfers between devices: 93.2 us -> 89.1 us
  waiting for transfers between devices: 64.7 us -> 68.4 us
    ppermute x5 -> x3, waiting for transfers between devices: 51.4 us -> 58 us  [local(): lax.ppermute(planes, 'z', ring(ZD, -s))]
    all_to_all x1, starting transfers between devices: 12.6 us -> 7.31 us  [local(): lax.all_to_all(total, ('x', 'y'), split_axis=0, concat_axis=0, tiled=True)]
    ppermute x5 -> x3, starting transfers between devices: 26.9 us -> 22.2 us  [local(): lax.ppermute(planes, 'z', ring(ZD, -s))]
    ppermute x2 -> x3, starting transfers between devices: 5.84 us -> 8.85 us  [local(): lax.ppermute(column, 'z', ring(ZD, -s))]
    all_to_all x1, waiting for transfers between devices: 6.63 us -> 3.72 us  [local(): lax.all_to_all(total, ('x', 'y'), split_axis=0, concat_axis=0, tiled=True)]
    all_to_all x1, starting transfers between devices: 4.16 us -> 6.65 us  [local(): lax.all_to_all(partial, ('z',), split_axis=0, concat_axis=0, tiled=True)]
    unnamed x15 -> x10, local copies, waits for them, and re-layouts: 5.47 us -> 5.45 us
  transfers between devices with their start and end apart: 18 -> 17, of which waited for: 7 -> 6; matrix products, arithmetic and copies ran while one was open for 1% -> 1% of each run, Pallas kernels for 14% -> 14%
where the time goes in v8:
time: 218 us; the launch traced here: 217 us
  starting transfers between devices  89.1 us (41%)
  waiting for transfers between devices  68.4 us (31%)
  Pallas kernels  30.4 us (14%)
  local copies, waits for them, and re-layouts  12 us (6%)
  blocking collectives  12 us (6%)
  other arithmetic  3.76 us (2%)
    ppermute x3, waiting for transfers between devices, local(): lax.ppermute(planes, 'z', ring(ZD, -s))  58 us
    ppermute x3, starting transfers between devices, local(): lax.ppermute(planes, 'z', ring(ZD, -s))  22.2 us
    all_to_all x1, starting transfers between devices, local(): lax.all_to_all(phi.transpose(1, 2, 0, 3), REGION, split_axis=0, concat_ax...  20 us
    pallas_call x1, Pallas kernels, orbital_apply(): pl.pallas_call(orbital_kernel, out_shape=jax.ShapeDtypeStruct(phi.shape,...  14.1 us
    all_gather x1, blocking collectives, local(): planes = lax.all_gather(potential, 'x', axis=0, tiled=True)  12 us
    pallas_call x1, Pallas kernels, hamiltonian_products(): pl.pallas_call(hamiltonian_kernel, out_shape=(SHARE, SHARE), in_specs=[SM...  10.9 us
    ppermute x3, starting transfers between devices, local(): lax.ppermute(column, 'z', ring(ZD, -s))  8.85 us
    all_to_all x1, starting transfers between devices, local(): lax.all_to_all(total, ('x', 'y'), split_axis=0, concat_axis=0, tiled=True)  7.31 us
  transfers between devices with their start and end apart: 17, of which 6 were waited for; matrix products, arithmetic and copies ran while one was open for 1% of the time, Pallas kernels for 14%

profile of v8, /device:TPU:6, one launch (start us, length us, event | category | flops | bytes accessed | tf_op | source)
XLA Modules:
  0.0 216.6 jit_solution(10095023521037352970)
XLA Ops:
  0.6 5.3 %copy.31 = bf16[8,128,8,128]{3,0,2,1:T(8,128)(2,1)} copy(bf16[8,128,8,128]{3,2,1,0:T(8,128)(2,1)} %phi.1) | data formatting | bytes 4194304 | tf_op args[0]
  6.0 20.0 %all-to-all-start = ((bf16[128,8,8,128]{3,2,1,0:T(8,128)(2,1)}), bf16[128,8,8,128]{3,2,1,0:T(8,128)(2,1)}, u32[]{:S(2)}, u32[]{:S(2)}) async-start(bf16[128,8,8,128]{3,2,1,0:T(8,128)(2,1)} %bitcast.32), calls=%async_computation | async-start | bytes 4194304 | tf_op jit(solution)/shard_map/all_to_all | solution.py:205
  26.0 0.0 copy-start.1
  26.0 0.9 fusion.2
  26.9 4.9 %collective-permute-start.1 = (bf16[8,128,1,128]{3,2,1,0:T(2,128)(2,1)S(1)}, bf16[8,128,1,128]{3,2,1,0:T(2,128)(2,1)S(1)}, u32[]{:S(2)}, u32[]{:S(2)}) collective-permute-start(bf16[8,128,1,128]{3,2,1,0:T(2,128)(2,1)S(1)} %get-tuple-element.59), channel_id=1, source_target_pairs={{0,3},{1,0},{2,1},{3,2},{4,7},{5,4},{6,5},{7,6},{8,11},{9,8},{10,9... | collective-permute-start | bytes 786440 | tf_op jit(solution)/shard_map/ppermute | solution.py:209
  31.8 1.9 collective-permute-start
  33.8 12.0 %all_gather.3 = f32[4,8,128]{2,1,0:T(8,128)S(1)} all-gather(f32[1,8,128]{2,1,0:T(8,128)S(1)} %copy-done.1), channel_id=1, replica_groups=mesh['z'=16,'x'=4,'c'=2,'y'=4] {'x'}, dimensions={0}, use_global_device_ids=true | all-gather | bytes 20480 | tf_op jit(solution)/shard_map/all_gather | solution.py:207
  45.7 0.0 collective-permute-done.1.above
  45.7 2.9 %collective-permute-done.below = bf16[8,128,1,128]{3,2,1,0:T(2,128)(2,1)S(1)} collective-permute-done((bf16[8,128,1,128]{3,2,1,0:T(2,128)(2,1)S(1)}, bf16[8,128,1,128]{3,2,1,0:T(2,128)(2,1)S(1)}, u32[]{:S(2)}, u32[]{:S(2)}) %collective-permute-start) | collective-permute-done | bytes 262176 | tf_op jit(solution)/shard_map/ppermute | solution.py:208
  48.6 7.4 %collective-permute-start.4 = (f32[4,8,128]{2,1,0:T(8,128)S(1)}, f32[4,8,128]{2,1,0:T(8,128)S(1)}, u32[]{:S(2)}, u32[]{:S(2)}) collective-permute-start(f32[4,8,128]{2,1,0:T(8,128)S(1)} %all_gather.3), channel_id=1, source_target_pairs={{0,128},{32,160},{64,192},{96,224},{128,256},{160,288},{192,320},{... | collective-permute-start | bytes 49160 | tf_op jit(solution)/shard_map/ppermute | solution.py:211
  56.1 7.7 %collective-permute-start.3 = (f32[4,8,128]{2,1,0:T(8,128)S(1)}, f32[4,8,128]{2,1,0:T(8,128)S(1)}, u32[]{:S(2)}, u32[]{:S(2)}) collective-permute-start(f32[4,8,128]{2,1,0:T(8,128)S(1)} %all_gather.3), channel_id=1, source_target_pairs={{0,256},{32,288},{64,320},{96,352},{128,384},{160,416},{192,448},{... | collective-permute-start | bytes 49160 | tf_op jit(solution)/shard_map/ppermute | solution.py:211
  63.8 7.1 %collective-permute-start.2 = (f32[4,8,128]{2,1,0:T(8,128)S(1)}, f32[4,8,128]{2,1,0:T(8,128)S(1)}, u32[]{:S(2)}, u32[]{:S(2)}) collective-permute-start(f32[4,8,128]{2,1,0:T(8,128)S(1)} %all_gather.3), channel_id=1, source_target_pairs={{0,384},{32,416},{64,448},{96,480},{128,0},{160,32},{192,64},{224,... | collective-permute-start | bytes 49160 | tf_op jit(solution)/shard_map/ppermute | solution.py:211
  70.8 48.5 %collective-permute-done.4 = f32[4,8,128]{2,1,0:T(8,128)S(1)} collective-permute-done((f32[4,8,128]{2,1,0:T(8,128)S(1)}, f32[4,8,128]{2,1,0:T(8,128)S(1)}, u32[]{:S(2)}, u32[]{:S(2)}) %collective-permute-start.4) | collective-permute-done | bytes 16416 | tf_op jit(solution)/shard_map/ppermute | solution.py:211
  119.4 9.5 %collective-permute-done.3 = f32[4,8,128]{2,1,0:T(8,128)S(1)} collective-permute-done((f32[4,8,128]{2,1,0:T(8,128)S(1)}, f32[4,8,128]{2,1,0:T(8,128)S(1)}, u32[]{:S(2)}, u32[]{:S(2)}) %collective-permute-start.3) | collective-permute-done | bytes 16416 | tf_op jit(solution)/shard_map/ppermute | solution.py:211
  128.9 0.0 collective-permute-done.2
  128.9 0.0 all-to-all-done.own
  128.9 1.0 slice_bitcast_fusion
  129.9 0.0 copy-start.3
  129.9 0.0 copy-start.2
  129.9 3.3 %fusion.1 = (bf16[128,4,8,128]{3,2,1,0:T(8,128)(2,1)}, bf16[128,4,8,128]{3,2,1,0:T(8,128)(2,1)}) fusion(bf16[128,8,8,128]{3,2,1,0:T(8,128)(2,1)} %all-to-all-done.own), kind=kLoop, calls=%fused_computation.12 | loop fusion | bytes 4194304 | tf_op jit(solution)/shard_map/slice | solution.py:214
  133.2 1.9 collective-permute-start.6
  135.1 2.4 %collective-permute-start.7 = (bf16[128,4,8,128]{3,2,1,0:T(8,128)(2,1)}, bf16[128,4,8,128]{3,2,1,0:T(8,128)(2,1)}, u32[]{:S(2)}, u32[]{:S(2)}) collective-permute-start(bf16[128,4,8,128]{3,2,1,0:T(8,128)(2,1)} %get-tuple-element.37), channel_id=1, source_target_pairs={{0,4},{4,8},{8,12},{12,16},{16,20},{20,24},{24,28},{28,32},{32,36}... | collective-permute-start | bytes 3145736 | tf_op jit(solution)/shard_map/ppermute | solution.py:216
  137.5 0.1 copy.22
  137.6 0.1 reshape.19.pairs
  137.7 4.9 %collective-permute-start.8 = (bf16[128,8,128]{2,1,0:T(8,128)(2,1)S(1)}, bf16[128,8,128]{2,1,0:T(8,128)(2,1)S(1)}, u32[]{:S(2)}, u32[]{:S(2)}) collective-permute-start(bf16[128,8,128]{2,1,0:T(8,128)(2,1)S(1)} %slice_bitcast_fusion), channel_id=1, source_target_pairs={{0,3},{1,0},{2,1},{3,2},{4,7},{5,4},{6,5},{7,6},{8,11},{9,8},{10,9... | collective-permute-start | bytes 786440 | tf_op jit(solution)/shard_map/ppermute | solution.py:217
  142.7 0.1 pad_add_fusion.where
  142.7 5.4 %overlap_products.1 = (bf16[1024,1024]{1,0:T(8,128)(2,1)S(1)}, f32[4,4,8,16,128]{4,3,2,1,0:T(8,128)S(1)}, f32[4,4,8,16,128]{4,3,2,1,0:T(8,128)S(1)}) custom-call(s32[64]{0:T(128)S(1)} %reshape.19.pairs, s32[1024]{0:T(1024)S(1)} %bitcast.29, s32[3]{0:T(128)S(1)} %pad_add_fusion.where, bf16[128,8,8,128]{3,2,1,0:T(8,128)(2,1)} %all-to-all-done.own), custom_call_target="tpu_custom_call" | custom-call | flops 2000000000 | bytes 8388608 | tf_op jit(solution)/shard_map/overlap_products/pallas_call | solution.py:125
  148.2 4.2 %collective-permute-start.5 = (f32[4,4,8,16,128]{4,3,2,1,0:T(8,128)S(1)}, f32[4,4,8,16,128]{4,3,2,1,0:T(8,128)S(1)}, u32[]{:S(2)}, u32[]{:S(2)}) collective-permute-start(f32[4,4,8,16,128]{4,3,2,1,0:T(8,128)S(1)} %get-tuple-element.34), channel_id=1, source_target_pairs={{0,4},{4,0},{1,5},{5,1},{2,6},{6,2},{3,7},{7,3},{8,12},{12,8},{9,1... | collective-permute-start | bytes 3145736 | tf_op jit(solution)/shard_map/ppermute | solution.py:220
  152.4 10.9 %hamiltonian_products.1 = (f32[4,4,8,16,128]{4,3,2,1,0:T(8,128)S(1)}, f32[4,4,8,16,128]{4,3,2,1,0:T(8,128)S(1)}) custom-call(s32[64]{0:T(128)S(1)} %reshape.19.pairs, s32[1024]{0:T(1024)S(1)} %bitcast.30, s32[3]{0:T(128)S(1)} %pad_add_fusion.where, bf16[1024,1024]{1,0:T(8,128)(2,1)S(1)} %get-tuple-element.35.conf, ...), custom_call_target="tpu_custom_call" | custom-call | flops 5000000000 | bytes 8388608 | tf_op jit(solution)/shard_map/hamiltonian_products/pallas_call | solution.py:138
  163.4 1.9 collective-permute-start.9
  165.3 0.1 add_convert_fusion.1
  165.4 2.5 %collective-permute-done.9 = f32[4,4,8,16,128]{4,3,2,1,0:T(8,128)S(1)} collective-permute-done((f32[4,4,8,16,128]{4,3,2,1,0:T(8,128)S(1)}, f32[4,4,8,16,128]{4,3,2,1,0:T(8,128)S(1)}, u32[]{:S(2)}, u32[]{:S(2)}) %collective-permute-start.9) | collective-permute-done | bytes 1048608 | tf_op jit(solution)/shard_map/ppermute | solution.py:223
  167.9 0.1 add_convert_fusion
  168.1 1.1 pad_maximum_fusion
  169.1 7.3 %all-to-all-start.1 = ((bf16[16,2,8,16,128]{4,3,2,1,0:T(8,128)(2,1)}), bf16[16,2,8,16,128]{4,3,2,1,0:T(8,128)(2,1)}, u32[]{:S(2)}, u32[]{:S(2)}) async-start(bf16[16,2,8,16,128]{4,3,2,1,0:T(8,128)(2,1)} %pad_maximum_fusion), calls=%async_computation.1 | async-start | bytes 2097152 | tf_op jit(solution)/shard_map/all_to_all | solution.py:229
  176.4 1.9 collective-permute-start.10
  178.4 1.2 collective-permute-done.10
  179.6 2.3 %collective-permute-start.13 = (f32[2,4,4,8,128]{4,3,2,1,0:T(8,128)S(1)}, f32[2,4,4,8,128]{4,3,2,1,0:T(8,128)S(1)}, u32[]{:S(2)}, u32[]{:S(2)}) collective-permute-start(f32[2,4,4,8,128]{4,3,2,1,0:T(8,128)S(1)} %pad_maximum_fusion.1.pot_1), channel_id=1, source_target_pairs={{0,448},{32,480},{64,0},{96,32},{128,64},{160,96},{192,128},{224,1... | collective-permute-start | bytes 393224 | tf_op jit(solution)/shard_map/ppermute | solution.py:228
  181.9 3.2 %collective-permute-start.12 = (f32[2,4,4,8,128]{4,3,2,1,0:T(8,128)S(1)}, f32[2,4,4,8,128]{4,3,2,1,0:T(8,128)S(1)}, u32[]{:S(2)}, u32[]{:S(2)}) collective-permute-start(f32[2,4,4,8,128]{4,3,2,1,0:T(8,128)S(1)} %pad_maximum_fusion.1.pot_1), channel_id=1, source_target_pairs={{0,480},{32,0},{64,32},{96,64},{128,96},{160,128},{192,160},{224,1... | collective-permute-start | bytes 393224 | tf_op jit(solution)/shard_map/ppermute | solution.py:228
  185.1 3.4 %collective-permute-start.11 = (f32[2,4,4,8,128]{4,3,2,1,0:T(8,128)S(1)}, f32[2,4,4,8,128]{4,3,2,1,0:T(8,128)}, u32[]{:S(2)}, u32[]{:S(2)}) collective-permute-start(f32[2,4,4,8,128]{4,3,2,1,0:T(8,128)S(1)} %pad_maximum_fusion.1.pot_1), channel_id=1, source_target_pairs={{0,32},{32,64},{64,96},{96,128},{128,160},{160,192},{192,224},{224... | collective-permute-start | bytes 393224 | tf_op jit(solution)/shard_map/ppermute | solution.py:228
  188.5 3.7 %all-to-all-done.1 = bf16[16,2,8,16,128]{4,3,2,1,0:T(8,128)(2,1)} async-done(((bf16[16,2,8,16,128]{4,3,2,1,0:T(8,128)(2,1)}), bf16[16,2,8,16,128]{4,3,2,1,0:T(8,128)(2,1)}, u32[]{:S(2)}, u32[]{:S(2)}) %all-to-all-start.1) | async-done | bytes 1048608 | tf_op jit(solution)/shard_map/all_to_all | solution.py:229
  192.2 1.4 convert_reduce_fusion
  193.6 0.0 collective-permute-done.12.pot_2
  193.6 0.7 copy.27
  194.3 6.6 %all-to-all-start.2 = ((f32[16,2,8,128]{3,2,1,0:T(8,128)}), f32[16,2,8,128]{3,2,1,0:T(8,128)}, u32[]{:S(2)}, u32[]{:S(2)}) async-start(f32[16,2,8,128]{3,2,1,0:T(8,128)} %copy.27), calls=%async_computation.2 | async-start | bytes 262144 | tf_op jit(solution)/shard_map/all_to_all | solution.py:233
  201.0 14.1 %orbital_apply.1 = bf16[8,128,8,128]{3,2,1,0:T(8,128)(2,1)} custom-call(s32[1024]{0:T(1024)S(1)} %bitcast.31, s32[3]{0:T(128)S(1)} %pad_add_fusion.where, bf16[8,128,8,128]{3,2,1,0:T(8,128)(2,1)S(1)} %copy-done, bf16[8,128,1,128]{3,2,1,0:T(2,128)(2,1)S(1)} %collective-permute-done.below, bf16[8,128,1,128]{3,2,1,0:T(2,128)(2,1)S(1)} %collective-permute-done.1.above, ...), custom_call_target="tpu_custom_call" | custom-call | tf_op jit(solution)/shard_map/orbital_apply/pallas_call | solution.py:183
  215.1 0.9 reduce_sum.19
  216.0 0.6 slice_bitcast_fusion.1
  (14 shorter events, 0.0 us)
Async XLA Ops:
  6.0 20.0 %copy-start = (bf16[8,128,8,128]{3,2,1,0:T(8,128)(2,1)S(1)}, bf16[8,128,8,128]{3,2,1,0:T(8,128)(2,1)}, u32[]{:S(2)}) copy-start(bf16[8,128,8,128]{3,2,1,0:T(8,128)(2,1)} %phi.1) | copy-start | bytes 6291460
  6.0 122.9 %all-to-all-start = ((bf16[128,8,8,128]{3,2,1,0:T(8,128)(2,1)}), bf16[128,8,8,128]{3,2,1,0:T(8,128)(2,1)}, u32[]{:S(2)}, u32[]{:S(2)}) async-start(bf16[128,8,8,128]{3,2,1,0:T(8,128)(2,1)} %bitcast.32), calls=%async_computation | async-start | bytes 4194304 | tf_op jit(solution)/shard_map/all_to_all | solution.py:205
  26.0 7.8 %copy-start.1 = (f32[1,8,128]{2,1,0:T(8,128)S(1)}, f32[1,8,128]{2,1,0:T(8,128)}, u32[]{:S(2)}) copy-start(f32[1,8,128]{2,1,0:T(8,128)} %param.5) | copy-start | bytes 12292
  26.9 18.8 %collective-permute-start.1 = (bf16[8,128,1,128]{3,2,1,0:T(2,128)(2,1)S(1)}, bf16[8,128,1,128]{3,2,1,0:T(2,128)(2,1)S(1)}, u32[]{:S(2)}, u32[]{:S(2)}) collective-permute-start(bf16[8,128,1,128]{3,2,1,0:T(2,128)(2,1)S(1)} %get-tuple-element.59), channel_id=1, source_target_pairs={{0,3},{1,0},{2,1},{3,2},{4,7},{5,4},{6,5},{7,6},{8,11},{9,8},{10,9... | collective-permute-start | bytes 786440 | tf_op jit(solution)/shard_map/ppermute | solution.py:209
  31.8 16.8 %collective-permute-start = (bf16[8,128,1,128]{3,2,1,0:T(2,128)(2,1)S(1)}, bf16[8,128,1,128]{3,2,1,0:T(2,128)(2,1)S(1)}, u32[]{:S(2)}, u32[]{:S(2)}) collective-permute-start(bf16[8,128,1,128]{3,2,1,0:T(2,128)(2,1)S(1)} %get-tuple-element.60), channel_id=1, source_target_pairs={{0,1},{1,2},{2,3},{3,0},{4,5},{5,6},{6,7},{7,4},{8,9},{9,10},{10,1... | collective-permute-start | bytes 786440 | tf_op jit(solution)/shard_map/ppermute | solution.py:208
  48.6 70.7 %collective-permute-start.4 = (f32[4,8,128]{2,1,0:T(8,128)S(1)}, f32[4,8,128]{2,1,0:T(8,128)S(1)}, u32[]{:S(2)}, u32[]{:S(2)}) collective-permute-start(f32[4,8,128]{2,1,0:T(8,128)S(1)} %all_gather.3), channel_id=1, source_target_pairs={{0,128},{32,160},{64,192},{96,224},{128,256},{160,288},{192,320},{... | collective-permute-start | bytes 49160 | tf_op jit(solution)/shard_map/ppermute | solution.py:211
  56.1 72.8 %collective-permute-start.3 = (f32[4,8,128]{2,1,0:T(8,128)S(1)}, f32[4,8,128]{2,1,0:T(8,128)S(1)}, u32[]{:S(2)}, u32[]{:S(2)}) collective-permute-start(f32[4,8,128]{2,1,0:T(8,128)S(1)} %all_gather.3), channel_id=1, source_target_pairs={{0,256},{32,288},{64,320},{96,352},{128,384},{160,416},{192,448},{... | collective-permute-start | bytes 49160 | tf_op jit(solution)/shard_map/ppermute | solution.py:211
  63.8 65.1 %collective-permute-start.2 = (f32[4,8,128]{2,1,0:T(8,128)S(1)}, f32[4,8,128]{2,1,0:T(8,128)S(1)}, u32[]{:S(2)}, u32[]{:S(2)}) collective-permute-start(f32[4,8,128]{2,1,0:T(8,128)S(1)} %all_gather.3), channel_id=1, source_target_pairs={{0,384},{32,416},{64,448},{96,480},{128,0},{160,32},{192,64},{224,... | collective-permute-start | bytes 49160 | tf_op jit(solution)/shard_map/ppermute | solution.py:211
  129.9 7.6 %copy-start.3 = (s32[32,2]{0,1:T(2,128)S(1)}, s32[32,2]{0,1:T(2,128)}, u32[]{:S(2)}) copy-start(s32[32,2]{0,1:T(2,128)} %param.6) | copy-start | bytes 772
  129.9 12.9 %copy-start.2 = (s32[8,128]{1,0:T(8,128)S(1)}, s32[8,128]{1,0:T(8,128)}, u32[]{:S(2)}) copy-start(s32[8,128]{1,0:T(8,128)} %param.7) | copy-start | bytes 12292
  133.2 19.2 %collective-permute-start.6 = (bf16[128,4,8,128]{3,2,1,0:T(8,128)(2,1)}, bf16[128,4,8,128]{3,2,1,0:T(8,128)(2,1)}, u32[]{:S(2)}, u32[]{:S(2)}) collective-permute-start(bf16[128,4,8,128]{3,2,1,0:T(8,128)(2,1)} %get-tuple-element.36), channel_id=1, source_target_pairs={{0,508},{4,0},{8,4},{12,8},{16,12},{20,16},{24,20},{28,24},{32,28}... | collective-permute-start | bytes 3145736 | tf_op jit(solution)/shard_map/ppermute | solution.py:215
  135.1 17.3 %collective-permute-start.7 = (bf16[128,4,8,128]{3,2,1,0:T(8,128)(2,1)}, bf16[128,4,8,128]{3,2,1,0:T(8,128)(2,1)}, u32[]{:S(2)}, u32[]{:S(2)}) collective-permute-start(bf16[128,4,8,128]{3,2,1,0:T(8,128)(2,1)} %get-tuple-element.37), channel_id=1, source_target_pairs={{0,4},{4,8},{8,12},{12,16},{16,20},{20,24},{24,28},{28,32},{32,36}... | collective-permute-start | bytes 3145736 | tf_op jit(solution)/shard_map/ppermute | solution.py:216
  137.7 14.6 %collective-permute-start.8 = (bf16[128,8,128]{2,1,0:T(8,128)(2,1)S(1)}, bf16[128,8,128]{2,1,0:T(8,128)(2,1)S(1)}, u32[]{:S(2)}, u32[]{:S(2)}) collective-permute-start(bf16[128,8,128]{2,1,0:T(8,128)(2,1)S(1)} %slice_bitcast_fusion), channel_id=1, source_target_pairs={{0,3},{1,0},{2,1},{3,2},{4,7},{5,4},{6,5},{7,6},{8,11},{9,8},{10,9... | collective-permute-start | bytes 786440 | tf_op jit(solution)/shard_map/ppermute | solution.py:217
  148.2 17.1 %collective-permute-start.5 = (f32[4,4,8,16,128]{4,3,2,1,0:T(8,128)S(1)}, f32[4,4,8,16,128]{4,3,2,1,0:T(8,128)S(1)}, u32[]{:S(2)}, u32[]{:S(2)}) collective-permute-start(f32[4,4,8,16,128]{4,3,2,1,0:T(8,128)S(1)} %get-tuple-element.34), channel_id=1, source_target_pairs={{0,4},{4,0},{1,5},{5,1},{2,6},{6,2},{3,7},{7,3},{8,12},{12,8},{9,1... | collective-permute-start | bytes 3145736 | tf_op jit(solution)/shard_map/ppermute | solution.py:220
  163.4 4.6 %collective-permute-start.9 = (f32[4,4,8,16,128]{4,3,2,1,0:T(8,128)S(1)}, f32[4,4,8,16,128]{4,3,2,1,0:T(8,128)S(1)}, u32[]{:S(2)}, u32[]{:S(2)}) collective-permute-start(f32[4,4,8,16,128]{4,3,2,1,0:T(8,128)S(1)} %get-tuple-element.40), channel_id=1, source_target_pairs={{0,4},{4,0},{1,5},{5,1},{2,6},{6,2},{3,7},{7,3},{8,12},{12,8},{9,1... | collective-permute-start | bytes 3145736 | tf_op jit(solution)/shard_map/ppermute | solution.py:223
  169.1 23.1 %all-to-all-start.1 = ((bf16[16,2,8,16,128]{4,3,2,1,0:T(8,128)(2,1)}), bf16[16,2,8,16,128]{4,3,2,1,0:T(8,128)(2,1)}, u32[]{:S(2)}, u32[]{:S(2)}) async-start(bf16[16,2,8,16,128]{4,3,2,1,0:T(8,128)(2,1)} %pad_maximum_fusion), calls=%async_computation.1 | async-start | bytes 2097152 | tf_op jit(solution)/shard_map/all_to_all | solution.py:229
  176.4 3.1 %collective-permute-start.10 = (f32[4,4,8,128]{3,2,1,0:T(8,128)S(1)}, f32[4,4,8,128]{3,2,1,0:T(8,128)S(1)}, u32[]{:S(2)}, u32[]{:S(2)}) collective-permute-start(f32[4,4,8,128]{3,2,1,0:T(8,128)S(1)} %get-tuple-element.62), channel_id=1, source_target_pairs={{0,4},{4,0},{1,5},{5,1},{2,6},{6,2},{3,7},{7,3},{8,12},{12,8},{9,1... | collective-permute-start | bytes 196616 | tf_op jit(solution)/shard_map/ppermute | solution.py:227
  179.6 14.0 %collective-permute-start.13 = (f32[2,4,4,8,128]{4,3,2,1,0:T(8,128)S(1)}, f32[2,4,4,8,128]{4,3,2,1,0:T(8,128)S(1)}, u32[]{:S(2)}, u32[]{:S(2)}) collective-permute-start(f32[2,4,4,8,128]{4,3,2,1,0:T(8,128)S(1)} %pad_maximum_fusion.1.pot_1), channel_id=1, source_target_pairs={{0,448},{32,480},{64,0},{96,32},{128,64},{160,96},{192,128},{224,1... | collective-permute-start | bytes 393224 | tf_op jit(solution)/shard_map/ppermute | solution.py:228
  181.9 11.7 %collective-permute-start.12 = (f32[2,4,4,8,128]{4,3,2,1,0:T(8,128)S(1)}, f32[2,4,4,8,128]{4,3,2,1,0:T(8,128)S(1)}, u32[]{:S(2)}, u32[]{:S(2)}) collective-permute-start(f32[2,4,4,8,128]{4,3,2,1,0:T(8,128)S(1)} %pad_maximum_fusion.1.pot_1), channel_id=1, source_target_pairs={{0,480},{32,0},{64,32},{96,64},{128,96},{160,128},{192,160},{224,1... | collective-permute-start | bytes 393224 | tf_op jit(solution)/shard_map/ppermute | solution.py:228
  185.1 8.5 %collective-permute-start.11 = (f32[2,4,4,8,128]{4,3,2,1,0:T(8,128)S(1)}, f32[2,4,4,8,128]{4,3,2,1,0:T(8,128)}, u32[]{:S(2)}, u32[]{:S(2)}) collective-permute-start(f32[2,4,4,8,128]{4,3,2,1,0:T(8,128)S(1)} %pad_maximum_fusion.1.pot_1), channel_id=1, source_target_pairs={{0,32},{32,64},{64,96},{96,128},{128,160},{160,192},{192,224},{224... | collective-permute-start | bytes 393224 | tf_op jit(solution)/shard_map/ppermute | solution.py:228
  194.3 20.7 %all-to-all-start.2 = ((f32[16,2,8,128]{3,2,1,0:T(8,128)}), f32[16,2,8,128]{3,2,1,0:T(8,128)}, u32[]{:S(2)}, u32[]{:S(2)}) async-start(f32[16,2,8,128]{3,2,1,0:T(8,128)} %copy.27), calls=%async_computation.2 | async-start | bytes 262144 | tf_op jit(solution)/shard_map/all_to_all | solution.py:233

commit v9 on v8

--- a/solution.py
+++ b/solution.py
@@ -176,7 +176,12 @@
         out[:, x] = applied.astype(BF16)
         return centre * live, 0
 
-    lax.fori_loop(0, PLANES, step, (masked(PLANES - 1), 0))
+    def eight(n, carry):
+        for part in range(8):
+            carry = step(8 * n + part, carry)
+        return carry
+
+    lax.fori_loop(0, PLANES // 8, eight, (masked(PLANES - 1), 0))
 
 
 def orbital_apply(support_flat, where, phi, below, above, pieces):

time: 218 us -> 217 us (level)
  Pallas kernels: 30.4 us -> 22.7 us
  waiting for transfers between devices: 68.4 us -> 75.9 us
    pallas_call x1, Pallas kernels: 14.1 us -> 6.36 us  [orbital_apply(): pl.pallas_call(orbital_kernel, out_shape=jax.ShapeDtypeStruct(phi.shape,...]
    all_to_all x1, waiting for transfers between devices: 0.01 us -> 7.53 us  [local(): lax.all_to_all(partial, ('z',), split_axis=0, concat_axis=0, tiled=True)]
  transfers between devices with their start and end apart: 17 -> 17, of which waited for: 6 -> 7; matrix products, arithmetic and copies ran while one was open for 1% -> 1% of each run, Pallas kernels for 14% -> 10%
where the time goes in v9:
time: 217 us; the launch traced here: 216 us
  starting transfers between devices  89.1 us (41%)
  waiting for transfers between devices  75.9 us (35%)
  Pallas kernels  22.7 us (10%)
  local copies, waits for them, and re-layouts  12 us (6%)
  blocking collectives  12 us (6%)
  other arithmetic  3.76 us (2%)
    ppermute x3, waiting for transfers between devices, local(): lax.ppermute(planes, 'z', ring(ZD, -s))  58 us
    ppermute x3, starting transfers between devices, local(): lax.ppermute(planes, 'z', ring(ZD, -s))  22.2 us
    all_to_all x1, starting transfers between devices, local(): lax.all_to_all(phi.transpose(1, 2, 0, 3), REGION, split_axis=0, concat_ax...  20 us
    all_gather x1, blocking collectives, local(): planes = lax.all_gather(potential, 'x', axis=0, tiled=True)  12 us
    pallas_call x1, Pallas kernels, hamiltonian_products(): pl.pallas_call(hamiltonian_kernel, out_shape=(SHARE, SHARE), in_specs=[SM...  10.9 us
    ppermute x3, starting transfers between devices, local(): lax.ppermute(column, 'z', ring(ZD, -s))  8.85 us
    all_to_all x1, waiting for transfers between devices, local(): lax.all_to_all(partial, ('z',), split_axis=0, concat_axis=0, tiled=True)  7.53 us
    all_to_all x1, starting transfers between devices, local(): lax.all_to_all(total, ('x', 'y'), split_axis=0, concat_axis=0, tiled=True)  7.31 us
  transfers between devices with their start and end apart: 17, of which 7 were waited for; matrix products, arithmetic and copies ran while one was open for 1% of the time, Pallas kernels for 10%

profile of v9, /device:TPU:6, one launch (start us, length us, event | category | flops | bytes accessed | tf_op | source)
XLA Modules:
  0.0 216.4 jit_solution(9203789889838052620)
XLA Ops:
  0.6 5.3 %copy.31 = bf16[8,128,8,128]{3,0,2,1:T(8,128)(2,1)} copy(bf16[8,128,8,128]{3,2,1,0:T(8,128)(2,1)} %phi.1) | data formatting | bytes 4194304 | tf_op args[0]
  6.0 20.0 %all-to-all-start = ((bf16[128,8,8,128]{3,2,1,0:T(8,128)(2,1)}), bf16[128,8,8,128]{3,2,1,0:T(8,128)(2,1)}, u32[]{:S(2)}, u32[]{:S(2)}) async-start(bf16[128,8,8,128]{3,2,1,0:T(8,128)(2,1)} %bitcast.32), calls=%async_computation | async-start | bytes 4194304 | tf_op jit(solution)/shard_map/all_to_all | solution.py:210
  26.0 0.0 copy-start.1
  26.0 0.9 fusion.2
  26.9 4.9 %collective-permute-start.1 = (bf16[8,128,1,128]{3,2,1,0:T(2,128)(2,1)S(1)}, bf16[8,128,1,128]{3,2,1,0:T(2,128)(2,1)S(1)}, u32[]{:S(2)}, u32[]{:S(2)}) collective-permute-start(bf16[8,128,1,128]{3,2,1,0:T(2,128)(2,1)S(1)} %get-tuple-element.59), channel_id=1, source_target_pairs={{0,3},{1,0},{2,1},{3,2},{4,7},{5,4},{6,5},{7,6},{8,11},{9,8},{10,9... | collective-permute-start | bytes 786440 | tf_op jit(solution)/shard_map/ppermute | solution.py:214
  31.8 1.9 collective-permute-start
  33.8 12.0 %all_gather.3 = f32[4,8,128]{2,1,0:T(8,128)S(1)} all-gather(f32[1,8,128]{2,1,0:T(8,128)S(1)} %copy-done.1), channel_id=1, replica_groups=mesh['z'=16,'x'=4,'c'=2,'y'=4] {'x'}, dimensions={0}, use_global_device_ids=true | all-gather | bytes 20480 | tf_op jit(solution)/shard_map/all_gather | solution.py:212
  45.7 0.0 collective-permute-done.1.above
  45.7 2.9 %collective-permute-done.below = bf16[8,128,1,128]{3,2,1,0:T(2,128)(2,1)S(1)} collective-permute-done((bf16[8,128,1,128]{3,2,1,0:T(2,128)(2,1)S(1)}, bf16[8,128,1,128]{3,2,1,0:T(2,128)(2,1)S(1)}, u32[]{:S(2)}, u32[]{:S(2)}) %collective-permute-start) | collective-permute-done | bytes 262176 | tf_op jit(solution)/shard_map/ppermute | solution.py:213
  48.6 7.4 %collective-permute-start.4 = (f32[4,8,128]{2,1,0:T(8,128)S(1)}, f32[4,8,128]{2,1,0:T(8,128)S(1)}, u32[]{:S(2)}, u32[]{:S(2)}) collective-permute-start(f32[4,8,128]{2,1,0:T(8,128)S(1)} %all_gather.3), channel_id=1, source_target_pairs={{0,128},{32,160},{64,192},{96,224},{128,256},{160,288},{192,320},{... | collective-permute-start | bytes 49160 | tf_op jit(solution)/shard_map/ppermute | solution.py:216
  56.1 7.7 %collective-permute-start.3 = (f32[4,8,128]{2,1,0:T(8,128)S(1)}, f32[4,8,128]{2,1,0:T(8,128)S(1)}, u32[]{:S(2)}, u32[]{:S(2)}) collective-permute-start(f32[4,8,128]{2,1,0:T(8,128)S(1)} %all_gather.3), channel_id=1, source_target_pairs={{0,256},{32,288},{64,320},{96,352},{128,384},{160,416},{192,448},{... | collective-permute-start | bytes 49160 | tf_op jit(solution)/shard_map/ppermute | solution.py:216
  63.8 7.1 %collective-permute-start.2 = (f32[4,8,128]{2,1,0:T(8,128)S(1)}, f32[4,8,128]{2,1,0:T(8,128)S(1)}, u32[]{:S(2)}, u32[]{:S(2)}) collective-permute-start(f32[4,8,128]{2,1,0:T(8,128)S(1)} %all_gather.3), channel_id=1, source_target_pairs={{0,384},{32,416},{64,448},{96,480},{128,0},{160,32},{192,64},{224,... | collective-permute-start | bytes 49160 | tf_op jit(solution)/shard_map/ppermute | solution.py:216
  70.8 48.5 %collective-permute-done.4 = f32[4,8,128]{2,1,0:T(8,128)S(1)} collective-permute-done((f32[4,8,128]{2,1,0:T(8,128)S(1)}, f32[4,8,128]{2,1,0:T(8,128)S(1)}, u32[]{:S(2)}, u32[]{:S(2)}) %collective-permute-start.4) | collective-permute-done | bytes 16416 | tf_op jit(solution)/shard_map/ppermute | solution.py:216
  119.4 9.5 %collective-permute-done.3 = f32[4,8,128]{2,1,0:T(8,128)S(1)} collective-permute-done((f32[4,8,128]{2,1,0:T(8,128)S(1)}, f32[4,8,128]{2,1,0:T(8,128)S(1)}, u32[]{:S(2)}, u32[]{:S(2)}) %collective-permute-start.3) | collective-permute-done | bytes 16416 | tf_op jit(solution)/shard_map/ppermute | solution.py:216
  128.9 0.0 collective-permute-done.2
  128.9 1.0 slice_bitcast_fusion
  129.9 0.0 copy-start.3
  129.9 0.0 copy-start.2
  129.9 3.3 %fusion.1 = (bf16[128,4,8,128]{3,2,1,0:T(8,128)(2,1)}, bf16[128,4,8,128]{3,2,1,0:T(8,128)(2,1)}) fusion(bf16[128,8,8,128]{3,2,1,0:T(8,128)(2,1)} %all-to-all-done.own), kind=kLoop, calls=%fused_computation.12 | loop fusion | bytes 4194304 | tf_op jit(solution)/shard_map/slice | solution.py:219
  133.2 1.9 collective-permute-start.6
  135.1 2.4 %collective-permute-start.7 = (bf16[128,4,8,128]{3,2,1,0:T(8,128)(2,1)}, bf16[128,4,8,128]{3,2,1,0:T(8,128)(2,1)}, u32[]{:S(2)}, u32[]{:S(2)}) collective-permute-start(bf16[128,4,8,128]{3,2,1,0:T(8,128)(2,1)} %get-tuple-element.37), channel_id=1, source_target_pairs={{0,4},{4,8},{8,12},{12,16},{16,20},{20,24},{24,28},{28,32},{32,36}... | collective-permute-start | bytes 3145736 | tf_op jit(solution)/shard_map/ppermute | solution.py:221
  137.5 0.1 copy.22
  137.6 0.1 reshape.19.pairs
  137.7 4.9 %collective-permute-start.8 = (bf16[128,8,128]{2,1,0:T(8,128)(2,1)S(1)}, bf16[128,8,128]{2,1,0:T(8,128)(2,1)S(1)}, u32[]{:S(2)}, u32[]{:S(2)}) collective-permute-start(bf16[128,8,128]{2,1,0:T(8,128)(2,1)S(1)} %slice_bitcast_fusion), channel_id=1, source_target_pairs={{0,3},{1,0},{2,1},{3,2},{4,7},{5,4},{6,5},{7,6},{8,11},{9,8},{10,9... | collective-permute-start | bytes 786440 | tf_op jit(solution)/shard_map/ppermute | solution.py:222
  142.7 0.1 pad_add_fusion.where
  142.7 5.4 %overlap_products.1 = (bf16[1024,1024]{1,0:T(8,128)(2,1)S(1)}, f32[4,4,8,16,128]{4,3,2,1,0:T(8,128)S(1)}, f32[4,4,8,16,128]{4,3,2,1,0:T(8,128)S(1)}) custom-call(s32[64]{0:T(128)S(1)} %reshape.19.pairs, s32[1024]{0:T(1024)S(1)} %bitcast.29, s32[3]{0:T(128)S(1)} %pad_add_fusion.where, bf16[128,8,8,128]{3,2,1,0:T(8,128)(2,1)} %all-to-all-done.own), custom_call_target="tpu_custom_call" | custom-call | flops 2000000000 | bytes 8388608 | tf_op jit(solution)/shard_map/overlap_products/pallas_call | solution.py:125
  148.2 4.2 %collective-permute-start.5 = (f32[4,4,8,16,128]{4,3,2,1,0:T(8,128)S(1)}, f32[4,4,8,16,128]{4,3,2,1,0:T(8,128)S(1)}, u32[]{:S(2)}, u32[]{:S(2)}) collective-permute-start(f32[4,4,8,16,128]{4,3,2,1,0:T(8,128)S(1)} %get-tuple-element.34), channel_id=1, source_target_pairs={{0,4},{4,0},{1,5},{5,1},{2,6},{6,2},{3,7},{7,3},{8,12},{12,8},{9,1... | collective-permute-start | bytes 3145736 | tf_op jit(solution)/shard_map/ppermute | solution.py:225
  152.4 10.9 %hamiltonian_products.1 = (f32[4,4,8,16,128]{4,3,2,1,0:T(8,128)S(1)}, f32[4,4,8,16,128]{4,3,2,1,0:T(8,128)S(1)}) custom-call(s32[64]{0:T(128)S(1)} %reshape.19.pairs, s32[1024]{0:T(1024)S(1)} %bitcast.30, s32[3]{0:T(128)S(1)} %pad_add_fusion.where, bf16[1024,1024]{1,0:T(8,128)(2,1)S(1)} %get-tuple-element.35.conf, ...), custom_call_target="tpu_custom_call" | custom-call | flops 5000000000 | bytes 8388608 | tf_op jit(solution)/shard_map/hamiltonian_products/pallas_call | solution.py:138
  163.4 1.9 collective-permute-start.9
  165.3 0.1 add_convert_fusion.1
  165.4 2.5 %collective-permute-done.9 = f32[4,4,8,16,128]{4,3,2,1,0:T(8,128)S(1)} collective-permute-done((f32[4,4,8,16,128]{4,3,2,1,0:T(8,128)S(1)}, f32[4,4,8,16,128]{4,3,2,1,0:T(8,128)S(1)}, u32[]{:S(2)}, u32[]{:S(2)}) %collective-permute-start.9) | collective-permute-done | bytes 1048608 | tf_op jit(solution)/shard_map/ppermute | solution.py:228
  167.9 0.1 add_convert_fusion
  168.1 1.1 pad_maximum_fusion
  169.1 7.3 %all-to-all-start.1 = ((bf16[16,2,8,16,128]{4,3,2,1,0:T(8,128)(2,1)}), bf16[16,2,8,16,128]{4,3,2,1,0:T(8,128)(2,1)}, u32[]{:S(2)}, u32[]{:S(2)}) async-start(bf16[16,2,8,16,128]{4,3,2,1,0:T(8,128)(2,1)} %pad_maximum_fusion), calls=%async_computation.1 | async-start | bytes 2097152 | tf_op jit(solution)/shard_map/all_to_all | solution.py:234
  176.4 1.9 collective-permute-start.10
  178.4 1.2 collective-permute-done.10
  179.6 2.3 %collective-permute-start.13 = (f32[2,4,4,8,128]{4,3,2,1,0:T(8,128)S(1)}, f32[2,4,4,8,128]{4,3,2,1,0:T(8,128)S(1)}, u32[]{:S(2)}, u32[]{:S(2)}) collective-permute-start(f32[2,4,4,8,128]{4,3,2,1,0:T(8,128)S(1)} %pad_maximum_fusion.1.pot_1), channel_id=1, source_target_pairs={{0,448},{32,480},{64,0},{96,32},{128,64},{160,96},{192,128},{224,1... | collective-permute-start | bytes 393224 | tf_op jit(solution)/shard_map/ppermute | solution.py:233
  181.9 3.2 %collective-permute-start.12 = (f32[2,4,4,8,128]{4,3,2,1,0:T(8,128)S(1)}, f32[2,4,4,8,128]{4,3,2,1,0:T(8,128)S(1)}, u32[]{:S(2)}, u32[]{:S(2)}) collective-permute-start(f32[2,4,4,8,128]{4,3,2,1,0:T(8,128)S(1)} %pad_maximum_fusion.1.pot_1), channel_id=1, source_target_pairs={{0,480},{32,0},{64,32},{96,64},{128,96},{160,128},{192,160},{224,1... | collective-permute-start | bytes 393224 | tf_op jit(solution)/shard_map/ppermute | solution.py:233
  185.1 3.4 %collective-permute-start.11 = (f32[2,4,4,8,128]{4,3,2,1,0:T(8,128)S(1)}, f32[2,4,4,8,128]{4,3,2,1,0:T(8,128)}, u32[]{:S(2)}, u32[]{:S(2)}) collective-permute-start(f32[2,4,4,8,128]{4,3,2,1,0:T(8,128)S(1)} %pad_maximum_fusion.1.pot_1), channel_id=1, source_target_pairs={{0,32},{32,64},{64,96},{96,128},{128,160},{160,192},{192,224},{224... | collective-permute-start | bytes 393224 | tf_op jit(solution)/shard_map/ppermute | solution.py:233
  188.5 3.7 %all-to-all-done.1 = bf16[16,2,8,16,128]{4,3,2,1,0:T(8,128)(2,1)} async-done(((bf16[16,2,8,16,128]{4,3,2,1,0:T(8,128)(2,1)}), bf16[16,2,8,16,128]{4,3,2,1,0:T(8,128)(2,1)}, u32[]{:S(2)}, u32[]{:S(2)}) %all-to-all-start.1) | async-done | bytes 1048608 | tf_op jit(solution)/shard_map/all_to_all | solution.py:234
  192.2 1.4 convert_reduce_fusion
  193.6 0.0 collective-permute-done.12.pot_2
  193.6 0.7 copy.27
  194.3 6.6 %all-to-all-start.2 = ((f32[16,2,8,128]{3,2,1,0:T(8,128)}), f32[16,2,8,128]{3,2,1,0:T(8,128)}, u32[]{:S(2)}, u32[]{:S(2)}) async-start(f32[16,2,8,128]{3,2,1,0:T(8,128)} %copy.27), calls=%async_computation.2 | async-start | bytes 262144 | tf_op jit(solution)/shard_map/all_to_all | solution.py:238
  201.0 6.4 %orbital_apply.1 = bf16[8,128,8,128]{3,2,1,0:T(8,128)(2,1)} custom-call(s32[1024]{0:T(1024)S(1)} %bitcast.31, s32[3]{0:T(128)S(1)} %pad_add_fusion.where, bf16[8,128,8,128]{3,2,1,0:T(8,128)(2,1)S(1)} %copy-done, bf16[8,128,1,128]{3,2,1,0:T(2,128)(2,1)S(1)} %collective-permute-done.below, bf16[8,128,1,128]{3,2,1,0:T(2,128)(2,1)S(1)} %collective-permute-done.1.above, ...), custom_call_target="tpu_custom_call" | custom-call | tf_op jit(solution)/shard_map/orbital_apply/pallas_call | solution.py:188
  207.3 7.5 %all-to-all-done.2 = f32[16,2,8,128]{3,2,1,0:T(8,128)} async-done(((f32[16,2,8,128]{3,2,1,0:T(8,128)}), f32[16,2,8,128]{3,2,1,0:T(8,128)}, u32[]{:S(2)}, u32[]{:S(2)}) %all-to-all-start.2) | async-done | bytes 131104 | tf_op jit(solution)/shard_map/all_to_all | solution.py:238
  214.9 0.9 reduce_sum.19
  215.8 0.6 slice_bitcast_fusion.1
  (14 shorter events, 0.0 us)
Async XLA Ops:
  6.0 20.0 %copy-start = (bf16[8,128,8,128]{3,2,1,0:T(8,128)(2,1)S(1)}, bf16[8,128,8,128]{3,2,1,0:T(8,128)(2,1)}, u32[]{:S(2)}) copy-start(bf16[8,128,8,128]{3,2,1,0:T(8,128)(2,1)} %phi.1) | copy-start | bytes 6291460
  6.0 122.9 %all-to-all-start = ((bf16[128,8,8,128]{3,2,1,0:T(8,128)(2,1)}), bf16[128,8,8,128]{3,2,1,0:T(8,128)(2,1)}, u32[]{:S(2)}, u32[]{:S(2)}) async-start(bf16[128,8,8,128]{3,2,1,0:T(8,128)(2,1)} %bitcast.32), calls=%async_computation | async-start | bytes 4194304 | tf_op jit(solution)/shard_map/all_to_all | solution.py:210
  26.0 7.8 %copy-start.1 = (f32[1,8,128]{2,1,0:T(8,128)S(1)}, f32[1,8,128]{2,1,0:T(8,128)}, u32[]{:S(2)}) copy-start(f32[1,8,128]{2,1,0:T(8,128)} %param.5) | copy-start | bytes 12292
  26.9 18.8 %collective-permute-start.1 = (bf16[8,128,1,128]{3,2,1,0:T(2,128)(2,1)S(1)}, bf16[8,128,1,128]{3,2,1,0:T(2,128)(2,1)S(1)}, u32[]{:S(2)}, u32[]{:S(2)}) collective-permute-start(bf16[8,128,1,128]{3,2,1,0:T(2,128)(2,1)S(1)} %get-tuple-element.59), channel_id=1, source_target_pairs={{0,3},{1,0},{2,1},{3,2},{4,7},{5,4},{6,5},{7,6},{8,11},{9,8},{10,9... | collective-permute-start | bytes 786440 | tf_op jit(solution)/shard_map/ppermute | solution.py:214
  31.8 16.8 %collective-permute-start = (bf16[8,128,1,128]{3,2,1,0:T(2,128)(2,1)S(1)}, bf16[8,128,1,128]{3,2,1,0:T(2,128)(2,1)S(1)}, u32[]{:S(2)}, u32[]{:S(2)}) collective-permute-start(bf16[8,128,1,128]{3,2,1,0:T(2,128)(2,1)S(1)} %get-tuple-element.60), channel_id=1, source_target_pairs={{0,1},{1,2},{2,3},{3,0},{4,5},{5,6},{6,7},{7,4},{8,9},{9,10},{10,1... | collective-permute-start | bytes 786440 | tf_op jit(solution)/shard_map/ppermute | solution.py:213
  48.6 70.7 %collective-permute-start.4 = (f32[4,8,128]{2,1,0:T(8,128)S(1)}, f32[4,8,128]{2,1,0:T(8,128)S(1)}, u32[]{:S(2)}, u32[]{:S(2)}) collective-permute-start(f32[4,8,128]{2,1,0:T(8,128)S(1)} %all_gather.3), channel_id=1, source_target_pairs={{0,128},{32,160},{64,192},{96,224},{128,256},{160,288},{192,320},{... | collective-permute-start | bytes 49160 | tf_op jit(solution)/shard_map/ppermute | solution.py:216
  56.1 72.8 %collective-permute-start.3 = (f32[4,8,128]{2,1,0:T(8,128)S(1)}, f32[4,8,128]{2,1,0:T(8,128)S(1)}, u32[]{:S(2)}, u32[]{:S(2)}) collective-permute-start(f32[4,8,128]{2,1,0:T(8,128)S(1)} %all_gather.3), channel_id=1, source_target_pairs={{0,256},{32,288},{64,320},{96,352},{128,384},{160,416},{192,448},{... | collective-permute-start | bytes 49160 | tf_op jit(solution)/shard_map/ppermute | solution.py:216
  63.8 65.1 %collective-permute-start.2 = (f32[4,8,128]{2,1,0:T(8,128)S(1)}, f32[4,8,128]{2,1,0:T(8,128)S(1)}, u32[]{:S(2)}, u32[]{:S(2)}) collective-permute-start(f32[4,8,128]{2,1,0:T(8,128)S(1)} %all_gather.3), channel_id=1, source_target_pairs={{0,384},{32,416},{64,448},{96,480},{128,0},{160,32},{192,64},{224,... | collective-permute-start | bytes 49160 | tf_op jit(solution)/shard_map/ppermute | solution.py:216
  129.9 7.6 %copy-start.3 = (s32[32,2]{0,1:T(2,128)S(1)}, s32[32,2]{0,1:T(2,128)}, u32[]{:S(2)}) copy-start(s32[32,2]{0,1:T(2,128)} %param.6) | copy-start | bytes 772
  129.9 12.9 %copy-start.2 = (s32[8,128]{1,0:T(8,128)S(1)}, s32[8,128]{1,0:T(8,128)}, u32[]{:S(2)}) copy-start(s32[8,128]{1,0:T(8,128)} %param.7) | copy-start | bytes 12292
  133.2 19.2 %collective-permute-start.6 = (bf16[128,4,8,128]{3,2,1,0:T(8,128)(2,1)}, bf16[128,4,8,128]{3,2,1,0:T(8,128)(2,1)}, u32[]{:S(2)}, u32[]{:S(2)}) collective-permute-start(bf16[128,4,8,128]{3,2,1,0:T(8,128)(2,1)} %get-tuple-element.36), channel_id=1, source_target_pairs={{0,508},{4,0},{8,4},{12,8},{16,12},{20,16},{24,20},{28,24},{32,28}... | collective-permute-start | bytes 3145736 | tf_op jit(solution)/shard_map/ppermute | solution.py:220
  135.1 17.3 %collective-permute-start.7 = (bf16[128,4,8,128]{3,2,1,0:T(8,128)(2,1)}, bf16[128,4,8,128]{3,2,1,0:T(8,128)(2,1)}, u32[]{:S(2)}, u32[]{:S(2)}) collective-permute-start(bf16[128,4,8,128]{3,2,1,0:T(8,128)(2,1)} %get-tuple-element.37), channel_id=1, source_target_pairs={{0,4},{4,8},{8,12},{12,16},{16,20},{20,24},{24,28},{28,32},{32,36}... | collective-permute-start | bytes 3145736 | tf_op jit(solution)/shard_map/ppermute | solution.py:221
  137.7 14.6 %collective-permute-start.8 = (bf16[128,8,128]{2,1,0:T(8,128)(2,1)S(1)}, bf16[128,8,128]{2,1,0:T(8,128)(2,1)S(1)}, u32[]{:S(2)}, u32[]{:S(2)}) collective-permute-start(bf16[128,8,128]{2,1,0:T(8,128)(2,1)S(1)} %slice_bitcast_fusion), channel_id=1, source_target_pairs={{0,3},{1,0},{2,1},{3,2},{4,7},{5,4},{6,5},{7,6},{8,11},{9,8},{10,9... | collective-permute-start | bytes 786440 | tf_op jit(solution)/shard_map/ppermute | solution.py:222
  148.2 17.1 %collective-permute-start.5 = (f32[4,4,8,16,128]{4,3,2,1,0:T(8,128)S(1)}, f32[4,4,8,16,128]{4,3,2,1,0:T(8,128)S(1)}, u32[]{:S(2)}, u32[]{:S(2)}) collective-permute-start(f32[4,4,8,16,128]{4,3,2,1,0:T(8,128)S(1)} %get-tuple-element.34), channel_id=1, source_target_pairs={{0,4},{4,0},{1,5},{5,1},{2,6},{6,2},{3,7},{7,3},{8,12},{12,8},{9,1... | collective-permute-start | bytes 3145736 | tf_op jit(solution)/shard_map/ppermute | solution.py:225
  163.4 4.6 %collective-permute-start.9 = (f32[4,4,8,16,128]{4,3,2,1,0:T(8,128)S(1)}, f32[4,4,8,16,128]{4,3,2,1,0:T(8,128)S(1)}, u32[]{:S(2)}, u32[]{:S(2)}) collective-permute-start(f32[4,4,8,16,128]{4,3,2,1,0:T(8,128)S(1)} %get-tuple-element.40), channel_id=1, source_target_pairs={{0,4},{4,0},{1,5},{5,1},{2,6},{6,2},{3,7},{7,3},{8,12},{12,8},{9,1... | collective-permute-start | bytes 3145736 | tf_op jit(solution)/shard_map/ppermute | solution.py:228
  169.1 23.1 %all-to-all-start.1 = ((bf16[16,2,8,16,128]{4,3,2,1,0:T(8,128)(2,1)}), bf16[16,2,8,16,128]{4,3,2,1,0:T(8,128)(2,1)}, u32[]{:S(2)}, u32[]{:S(2)}) async-start(bf16[16,2,8,16,128]{4,3,2,1,0:T(8,128)(2,1)} %pad_maximum_fusion), calls=%async_computation.1 | async-start | bytes 2097152 | tf_op jit(solution)/shard_map/all_to_all | solution.py:234
  176.4 3.1 %collective-permute-start.10 = (f32[4,4,8,128]{3,2,1,0:T(8,128)S(1)}, f32[4,4,8,128]{3,2,1,0:T(8,128)S(1)}, u32[]{:S(2)}, u32[]{:S(2)}) collective-permute-start(f32[4,4,8,128]{3,2,1,0:T(8,128)S(1)} %get-tuple-element.62), channel_id=1, source_target_pairs={{0,4},{4,0},{1,5},{5,1},{2,6},{6,2},{3,7},{7,3},{8,12},{12,8},{9,1... | collective-permute-start | bytes 196616 | tf_op jit(solution)/shard_map/ppermute | solution.py:232
  179.6 14.0 %collective-permute-start.13 = (f32[2,4,4,8,128]{4,3,2,1,0:T(8,128)S(1)}, f32[2,4,4,8,128]{4,3,2,1,0:T(8,128)S(1)}, u32[]{:S(2)}, u32[]{:S(2)}) collective-permute-start(f32[2,4,4,8,128]{4,3,2,1,0:T(8,128)S(1)} %pad_maximum_fusion.1.pot_1), channel_id=1, source_target_pairs={{0,448},{32,480},{64,0},{96,32},{128,64},{160,96},{192,128},{224,1... | collective-permute-start | bytes 393224 | tf_op jit(solution)/shard_map/ppermute | solution.py:233
  181.9 11.7 %collective-permute-start.12 = (f32[2,4,4,8,128]{4,3,2,1,0:T(8,128)S(1)}, f32[2,4,4,8,128]{4,3,2,1,0:T(8,128)S(1)}, u32[]{:S(2)}, u32[]{:S(2)}) collective-permute-start(f32[2,4,4,8,128]{4,3,2,1,0:T(8,128)S(1)} %pad_maximum_fusion.1.pot_1), channel_id=1, source_target_pairs={{0,480},{32,0},{64,32},{96,64},{128,96},{160,128},{192,160},{224,1... | collective-permute-start | bytes 393224 | tf_op jit(solution)/shard_map/ppermute | solution.py:233
  185.1 8.5 %collective-permute-start.11 = (f32[2,4,4,8,128]{4,3,2,1,0:T(8,128)S(1)}, f32[2,4,4,8,128]{4,3,2,1,0:T(8,128)}, u32[]{:S(2)}, u32[]{:S(2)}) collective-permute-start(f32[2,4,4,8,128]{4,3,2,1,0:T(8,128)S(1)} %pad_maximum_fusion.1.pot_1), channel_id=1, source_target_pairs={{0,32},{32,64},{64,96},{96,128},{128,160},{160,192},{192,224},{224... | collective-permute-start | bytes 393224 | tf_op jit(solution)/shard_map/ppermute | solution.py:233
  194.3 20.5 %all-to-all-start.2 = ((f32[16,2,8,128]{3,2,1,0:T(8,128)}), f32[16,2,8,128]{3,2,1,0:T(8,128)}, u32[]{:S(2)}, u32[]{:S(2)}) async-start(f32[16,2,8,128]{3,2,1,0:T(8,128)} %copy.27), calls=%async_computation.2 | async-start | bytes 262144 | tf_op jit(solution)/shard_map/all_to_all | solution.py:238

commit v10 on v9

--- a/solution.py
+++ b/solution.py
@@ -129,7 +129,6 @@
         out_specs=(VMEM,) * 3,
         scratch_shapes=[pltpu.VMEM((NB, NB * W, W), F32)],
         compiler_params=pltpu.CompilerParams(vmem_limit_bytes=16 << 20),
-        cost_estimate=pl.CostEstimate(flops=2 * 10**9, transcendentals=0, bytes_accessed=8 << 20),
         name="overlap_products",
     )(pair_flat, support_flat, where, own)
 

time: 217 us -> 215 us (level)
  waiting for transfers between devices: 75.9 us -> 73.4 us
    slice x1, local copies, waits for them, and re-layouts: 0.94 us -> 3.27 us  [local(): row_above = lax.ppermute(phi[:, :, :1], 'y', ring(YD, -1))]
  transfers between devices with their start and end apart: 17 -> 17, of which waited for: 7 -> 8; matrix products, arithmetic and copies ran while one was open for 1% -> 2% of each run, Pallas kernels for 10% -> 10%
where the time goes in v10:
time: 215 us; the launch traced here: 214 us
  starting transfers between devices  89.9 us (42%)
  waiting for transfers between devices  73.4 us (34%)
  Pallas kernels  21.7 us (10%)
  local copies, waits for them, and re-layouts  12.6 us (6%)
  blocking collectives  11.9 us (6%)
  other arithmetic  3.76 us (2%)
    ppermute x3, waiting for transfers between devices, local(): lax.ppermute(planes, 'z', ring(ZD, -s))  56.2 us
    ppermute x3, starting transfers between devices, local(): lax.ppermute(planes, 'z', ring(ZD, -s))  22.2 us
    all_to_all x1, starting transfers between devices, local(): lax.all_to_all(phi.transpose(1, 2, 0, 3), REGION, split_axis=0, concat_ax...  19.4 us
    all_gather x1, blocking collectives, local(): planes = lax.all_gather(potential, 'x', axis=0, tiled=True)  11.9 us
    pallas_call x1, Pallas kernels, hamiltonian_products(): pl.pallas_call(hamiltonian_kernel, out_shape=(SHARE, SHARE), in_specs=[SM...  10.9 us
    ppermute x3, starting transfers between devices, local(): lax.ppermute(column, 'z', ring(ZD, -s))  8.85 us
    all_to_all x1, starting transfers between devices, local(): lax.all_to_all(total, ('x', 'y'), split_axis=0, concat_axis=0, tiled=True)  8.11 us
    all_to_all x1, waiting for transfers between devices, local(): lax.all_to_all(partial, ('z',), split_axis=0, concat_axis=0, tiled=True)  7.18 us
  transfers between devices with their start and end apart: 17, of which 8 were waited for; matrix products, arithmetic and copies ran while one was open for 2% of the time, Pallas kernels for 10%

profile of v10, /device:TPU:6, one launch (start us, length us, event | category | flops | bytes accessed | tf_op | source)
XLA Modules:
  0.0 214.3 jit_solution(18315138755580447283)
XLA Ops:
  0.6 5.3 %copy.31 = bf16[8,128,8,128]{3,0,2,1:T(8,128)(2,1)} copy(bf16[8,128,8,128]{3,2,1,0:T(8,128)(2,1)} %phi.1) | data formatting | bytes 4194304 | tf_op args[0]
  6.0 19.4 %all-to-all-start = ((bf16[128,8,8,128]{3,2,1,0:T(8,128)(2,1)}), bf16[128,8,8,128]{3,2,1,0:T(8,128)(2,1)S(1)}, u32[]{:S(2)}, u32[]{:S(2)}) async-start(bf16[128,8,8,128]{3,2,1,0:T(8,128)(2,1)} %bitcast.32), calls=%async_computation | async-start | bytes 4194304 | tf_op jit(solution)/shard_map/all_to_all | solution.py:209
  25.3 0.0 copy-start.2
  25.4 3.3 %fusion.2 = (bf16[8,128,1,128]{3,2,1,0:T(2,128)(2,1)S(1)}, bf16[8,128,1,128]{3,2,1,0:T(2,128)(2,1)S(1)}) fusion(bf16[8,128,8,128]{3,2,1,0:T(8,128)(2,1)} %phi.1), kind=kLoop, calls=%fused_computation.13 | loop fusion | bytes 1048576 | tf_op jit(solution)/shard_map/slice | solution.py:213
  28.6 4.9 %collective-permute-start.1 = (bf16[8,128,1,128]{3,2,1,0:T(2,128)(2,1)S(1)}, bf16[8,128,1,128]{3,2,1,0:T(2,128)(2,1)S(1)}, u32[]{:S(2)}, u32[]{:S(2)}) collective-permute-start(bf16[8,128,1,128]{3,2,1,0:T(2,128)(2,1)S(1)} %get-tuple-element.59), channel_id=1, source_target_pairs={{0,3},{1,0},{2,1},{3,2},{4,7},{5,4},{6,5},{7,6},{8,11},{9,8},{10,9... | collective-permute-start | bytes 786440 | tf_op jit(solution)/shard_map/ppermute | solution.py:213
  33.6 1.9 collective-permute-start
  35.5 11.9 %all_gather.3 = f32[4,8,128]{2,1,0:T(8,128)S(1)} all-gather(f32[1,8,128]{2,1,0:T(8,128)S(1)} %copy-done.2), channel_id=1, replica_groups=mesh['z'=16,'x'=4,'c'=2,'y'=4] {'x'}, dimensions={0}, use_global_device_ids=true | all-gather | bytes 20480 | tf_op jit(solution)/shard_map/all_gather | solution.py:211
  47.4 0.0 collective-permute-done.1.above
  47.5 2.9 %collective-permute-done.below = bf16[8,128,1,128]{3,2,1,0:T(2,128)(2,1)S(1)} collective-permute-done((bf16[8,128,1,128]{3,2,1,0:T(2,128)(2,1)S(1)}, bf16[8,128,1,128]{3,2,1,0:T(2,128)(2,1)S(1)}, u32[]{:S(2)}, u32[]{:S(2)}) %collective-permute-start) | collective-permute-done | bytes 262176 | tf_op jit(solution)/shard_map/ppermute | solution.py:212
  50.4 7.4 %collective-permute-start.4 = (f32[4,8,128]{2,1,0:T(8,128)S(1)}, f32[4,8,128]{2,1,0:T(8,128)S(1)}, u32[]{:S(2)}, u32[]{:S(2)}) collective-permute-start(f32[4,8,128]{2,1,0:T(8,128)S(1)} %all_gather.3), channel_id=1, source_target_pairs={{0,128},{32,160},{64,192},{96,224},{128,256},{160,288},{192,320},{... | collective-permute-start | bytes 49160 | tf_op jit(solution)/shard_map/ppermute | solution.py:215
  57.8 7.7 %collective-permute-start.3 = (f32[4,8,128]{2,1,0:T(8,128)S(1)}, f32[4,8,128]{2,1,0:T(8,128)S(1)}, u32[]{:S(2)}, u32[]{:S(2)}) collective-permute-start(f32[4,8,128]{2,1,0:T(8,128)S(1)} %all_gather.3), channel_id=1, source_target_pairs={{0,256},{32,288},{64,320},{96,352},{128,384},{160,416},{192,448},{... | collective-permute-start | bytes 49160 | tf_op jit(solution)/shard_map/ppermute | solution.py:215
  65.5 7.1 %collective-permute-start.2 = (f32[4,8,128]{2,1,0:T(8,128)S(1)}, f32[4,8,128]{2,1,0:T(8,128)S(1)}, u32[]{:S(2)}, u32[]{:S(2)}) collective-permute-start(f32[4,8,128]{2,1,0:T(8,128)S(1)} %all_gather.3), channel_id=1, source_target_pairs={{0,384},{32,416},{64,448},{96,480},{128,0},{160,32},{192,64},{224,... | collective-permute-start | bytes 49160 | tf_op jit(solution)/shard_map/ppermute | solution.py:215
  72.6 46.6 %collective-permute-done.4 = f32[4,8,128]{2,1,0:T(8,128)S(1)} collective-permute-done((f32[4,8,128]{2,1,0:T(8,128)S(1)}, f32[4,8,128]{2,1,0:T(8,128)S(1)}, u32[]{:S(2)}, u32[]{:S(2)}) %collective-permute-start.4) | collective-permute-done | bytes 16416 | tf_op jit(solution)/shard_map/ppermute | solution.py:215
  119.2 9.5 %collective-permute-done.3 = f32[4,8,128]{2,1,0:T(8,128)S(1)} collective-permute-done((f32[4,8,128]{2,1,0:T(8,128)S(1)}, f32[4,8,128]{2,1,0:T(8,128)S(1)}, u32[]{:S(2)}, u32[]{:S(2)}) %collective-permute-start.3) | collective-permute-done | bytes 16416 | tf_op jit(solution)/shard_map/ppermute | solution.py:215
  128.8 0.0 collective-permute-done.2
  128.8 0.0 all-to-all-done.own
  128.8 0.8 slice_bitcast_fusion
  129.5 1.7 fusion.1
  131.3 1.9 collective-permute-start.6
  133.2 2.4 %collective-permute-start.7 = (bf16[128,4,8,128]{3,2,1,0:T(8,128)(2,1)}, bf16[128,4,8,128]{3,2,1,0:T(8,128)(2,1)}, u32[]{:S(2)}, u32[]{:S(2)}) collective-permute-start(bf16[128,4,8,128]{3,2,1,0:T(8,128)(2,1)} %get-tuple-element.37), channel_id=1, source_target_pairs={{0,4},{4,8},{8,12},{12,16},{16,20},{20,24},{24,28},{28,32},{32,36}... | collective-permute-start | bytes 3145736 | tf_op jit(solution)/shard_map/ppermute | solution.py:220
  135.6 4.9 %collective-permute-start.8 = (bf16[128,8,128]{2,1,0:T(8,128)(2,1)}, bf16[128,8,128]{2,1,0:T(8,128)(2,1)S(1)}, u32[]{:S(2)}, u32[]{:S(2)}) collective-permute-start(bf16[128,8,128]{2,1,0:T(8,128)(2,1)} %slice_bitcast_fusion), channel_id=1, source_target_pairs={{0,3},{1,0},{2,1},{3,2},{4,7},{5,4},{6,5},{7,6},{8,11},{9,8},{10,9... | collective-permute-start | bytes 786440 | tf_op jit(solution)/shard_map/ppermute | solution.py:221
  140.5 0.1 copy.22
  140.6 0.1 reshape.19.pairs
  140.8 0.1 pad_add_fusion.where
  140.8 4.4 %overlap_products.1 = (bf16[1024,1024]{1,0:T(8,128)(2,1)S(1)}, f32[4,4,8,16,128]{4,3,2,1,0:T(8,128)S(1)}, f32[4,4,8,16,128]{4,3,2,1,0:T(8,128)S(1)}) custom-call(s32[64]{0:T(128)S(1)} %reshape.19.pairs, s32[1024]{0:T(1024)S(1)} %bitcast.28, s32[3]{0:T(128)S(1)} %pad_add_fusion.where, bf16[128,8,8,128]{3,2,1,0:T(8,128)(2,1)S(1)} %all-to-all-done.own), custom_call_target="tpu_custom_call" | custom-call | tf_op jit(solution)/shard_map/overlap_products/pallas_call | solution.py:125
  145.3 4.2 %collective-permute-start.5 = (f32[4,4,8,16,128]{4,3,2,1,0:T(8,128)S(1)}, f32[4,4,8,16,128]{4,3,2,1,0:T(8,128)S(1)}, u32[]{:S(2)}, u32[]{:S(2)}) collective-permute-start(f32[4,4,8,16,128]{4,3,2,1,0:T(8,128)S(1)} %get-tuple-element.34), channel_id=1, source_target_pairs={{0,4},{4,0},{1,5},{5,1},{2,6},{6,2},{3,7},{7,3},{8,12},{12,8},{9,1... | collective-permute-start | bytes 3145736 | tf_op jit(solution)/shard_map/ppermute | solution.py:224
  149.5 0.0 collective-permute-done.8.above
  149.5 0.1 collective-permute-done.7.behind
  149.6 10.9 %hamiltonian_products.1 = (f32[4,4,8,16,128]{4,3,2,1,0:T(8,128)S(1)}, f32[4,4,8,16,128]{4,3,2,1,0:T(8,128)S(1)}) custom-call(s32[64]{0:T(128)S(1)} %reshape.19.pairs, s32[1024]{0:T(1024)S(1)} %bitcast.29, s32[3]{0:T(128)S(1)} %pad_add_fusion.where, bf16[1024,1024]{1,0:T(8,128)(2,1)S(1)} %get-tuple-element.35.conf, ...), custom_call_target="tpu_custom_call" | custom-call | flops 5000000000 | bytes 8388608 | tf_op jit(solution)/shard_map/hamiltonian_products/pallas_call | solution.py:137
  160.6 2.5 %collective-permute-start.9 = (f32[4,4,8,16,128]{4,3,2,1,0:T(8,128)S(1)}, f32[4,4,8,16,128]{4,3,2,1,0:T(8,128)S(1)}, u32[]{:S(2)}, u32[]{:S(2)}) collective-permute-start(f32[4,4,8,16,128]{4,3,2,1,0:T(8,128)S(1)} %get-tuple-element.40), channel_id=1, source_target_pairs={{0,4},{4,0},{1,5},{5,1},{2,6},{6,2},{3,7},{7,3},{8,12},{12,8},{9,1... | collective-permute-start | bytes 3145736 | tf_op jit(solution)/shard_map/ppermute | solution.py:227
  163.1 0.1 add_convert_fusion.1
  163.2 2.1 collective-permute-done.9
  165.3 0.1 add_convert_fusion
  165.5 1.1 pad_maximum_fusion
  166.6 8.1 %all-to-all-start.1 = ((bf16[16,2,8,16,128]{4,3,2,1,0:T(8,128)(2,1)}), bf16[16,2,8,16,128]{4,3,2,1,0:T(8,128)(2,1)}, u32[]{:S(2)}, u32[]{:S(2)}) async-start(bf16[16,2,8,16,128]{4,3,2,1,0:T(8,128)(2,1)} %pad_maximum_fusion), calls=%async_computation.1 | async-start | bytes 2097152 | tf_op jit(solution)/shard_map/all_to_all | solution.py:233
  174.7 1.9 collective-permute-start.10
  176.6 1.2 collective-permute-done.10
  177.8 2.3 %collective-permute-start.13 = (f32[2,4,4,8,128]{4,3,2,1,0:T(8,128)S(1)}, f32[2,4,4,8,128]{4,3,2,1,0:T(8,128)S(1)}, u32[]{:S(2)}, u32[]{:S(2)}) collective-permute-start(f32[2,4,4,8,128]{4,3,2,1,0:T(8,128)S(1)} %pad_maximum_fusion.1.pot_1), channel_id=1, source_target_pairs={{0,448},{32,480},{64,0},{96,32},{128,64},{160,96},{192,128},{224,1... | collective-permute-start | bytes 393224 | tf_op jit(solution)/shard_map/ppermute | solution.py:232
  180.1 3.2 %collective-permute-start.12 = (f32[2,4,4,8,128]{4,3,2,1,0:T(8,128)S(1)}, f32[2,4,4,8,128]{4,3,2,1,0:T(8,128)S(1)}, u32[]{:S(2)}, u32[]{:S(2)}) collective-permute-start(f32[2,4,4,8,128]{4,3,2,1,0:T(8,128)S(1)} %pad_maximum_fusion.1.pot_1), channel_id=1, source_target_pairs={{0,480},{32,0},{64,32},{96,64},{128,96},{160,128},{192,160},{224,1... | collective-permute-start | bytes 393224 | tf_op jit(solution)/shard_map/ppermute | solution.py:232
  183.3 3.4 %collective-permute-start.11 = (f32[2,4,4,8,128]{4,3,2,1,0:T(8,128)S(1)}, f32[2,4,4,8,128]{4,3,2,1,0:T(8,128)}, u32[]{:S(2)}, u32[]{:S(2)}) collective-permute-start(f32[2,4,4,8,128]{4,3,2,1,0:T(8,128)S(1)} %pad_maximum_fusion.1.pot_1), channel_id=1, source_target_pairs={{0,32},{32,64},{64,96},{96,128},{128,160},{160,192},{192,224},{224... | collective-permute-start | bytes 393224 | tf_op jit(solution)/shard_map/ppermute | solution.py:232
  186.7 3.7 %all-to-all-done.1 = bf16[16,2,8,16,128]{4,3,2,1,0:T(8,128)(2,1)} async-done(((bf16[16,2,8,16,128]{4,3,2,1,0:T(8,128)(2,1)}), bf16[16,2,8,16,128]{4,3,2,1,0:T(8,128)(2,1)}, u32[]{:S(2)}, u32[]{:S(2)}) %all-to-all-start.1) | async-done | bytes 1048608 | tf_op jit(solution)/shard_map/all_to_all | solution.py:233
  190.4 1.4 convert_reduce_fusion
  191.8 0.7 copy.27
  192.5 6.7 %all-to-all-start.2 = ((f32[16,2,8,128]{3,2,1,0:T(8,128)}), f32[16,2,8,128]{3,2,1,0:T(8,128)}, u32[]{:S(2)}, u32[]{:S(2)}) async-start(f32[16,2,8,128]{3,2,1,0:T(8,128)} %copy.27), calls=%async_computation.2 | async-start | bytes 262144 | tf_op jit(solution)/shard_map/all_to_all | solution.py:237
  199.2 6.3 %orbital_apply.1 = bf16[8,128,8,128]{3,2,1,0:T(8,128)(2,1)} custom-call(s32[1024]{0:T(1024)S(1)} %bitcast.30, s32[3]{0:T(128)S(1)} %pad_add_fusion.where, bf16[8,128,8,128]{3,2,1,0:T(8,128)(2,1)S(1)} %copy-done, bf16[8,128,1,128]{3,2,1,0:T(2,128)(2,1)S(1)} %collective-permute-done.below, bf16[8,128,1,128]{3,2,1,0:T(2,128)(2,1)S(1)} %collective-permute-done.1.above, ...), custom_call_target="tpu_custom_call" | custom-call | tf_op jit(solution)/shard_map/orbital_apply/pallas_call | solution.py:187
  205.6 7.2 %all-to-all-done.2 = f32[16,2,8,128]{3,2,1,0:T(8,128)} async-done(((f32[16,2,8,128]{3,2,1,0:T(8,128)}), f32[16,2,8,128]{3,2,1,0:T(8,128)}, u32[]{:S(2)}, u32[]{:S(2)}) %all-to-all-start.2) | async-done | bytes 131104 | tf_op jit(solution)/shard_map/all_to_all | solution.py:237
  212.7 0.9 reduce_sum.19
  213.7 0.6 slice_bitcast_fusion.1
  (14 shorter events, 0.0 us)
Async XLA Ops:
  6.0 122.8 %all-to-all-start = ((bf16[128,8,8,128]{3,2,1,0:T(8,128)(2,1)}), bf16[128,8,8,128]{3,2,1,0:T(8,128)(2,1)S(1)}, u32[]{:S(2)}, u32[]{:S(2)}) async-start(bf16[128,8,8,128]{3,2,1,0:T(8,128)(2,1)} %bitcast.32), calls=%async_computation | async-start | bytes 4194304 | tf_op jit(solution)/shard_map/all_to_all | solution.py:209
  25.3 10.2 %copy-start.2 = (f32[1,8,128]{2,1,0:T(8,128)S(1)}, f32[1,8,128]{2,1,0:T(8,128)}, u32[]{:S(2)}) copy-start(f32[1,8,128]{2,1,0:T(8,128)} %param.5) | copy-start | bytes 12292
  28.6 18.8 %collective-permute-start.1 = (bf16[8,128,1,128]{3,2,1,0:T(2,128)(2,1)S(1)}, bf16[8,128,1,128]{3,2,1,0:T(2,128)(2,1)S(1)}, u32[]{:S(2)}, u32[]{:S(2)}) collective-permute-start(bf16[8,128,1,128]{3,2,1,0:T(2,128)(2,1)S(1)} %get-tuple-element.59), channel_id=1, source_target_pairs={{0,3},{1,0},{2,1},{3,2},{4,7},{5,4},{6,5},{7,6},{8,11},{9,8},{10,9... | collective-permute-start | bytes 786440 | tf_op jit(solution)/shard_map/ppermute | solution.py:213
  33.6 16.8 %collective-permute-start = (bf16[8,128,1,128]{3,2,1,0:T(2,128)(2,1)S(1)}, bf16[8,128,1,128]{3,2,1,0:T(2,128)(2,1)S(1)}, u32[]{:S(2)}, u32[]{:S(2)}) collective-permute-start(bf16[8,128,1,128]{3,2,1,0:T(2,128)(2,1)S(1)} %get-tuple-element.60), channel_id=1, source_target_pairs={{0,1},{1,2},{2,3},{3,0},{4,5},{5,6},{6,7},{7,4},{8,9},{9,10},{10,1... | collective-permute-start | bytes 786440 | tf_op jit(solution)/shard_map/ppermute | solution.py:212
  50.4 68.8 %collective-permute-start.4 = (f32[4,8,128]{2,1,0:T(8,128)S(1)}, f32[4,8,128]{2,1,0:T(8,128)S(1)}, u32[]{:S(2)}, u32[]{:S(2)}) collective-permute-start(f32[4,8,128]{2,1,0:T(8,128)S(1)} %all_gather.3), channel_id=1, source_target_pairs={{0,128},{32,160},{64,192},{96,224},{128,256},{160,288},{192,320},{... | collective-permute-start | bytes 49160 | tf_op jit(solution)/shard_map/ppermute | solution.py:215
  57.8 71.0 %collective-permute-start.3 = (f32[4,8,128]{2,1,0:T(8,128)S(1)}, f32[4,8,128]{2,1,0:T(8,128)S(1)}, u32[]{:S(2)}, u32[]{:S(2)}) collective-permute-start(f32[4,8,128]{2,1,0:T(8,128)S(1)} %all_gather.3), channel_id=1, source_target_pairs={{0,256},{32,288},{64,320},{96,352},{128,384},{160,416},{192,448},{... | collective-permute-start | bytes 49160 | tf_op jit(solution)/shard_map/ppermute | solution.py:215
  65.5 63.2 %collective-permute-start.2 = (f32[4,8,128]{2,1,0:T(8,128)S(1)}, f32[4,8,128]{2,1,0:T(8,128)S(1)}, u32[]{:S(2)}, u32[]{:S(2)}) collective-permute-start(f32[4,8,128]{2,1,0:T(8,128)S(1)} %all_gather.3), channel_id=1, source_target_pairs={{0,384},{32,416},{64,448},{96,480},{128,0},{160,32},{192,64},{224,... | collective-permute-start | bytes 49160 | tf_op jit(solution)/shard_map/ppermute | solution.py:215
  129.5 11.0 %copy-start.3 = (s32[32,2]{0,1:T(2,128)S(1)}, s32[32,2]{0,1:T(2,128)}, u32[]{:S(2)}) copy-start(s32[32,2]{0,1:T(2,128)} %param.6) | copy-start | bytes 772
  129.5 11.3 %copy-start.1 = (s32[8,128]{1,0:T(8,128)S(1)}, s32[8,128]{1,0:T(8,128)}, u32[]{:S(2)}) copy-start(s32[8,128]{1,0:T(8,128)} %param.7) | copy-start | bytes 12292
  131.3 18.2 %collective-permute-start.6 = (bf16[128,4,8,128]{3,2,1,0:T(8,128)(2,1)}, bf16[128,4,8,128]{3,2,1,0:T(8,128)(2,1)}, u32[]{:S(2)}, u32[]{:S(2)}) collective-permute-start(bf16[128,4,8,128]{3,2,1,0:T(8,128)(2,1)} %get-tuple-element.36), channel_id=1, source_target_pairs={{0,508},{4,0},{8,4},{12,8},{16,12},{20,16},{24,20},{28,24},{32,28}... | collective-permute-start | bytes 3145736 | tf_op jit(solution)/shard_map/ppermute | solution.py:219
  133.2 16.4 %collective-permute-start.7 = (bf16[128,4,8,128]{3,2,1,0:T(8,128)(2,1)}, bf16[128,4,8,128]{3,2,1,0:T(8,128)(2,1)}, u32[]{:S(2)}, u32[]{:S(2)}) collective-permute-start(bf16[128,4,8,128]{3,2,1,0:T(8,128)(2,1)} %get-tuple-element.37), channel_id=1, source_target_pairs={{0,4},{4,8},{8,12},{12,16},{16,20},{20,24},{24,28},{28,32},{32,36}... | collective-permute-start | bytes 3145736 | tf_op jit(solution)/shard_map/ppermute | solution.py:220
  135.6 13.9 %collective-permute-start.8 = (bf16[128,8,128]{2,1,0:T(8,128)(2,1)}, bf16[128,8,128]{2,1,0:T(8,128)(2,1)S(1)}, u32[]{:S(2)}, u32[]{:S(2)}) collective-permute-start(bf16[128,8,128]{2,1,0:T(8,128)(2,1)} %slice_bitcast_fusion), channel_id=1, source_target_pairs={{0,3},{1,0},{2,1},{3,2},{4,7},{5,4},{6,5},{7,6},{8,11},{9,8},{10,9... | collective-permute-start | bytes 786440 | tf_op jit(solution)/shard_map/ppermute | solution.py:221
  145.3 17.8 %collective-permute-start.5 = (f32[4,4,8,16,128]{4,3,2,1,0:T(8,128)S(1)}, f32[4,4,8,16,128]{4,3,2,1,0:T(8,128)S(1)}, u32[]{:S(2)}, u32[]{:S(2)}) collective-permute-start(f32[4,4,8,16,128]{4,3,2,1,0:T(8,128)S(1)} %get-tuple-element.34), channel_id=1, source_target_pairs={{0,4},{4,0},{1,5},{5,1},{2,6},{6,2},{3,7},{7,3},{8,12},{12,8},{9,1... | collective-permute-start | bytes 3145736 | tf_op jit(solution)/shard_map/ppermute | solution.py:224
  160.6 4.8 %collective-permute-start.9 = (f32[4,4,8,16,128]{4,3,2,1,0:T(8,128)S(1)}, f32[4,4,8,16,128]{4,3,2,1,0:T(8,128)S(1)}, u32[]{:S(2)}, u32[]{:S(2)}) collective-permute-start(f32[4,4,8,16,128]{4,3,2,1,0:T(8,128)S(1)} %get-tuple-element.40), channel_id=1, source_target_pairs={{0,4},{4,0},{1,5},{5,1},{2,6},{6,2},{3,7},{7,3},{8,12},{12,8},{9,1... | collective-permute-start | bytes 3145736 | tf_op jit(solution)/shard_map/ppermute | solution.py:227
  166.6 32.7 %copy-start = (bf16[8,128,8,128]{3,2,1,0:T(8,128)(2,1)S(1)}, bf16[8,128,8,128]{3,2,1,0:T(8,128)(2,1)}, u32[]{:S(2)}) copy-start(bf16[8,128,8,128]{3,2,1,0:T(8,128)(2,1)} %phi.1) | copy-start | bytes 6291460
  166.6 23.9 %all-to-all-start.1 = ((bf16[16,2,8,16,128]{4,3,2,1,0:T(8,128)(2,1)}), bf16[16,2,8,16,128]{4,3,2,1,0:T(8,128)(2,1)}, u32[]{:S(2)}, u32[]{:S(2)}) async-start(bf16[16,2,8,16,128]{4,3,2,1,0:T(8,128)(2,1)} %pad_maximum_fusion), calls=%async_computation.1 | async-start | bytes 2097152 | tf_op jit(solution)/shard_map/all_to_all | solution.py:233
  174.7 3.1 %collective-permute-start.10 = (f32[4,4,8,128]{3,2,1,0:T(8,128)S(1)}, f32[4,4,8,128]{3,2,1,0:T(8,128)S(1)}, u32[]{:S(2)}, u32[]{:S(2)}) collective-permute-start(f32[4,4,8,128]{3,2,1,0:T(8,128)S(1)} %get-tuple-element.62), channel_id=1, source_target_pairs={{0,4},{4,0},{1,5},{5,1},{2,6},{6,2},{3,7},{7,3},{8,12},{12,8},{9,1... | collective-permute-start | bytes 196616 | tf_op jit(solution)/shard_map/ppermute | solution.py:231
  177.8 14.0 %collective-permute-start.13 = (f32[2,4,4,8,128]{4,3,2,1,0:T(8,128)S(1)}, f32[2,4,4,8,128]{4,3,2,1,0:T(8,128)S(1)}, u32[]{:S(2)}, u32[]{:S(2)}) collective-permute-start(f32[2,4,4,8,128]{4,3,2,1,0:T(8,128)S(1)} %pad_maximum_fusion.1.pot_1), channel_id=1, source_target_pairs={{0,448},{32,480},{64,0},{96,32},{128,64},{160,96},{192,128},{224,1... | collective-permute-start | bytes 393224 | tf_op jit(solution)/shard_map/ppermute | solution.py:232
  180.1 11.7 %collective-permute-start.12 = (f32[2,4,4,8,128]{4,3,2,1,0:T(8,128)S(1)}, f32[2,4,4,8,128]{4,3,2,1,0:T(8,128)S(1)}, u32[]{:S(2)}, u32[]{:S(2)}) collective-permute-start(f32[2,4,4,8,128]{4,3,2,1,0:T(8,128)S(1)} %pad_maximum_fusion.1.pot_1), channel_id=1, source_target_pairs={{0,480},{32,0},{64,32},{96,64},{128,96},{160,128},{192,160},{224,1... | collective-permute-start | bytes 393224 | tf_op jit(solution)/shard_map/ppermute | solution.py:232
  183.3 8.5 %collective-permute-start.11 = (f32[2,4,4,8,128]{4,3,2,1,0:T(8,128)S(1)}, f32[2,4,4,8,128]{4,3,2,1,0:T(8,128)}, u32[]{:S(2)}, u32[]{:S(2)}) collective-permute-start(f32[2,4,4,8,128]{4,3,2,1,0:T(8,128)S(1)} %pad_maximum_fusion.1.pot_1), channel_id=1, source_target_pairs={{0,32},{32,64},{64,96},{96,128},{128,160},{160,192},{192,224},{224... | collective-permute-start | bytes 393224 | tf_op jit(solution)/shard_map/ppermute | solution.py:232
  192.5 20.2 %all-to-all-start.2 = ((f32[16,2,8,128]{3,2,1,0:T(8,128)}), f32[16,2,8,128]{3,2,1,0:T(8,128)}, u32[]{:S(2)}, u32[]{:S(2)}) async-start(f32[16,2,8,128]{3,2,1,0:T(8,128)} %copy.27), calls=%async_computation.2 | async-start | bytes 262144 | tf_op jit(solution)/shard_map/all_to_all | solution.py:237
